TPU v7x, 256 devices: a whole 4x4x8 slice. The times are simulated.
256 devices in a mesh: ax: 32 (over x, y, core), az: 8 (over z).
Axes of the slice: x: 4, y: 4, z: 8, core: 2. Of those that a mesh axis runs over, the one named last changes fastest.
Arguments:
- initial_state: float32 [16, 5, 64, 64, 128], P(None, None, 'ax', 'az'), may hold values from -6 to 6
- forcing: float32 [16, 5, 64, 64, 128], P(None, None, 'ax', 'az'), may hold values from -12 to 12
- axial_speed: float32 [64, 64, 128], P('ax', 'az'), may hold values from 0.2 to 1
- swirl_speed: float32 [64, 64, 128], P('ax', 'az'), may hold values from -0.5 to 0.5
- coupling: float32 [5, 5, 64, 64, 128], P(None, None, 'ax', 'az'), may hold values from -1.5 to 1.5
Outputs:
- final_state: float32 [16, 5, 64, 64, 128], P(None, None, 'ax', 'az')
- basis: float32 [8, 16, 2, 5, 64, 64, 128], P(None, None, None, None, 'ax', 'az')
- upper: float32 [8, 16, 16], replicated
All inputs are finite; a program needn't handle non-finite values.
Results may differ from a plain program's by a relative error of at most 0.0001.
Values sent between devices are 32-bit elements; how exact they have to be, the bound alone decides.
No kernel may reach another device: no remote copies, remote signals or barrier semaphores. Data moves between devices by JAX's collectives and lax.ppermute only.
A program may use at most 64 MiB of HBM per device.

v0:
```python
import math

import jax
import jax.numpy as jnp
import numpy as np
from jax import lax
from jax.experimental import pallas as pl
from jax.experimental.pallas import tpu as pltpu
from jax.sharding import PartitionSpec as P

NFORCE = 16
NVAR = 5
NFREQ = 8
STEPS = 2
ROWS = NFORCE * NVAR * 8
step_size = 0.25
viscous = 0.1
F32, BF16 = jnp.float32, jnp.bfloat16
VMEM = pl.BlockSpec(memory_space=pltpu.VMEM)
LIMIT = 48 << 20


def frequencies():
    return [0.4 * (k + 1) for k in range(NFREQ)]


def forcing_time(moment):
    return sum(math.cos(w * moment) for w in frequencies())


def call(body, outs, cost, **kw):
    shapes = [jax.ShapeDtypeStruct(s, d) for s, d in outs]
    return pl.pallas_call(
        body,
        out_shape=shapes,
        compiler_params=pltpu.CompilerParams(vmem_limit_bytes=LIMIT),
        cost_estimate=pl.CostEstimate(flops=cost, bytes_accessed=cost, transcendentals=0),
        **kw,
    )


def parities():
    return lax.rem(lax.axis_index("ax"), 2), lax.rem(lax.axis_index("az"), 2)


def pack_rows(outer, inner, odd, first, second):
    for half, ref in enumerate((outer, inner)):
        low = ref[pl.ds(0, 80, stride=8), :]
        high = ref[pl.ds(7, 80, stride=8), :]
        where = pl.ds(half * 80, 80)
        first[where, :] = jnp.where(odd == 0, high, low)
        second[where, :] = jnp.where(odd == 0, low, high)


def split_state(state, outer, inner, first, second):
    odd_x, odd_z = parities()

    def one(j, carry):
        for v in range(NVAR):
            rows = pl.ds(pl.multiple_of(j * 40 + v * 8, 8), 8)
            outer[rows, :] = state[j, v, odd_x]
            inner[rows, :] = state[j, v, 1 - odd_x]
        return carry

    lax.fori_loop(0, NFORCE, one, 0, unroll=4)
    pack_rows(outer, inner, odd_z, first, second)


def split_fixed(forcing, axial, swirl, coupling, f_out, f_in, c_out, c_in, s_out, s_in):
    odd_x, _ = parities()
    sign = jnp.where(odd_x == 0, 1.0, -1.0)

    def one(j, carry):
        for v in range(NVAR):
            rows = pl.ds(pl.multiple_of(j * 40 + v * 8, 8), 8)
            f_out[rows, :] = forcing[j, v, odd_x]
            f_in[rows, :] = forcing[j, v, 1 - odd_x]
        return carry

    lax.fori_loop(0, NFORCE, one, 0, unroll=4)
    for layer, c, s, toward in ((odd_x, c_out, s_out, -sign), (1 - odd_x, c_in, s_in, sign)):
        for v in range(NVAR):
            for w in range(NVAR):
                shift = 6.0 * viscous if v == w else 0.0
                c[pl.ds((v * NVAR + w) * 8, 8), :] = coupling[v, w, layer] - shift
        s[0:8, :] = axial[layer] * (0.5 * toward)
        s[8:16, :] = swirl[layer] * 0.5


def layer_body(inner, stage, gval, refs):
    (own, other, recv, z1, z2, forcing, coupling, speed), rest = refs[:8], refs[8:]
    odd_x, odd_z = parities()
    sign = jnp.where(odd_x == 0, 0.5, -0.5)
    if not inner:
        sign = -sign
    sub = lax.broadcasted_iota(jnp.int32, (8, 128), 0)
    lane = lax.broadcasted_iota(jnp.int32, (8, 128), 1)
    row0, row7, lane0, lane127 = sub == 0, sub == 7, lane == 0, lane == 127
    pick = (sub < 4) == (odd_z == 1)
    base = 80 if inner else 0
    adv, swr = speed[0:8, :], speed[8:16, :]
    if stage == 1:
        start, (out,) = own, rest[:1]
    elif stage in (2, 3):
        start, (out,) = rest[0], rest[1:2]
    else:
        start, y2, y3, out = rest[:4]

    def one(j, carry):
        at = pl.multiple_of(j * 40, 8)
        rows = [pl.ds(at + v * 8, 8) for v in range(NVAR)]
        y = [own[r, :] for r in rows]
        dx, dt, rate = [], [], []
        for v in range(NVAR):
            a, b = other[rows[v], :], recv[rows[v], :]
            n = base + j * NVAR + v
            edge = jnp.where(
                pick,
                jnp.broadcast_to(z1[pl.ds(n, 1), :], (8, 128)),
                jnp.broadcast_to(z2[pl.ds(n, 1), :], (8, 128)),
            )
            tm = jnp.where(row0, edge, pltpu.roll(y[v], 1, 0))
            tp = jnp.where(row7, edge, pltpu.roll(y[v], 7, 0))
            rm = jnp.where(lane0, 0.0, pltpu.roll(y[v], 1, 1))
            rp = jnp.where(lane127, 0.0, pltpu.roll(y[v], 127, 1))
            dx.append(b - a)
            dt.append(tp - tm)
            lap = (a + b) + (tm + tp) + (rm + rp)
            total = viscous * lap + gval * forcing[rows[v], :] - adv * dx[v] - swr * dt[v]
            for w in range(NVAR):
                total = total + coupling[(v * NVAR + w) * 8 : (v * NVAR + w) * 8 + 8, :] * y[w]
            rate.append(total)
        rate[1] = rate[1] - sign * dx[4]
        rate[2] = rate[2] - 0.5 * dt[4]
        rate[4] = rate[4] - (sign * dx[1] + 0.5 * dt[2])
        for v in range(NVAR):
            q = y[v] if stage == 1 else start[rows[v], :]
            if stage < 4:
                weight = step_size if stage == 3 else 0.5 * step_size
                out[rows[v], :] = q + weight * rate[v]
            else:
                mean = (y2[rows[v], :] - q) + (2.0 * y3[rows[v], :] + y[v])
                out[rows[v], :] = mean * (1.0 / 3.0) + (step_size / 6.0) * rate[v]
        return carry

    lax.fori_loop(0, NFORCE, one, 0, unroll=2)


def outer_layer(stage, gval, *args):
    def body(*refs):
        layer_body(False, stage, gval, refs)

    return call(body, [((ROWS, 128), F32)], 1 << 20, in_specs=[VMEM] * len(args), out_specs=[VMEM])(*args)[0]


def inner_layer(stage, gval, new_outer, *args):
    def body(done, *refs):
        layer_body(True, stage, gval, refs)
        _, odd_z = parities()
        pack_rows(done, refs[-3], odd_z, refs[-2], refs[-1])

    return call(
        body,
        [((ROWS, 128), F32), ((160, 128), F32), ((160, 128), F32)],
        1 << 20,
        in_specs=[VMEM] * (len(args) + 1),
        out_specs=[VMEM] * 3,
    )(new_outer, *args)


def swaps():
    core = [(i, i ^ 1) for i in range(32)]
    chip = [(i, i + 1) for i in range(1, 31, 2)]
    chip += [(b, a) for a, b in chip]
    z1 = [(i, i ^ 1) for i in range(8)]
    z2 = [(i, (i + 1) % 8) for i in range(1, 8, 2)]
    z2 += [(b, a) for a, b in z2]
    return core, chip, z1, z2


def three_parts(x):
    high = x.astype(BF16)
    rest = x - high.astype(F32)
    mid = rest.astype(BF16)
    low = (rest - mid.astype(F32)).astype(BF16)
    return high, mid, low


def gram_body(first_out, first_in, last_out, last_in, final, parts, packed, sem):
    odd_x, _ = parities()
    copies = [
        pltpu.make_async_copy(ref, final.at[:, :, at], sem.at[i])
        for i, (ref, at) in enumerate(((last_out, odd_x), (last_in, 1 - odd_x)))
    ]
    for copy in copies:
        copy.start()
    layers = ((first_out, last_out), (first_in, last_in))
    total = jnp.zeros((96, 96), F32)
    for v in range(NVAR):
        for half, pair in enumerate(layers):
            for t in range(8):
                lanes = pl.ds(half * 1024 + t * 128, 128)
                for n, ref in enumerate(pair):
                    x = ref.reshape(ROWS, 128)[pl.ds(v * 8 + t, NFORCE, stride=40), :]
                    high, mid, low = three_parts(x)
                    for place, part in enumerate((high, mid, low, high, mid, high)):
                        parts[v, pl.ds(place * 32 + n * 16, 16), lanes] = part
        block = parts[v, 0:96, :]
        total = total + lax.dot_general(
            block, block, (((1,), (1,)), ((), ())), preferred_element_type=F32
        )
    small = total[0:32] + total[32:64] + total[64:96]
    small = small[:, 0:32] + small[:, 32:64] + small[:, 64:96]
    flat = jnp.concatenate([small[8 * a : 8 * a + 8] for a in range(4)], axis=1)
    for i in range(32):
        packed[i] = flat
    for copy in copies:
        copy.wait()


def gram_parts(first_out, first_in, last_out, last_in):
    cube = lambda x: x.reshape(NFORCE, NVAR, 8, 128)
    return call(
        gram_body,
        [
            ((NFORCE, NVAR, 2, 8, 128), F32),
            ((NVAR, 192, 2048), BF16),
            ((32, 8, 128), F32),
        ],
        1 << 22,
        in_specs=[VMEM] * 4,
        out_specs=[pl.BlockSpec(memory_space=pl.ANY), VMEM, VMEM],
        scratch_shapes=[pltpu.SemaphoreType.DMA((2,))],
    )(*map(cube, (first_out, first_in, last_out, last_in)))


def lane_tables():
    rows = []
    for k, w in enumerate(frequencies()):
        for j in range(NFORCE):
            for c in range(2):
                f = math.cos if c == 0 else (lambda a: -math.sin(a))
                rows.append(
                    (
                        math.cos(w * step_size),
                        float(j),
                        f(w * step_size) * step_size,
                        f(w * 2 * step_size) * step_size,
                    )
                )
    table = np.zeros((8, 256), np.float32)
    table[:4] = np.array(rows).T
    return table


def factor(gathered, table, weights, upper, work):
    gram = gathered[0]
    for i in range(1, 8):
        gram = gram + gathered[i]
    cells = 64.0 * 64.0 * 128.0
    gram = gram * (step_size * step_size / cells)
    both = gram + pltpu.roll(gram, 48, 1)
    cross = pltpu.roll(gram, 112, 1) + pltpu.roll(gram, 64, 1)
    cosine = table[0:1, :]
    wanted = table[1:2, :]
    rows, inv = [], []
    sub = lax.broadcasted_iota(jnp.int32, (16, 256), 0)
    for i in range(NFORCE):
        column = lambda m: jnp.concatenate(
            [jnp.broadcast_to(m[:, a * 32 + i : a * 32 + i + 1], (8, 256)) for a in range(2)], axis=0
        )
        rows.append(column(both) + cosine * column(cross))
        inv.append(jnp.where(sub == i, 1.0, 0.0))
    low = jnp.zeros((16, 256), F32)
    up = jnp.zeros((16, 256), F32)
    for p in range(NFORCE):
        pivot = rows[p][p : p + 1, :]
        scaled = rows[p] * (1.0 / pivot)
        root = lax.rsqrt(pivot)
        root = root * (1.5 - 0.5 * pivot * root * root)
        mine = wanted == float(p)
        low = jnp.where(mine, inv[p] * root, low)
        up = jnp.where(mine & (sub >= p), rows[p] * root, up)
        for i in range(p + 1, NFORCE):
            m = scaled[i : i + 1, :]
            rows[i] = rows[i] - m * rows[p]
            inv[i] = inv[i] - m * inv[p]
    side = jnp.concatenate([low * table[2:3, :], low * table[3:4, :]], axis=0)
    high, mid, tail = (x.astype(F32) for x in three_parts(side))
    stack = jnp.concatenate([high, high, high, mid, mid, tail, up, jnp.zeros((48, 256), F32)], axis=0)
    turned = stack.T
    weights[...] = turned[:, 0:192].astype(BF16)
    work[...] = turned[:, 128:256]
    upper[...] = work[pl.ds(0, 128, stride=2), :][:, 64:80].reshape(NFREQ, NFORCE, NFORCE)


def basis_body(gathered, table, parts, basis, upper, weights, work):
    @pl.when(pl.program_id(0) == 0)
    def _():
        factor(gathered, table, weights, upper, work)

    odd_x, _ = parities()
    flat = basis.reshape(256 * 16, 128)
    for half in range(2):
        at = odd_x if half == 0 else 1 - odd_x
        for t in range(0, 8, 2):
            lanes = pl.ds(half * 1024 + t * 128, 256)
            block = jnp.dot(weights[...], parts[0, :, lanes], preferred_element_type=F32)
            for u in range(2):
                flat[pl.ds(at * 8 + t + u, 256, stride=16), :] = block[:, u * 128 : u * 128 + 128]


def basis_of(gathered, parts):
    whole = lambda *shape: pl.BlockSpec(shape, lambda v: (0,) * len(shape))
    return pl.pallas_call(
        basis_body,
        grid=(NVAR,),
        out_shape=[
            jax.ShapeDtypeStruct((NFREQ, NFORCE, 2, NVAR, 2, 8, 128), F32),
            jax.ShapeDtypeStruct((NFREQ, NFORCE, NFORCE), F32),
        ],
        in_specs=[
            whole(8, 8, 128),
            whole(8, 256),
            pl.BlockSpec((1, 192, 2048), lambda v: (v, 0, 0)),
        ],
        out_specs=[
            pl.BlockSpec((NFREQ, NFORCE, 2, 1, 2, 8, 128), lambda v: (0, 0, 0, v, 0, 0, 0)),
            whole(NFREQ, NFORCE, NFORCE),
        ],
        scratch_shapes=[pltpu.VMEM((256, 192), BF16), pltpu.VMEM((256, 128), F32)],
        compiler_params=pltpu.CompilerParams(vmem_limit_bytes=LIMIT),
    )(gathered, jnp.asarray(lane_tables()), parts)


def on_device(initial_state, forcing, axial_speed, swirl_speed, coupling):
    core, chip, z1, z2 = swaps()
    layer, rows = ((ROWS, 128), F32), ((160, 128), F32)
    outer, inner, first, second = call(
        split_state, [layer, layer, rows, rows], 1 << 20, in_specs=[VMEM], out_specs=[VMEM] * 4
    )(initial_state)
    c, s = ((200, 128), F32), ((16, 128), F32)
    f_out, f_in, c_out, c_in, s_out, s_in = call(
        split_fixed, [layer, layer, c, c, s, s], 1 << 20, in_specs=[VMEM] * 4, out_specs=[VMEM] * 6
    )(forcing, axial_speed, swirl_speed, coupling)

    kept = []
    for step in range(STEPS):
        moment = step * step_size
        times = (moment, moment + 0.5 * step_size, moment + 0.5 * step_size, moment + step_size)
        base = (outer, inner)
        history = []
        for stage in range(1, 5):
            gval = forcing_time(times[stage - 1])
            from_chip = lax.ppermute(outer, "ax", chip)
            from_core = lax.ppermute(inner, "ax", core)
            r1 = lax.ppermute(first, "az", z1)
            r2 = lax.ppermute(second, "az", z2)
            if stage == 1:
                more = ((), ())
            elif stage < 4:
                more = ((base[0],), (base[1],))
            else:
                more = tuple((base[i], history[0][i], history[1][i]) for i in range(2))
            new_outer = outer_layer(stage, gval, outer, inner, from_chip, r1, r2, f_out, c_out, s_out, *more[0])
            new_inner, first, second = inner_layer(
                stage, gval, new_outer, inner, outer, from_core, r1, r2, f_in, c_in, s_in, *more[1]
            )
            outer, inner = new_outer, new_inner
            history.append((outer, inner))
        kept.append((outer, inner))
    final, parts, packed = gram_parts(*kept[0], *kept[1])
    gathered = lax.all_to_all(packed, "ax", 0, 0, tiled=True)
    partial = jnp.broadcast_to(jnp.sum(gathered, axis=0)[None], (8, 8, 128))
    gathered = lax.all_to_all(partial, "az", 0, 0, tiled=True)
    basis, upper = basis_of(gathered, parts)
    return final, basis, upper


def solution(mesh):
    return jax.shard_map(
        on_device,
        mesh=mesh,
        in_specs=(
            P(None, None, "ax", "az", None),
            P(None, None, "ax", "az", None),
            P("ax", "az", None),
            P("ax", "az", None),
            P(None, None, "ax", "az", None),
        ),
        out_specs=(
            P(None, None, "ax", "az", None),
            P(None, None, None, None, "ax", "az", None),
            P(),
        ),
        check_vma=False,
    )
```

profile of v0, /device:TPU:1, one launch (start us, length us, event | category | flops | bytes accessed | tf_op | source)
XLA Modules:
  0.0 140.0 jit_solution(3711989393079018613)
XLA Ops:
  1.8 4.6 %collective-permute-start = (f32[640,128]{1,0:T(8,128)S(1)}, f32[640,128]{1,0:T(8,128)S(1)}, u32[]{:S(2)}, u32[]{:S(2)}) collective-permute-start(f32[640,128]{1,0:T(8,128)S(1)} %get-tuple-element.40.refs_0_.refs_1_.refs_8_), channel_id=1, source_target_pairs={{8,16},{24,32},{40,48},{56,64},{72,80},{88,96},{104,112},{120,128}... | collective-permute-start | bytes 983048 | tf_op jit(solution)/shard_map/ppermute | solution.py:355
  6.5 1.7 %collective-permute-start.1 = (f32[160,128]{1,0:T(8,128)S(1)}, f32[160,128]{1,0:T(8,128)S(1)}, u32[]{:S(2)}, u32[]{:S(2)}) collective-permute-start(f32[160,128]{1,0:T(8,128)S(1)} %get-tuple-element.42), channel_id=1, source_target_pairs={{0,1},{1,0},{2,3},{3,2},{4,5},{5,4},{6,7},{7,6},{8,9},{9,8},{10,11... | collective-permute-start | bytes 245768 | tf_op jit(solution)/shard_map/ppermute | solution.py:357
  8.2 4.7 %collective-permute-start.2 = (f32[160,128]{1,0:T(8,128)S(1)}, f32[160,128]{1,0:T(8,128)S(1)}, u32[]{:S(2)}, u32[]{:S(2)}) collective-permute-start(f32[160,128]{1,0:T(8,128)S(1)} %get-tuple-element.43), channel_id=1, source_target_pairs={{1,2},{3,4},{5,6},{7,0},{2,1},{4,3},{6,5},{0,7},{9,10},{11,12},{13... | collective-permute-start | bytes 245768 | tf_op jit(solution)/shard_map/ppermute | solution.py:358
  17.3 4.1 %collective-permute-start.4 = (f32[640,128]{1,0:T(8,128)S(1)}, f32[640,128]{1,0:T(8,128)S(1)}, u32[]{:S(2)}, u32[]{:S(2)}) collective-permute-start(f32[640,128]{1,0:T(8,128)S(1)} %shard_map.87.done.refs_0_.refs_1_.refs_9_), channel_id=1, source_target_pairs={{8,16},{24,32},{40,48},{56,64},{72,80},{88,96},{104,112},{120,128}... | collective-permute-start | bytes 983048 | tf_op jit(solution)/shard_map/ppermute | solution.py:355
  22.5 1.9 %collective-permute-start.6 = (f32[160,128]{1,0:T(8,128)S(1)}, f32[160,128]{1,0:T(8,128)S(1)}, u32[]{:S(2)}, u32[]{:S(2)}) collective-permute-start(f32[160,128]{1,0:T(8,128)S(1)} %get-tuple-element.52), channel_id=1, source_target_pairs={{1,2},{3,4},{5,6},{7,0},{2,1},{4,3},{6,5},{0,7},{9,10},{11,12},{13... | collective-permute-start | bytes 245768 | tf_op jit(solution)/shard_map/ppermute | solution.py:358
  28.4 3.9 %collective-permute-start.8 = (f32[640,128]{1,0:T(8,128)S(1)}, f32[640,128]{1,0:T(8,128)S(1)}, u32[]{:S(2)}, u32[]{:S(2)}) collective-permute-start(f32[640,128]{1,0:T(8,128)S(1)} %shard_map.89.done.refs_0_.refs_1_.refs_10_), channel_id=1, source_target_pairs={{8,16},{24,32},{40,48},{56,64},{72,80},{88,96},{104,112},{120,128}... | collective-permute-start | bytes 983048 | tf_op jit(solution)/shard_map/ppermute | solution.py:355
  33.9 1.8 %collective-permute-start.10 = (f32[160,128]{1,0:T(8,128)S(1)}, f32[160,128]{1,0:T(8,128)S(1)}, u32[]{:S(2)}, u32[]{:S(2)}) collective-permute-start(f32[160,128]{1,0:T(8,128)S(1)} %get-tuple-element.55), channel_id=1, source_target_pairs={{1,2},{3,4},{5,6},{7,0},{2,1},{4,3},{6,5},{0,7},{9,10},{11,12},{13... | collective-permute-start | bytes 245768 | tf_op jit(solution)/shard_map/ppermute | solution.py:358
  39.3 4.5 %collective-permute-start.12 = (f32[640,128]{1,0:T(8,128)S(1)}, f32[640,128]{1,0:T(8,128)S(1)}, u32[]{:S(2)}, u32[]{:S(2)}) collective-permute-start(f32[640,128]{1,0:T(8,128)S(1)} %shard_map.91.done.refs_0_.refs_1_), channel_id=1, source_target_pairs={{8,16},{24,32},{40,48},{56,64},{72,80},{88,96},{104,112},{120,128}... | collective-permute-start | bytes 983048 | tf_op jit(solution)/shard_map/ppermute | solution.py:355
  45.0 1.9 %collective-permute-start.14 = (f32[160,128]{1,0:T(8,128)S(1)}, f32[160,128]{1,0:T(8,128)S(1)}, u32[]{:S(2)}, u32[]{:S(2)}) collective-permute-start(f32[160,128]{1,0:T(8,128)S(1)} %get-tuple-element.58), channel_id=1, source_target_pairs={{1,2},{3,4},{5,6},{7,0},{2,1},{4,3},{6,5},{0,7},{9,10},{11,12},{13... | collective-permute-start | bytes 245768 | tf_op jit(solution)/shard_map/ppermute | solution.py:358
  46.9 1.7 %collective-permute-done.13.refs_3_ = f32[160,128]{1,0:T(8,128)S(1)} collective-permute-done((f32[160,128]{1,0:T(8,128)S(1)}, f32[160,128]{1,0:T(8,128)S(1)}, u32[]{:S(2)}, u32[]{:S(2)}) %collective-permute-start.13) | collective-permute-done | bytes 81952 | tf_op jit(solution)/shard_map/ppermute | solution.py:357
  50.4 5.5 %collective-permute-start.16 = (f32[640,128]{1,0:T(8,128)S(1)}, f32[640,128]{1,0:T(8,128)S(1)}, u32[]{:S(2)}, u32[]{:S(2)}) collective-permute-start(f32[640,128]{1,0:T(8,128)S(1)} %shard_map.93.done.refs_0_.refs_1_.refs_8_), channel_id=1, source_target_pairs={{8,16},{24,32},{40,48},{56,64},{72,80},{88,96},{104,112},{120,128}... | collective-permute-start | bytes 983048 | tf_op jit(solution)/shard_map/ppermute | solution.py:355
  57.5 1.9 %collective-permute-start.18 = (f32[160,128]{1,0:T(8,128)S(1)}, f32[160,128]{1,0:T(8,128)S(1)}, u32[]{:S(2)}, u32[]{:S(2)}) collective-permute-start(f32[160,128]{1,0:T(8,128)S(1)} %get-tuple-element.61), channel_id=1, source_target_pairs={{1,2},{3,4},{5,6},{7,0},{2,1},{4,3},{6,5},{0,7},{9,10},{11,12},{13... | collective-permute-start | bytes 245768 | tf_op jit(solution)/shard_map/ppermute | solution.py:358
  62.9 4.6 %collective-permute-start.20 = (f32[640,128]{1,0:T(8,128)S(1)}, f32[640,128]{1,0:T(8,128)S(1)}, u32[]{:S(2)}, u32[]{:S(2)}) collective-permute-start(f32[640,128]{1,0:T(8,128)S(1)} %shard_map.95.done.refs_0_.refs_1_.refs_9_), channel_id=1, source_target_pairs={{8,16},{24,32},{40,48},{56,64},{72,80},{88,96},{104,112},{120,128}... | collective-permute-start | bytes 983048 | tf_op jit(solution)/shard_map/ppermute | solution.py:355
  69.0 2.7 %collective-permute-start.22 = (f32[160,128]{1,0:T(8,128)S(1)}, f32[160,128]{1,0:T(8,128)S(1)}, u32[]{:S(2)}, u32[]{:S(2)}) collective-permute-start(f32[160,128]{1,0:T(8,128)S(1)} %get-tuple-element.64), channel_id=1, source_target_pairs={{1,2},{3,4},{5,6},{7,0},{2,1},{4,3},{6,5},{0,7},{9,10},{11,12},{13... | collective-permute-start | bytes 245768 | tf_op jit(solution)/shard_map/ppermute | solution.py:358
  74.4 4.7 %collective-permute-start.24 = (f32[640,128]{1,0:T(8,128)S(1)}, f32[640,128]{1,0:T(8,128)S(1)}, u32[]{:S(2)}, u32[]{:S(2)}) collective-permute-start(f32[640,128]{1,0:T(8,128)S(1)} %shard_map.97.done.refs_0_.refs_1_.refs_10_), channel_id=1, source_target_pairs={{8,16},{24,32},{40,48},{56,64},{72,80},{88,96},{104,112},{120,128}... | collective-permute-start | bytes 983048 | tf_op jit(solution)/shard_map/ppermute | solution.py:355
  80.6 2.7 %collective-permute-start.26 = (f32[160,128]{1,0:T(8,128)S(1)}, f32[160,128]{1,0:T(8,128)S(1)}, u32[]{:S(2)}, u32[]{:S(2)}) collective-permute-start(f32[160,128]{1,0:T(8,128)S(1)} %get-tuple-element.67), channel_id=1, source_target_pairs={{1,2},{3,4},{5,6},{7,0},{2,1},{4,3},{6,5},{0,7},{9,10},{11,12},{13... | collective-permute-start | bytes 245768 | tf_op jit(solution)/shard_map/ppermute | solution.py:358
  86.0 4.8 %collective-permute-start.28 = (f32[640,128]{1,0:T(8,128)S(1)}, f32[640,128]{1,0:T(8,128)S(1)}, u32[]{:S(2)}, u32[]{:S(2)}) collective-permute-start(f32[640,128]{1,0:T(8,128)S(1)} %shard_map.99.done.refs_0_.refs_1_), channel_id=1, source_target_pairs={{8,16},{24,32},{40,48},{56,64},{72,80},{88,96},{104,112},{120,128}... | collective-permute-start | bytes 983048 | tf_op jit(solution)/shard_map/ppermute | solution.py:355
  92.0 2.7 %collective-permute-start.30 = (f32[160,128]{1,0:T(8,128)S(1)}, f32[160,128]{1,0:T(8,128)S(1)}, u32[]{:S(2)}, u32[]{:S(2)}) collective-permute-start(f32[160,128]{1,0:T(8,128)S(1)} %get-tuple-element.70), channel_id=1, source_target_pairs={{1,2},{3,4},{5,6},{7,0},{2,1},{4,3},{6,5},{0,7},{9,10},{11,12},{13... | collective-permute-start | bytes 245768 | tf_op jit(solution)/shard_map/ppermute | solution.py:358
  99.1 1.7 %shard_map.103 = (f32[16,5,2,8,128]{4,3,2,1,0:T(8,128)}, bf16[5,192,2048]{2,1,0:T(8,128)(2,1)S(1)}, f32[32,8,128]{2,1,0:T(8,128)S(1)}) custom-call(f32[16,5,8,128]{3,2,1,0:T(8,128)S(1)} %bitcast.4, f32[16,5,8,128]{3,2,1,0:T(8,128)S(1)} %bitcast.5, f32[16,5,8,128]{3,2,1,0:T(8,128)S(1)} %bitcast.6, f32[16,5,8,128]{3,2,1,0:T(8,128)S(1)} %bitcast.7), custom_call_target="tpu_custom_call" | custom-call | flops 4194304 | bytes 4194304 | tf_op jit(solution)/shard_map/pallas_call | solution.py:223
  100.8 1.9 %copy-done = bf16[5,192,2048]{2,1,0:T(8,128)(2,1)} copy-done((bf16[5,192,2048]{2,1,0:T(8,128)(2,1)}, bf16[5,192,2048]{2,1,0:T(8,128)(2,1)S(1)}, u32[]{:S(2)}) %copy-start) | copy-done | bytes 3932184
  102.7 16.0 %all_to_all.10 = f32[32,8,128]{2,1,0:T(8,128)S(1)} all-to-all(f32[32,8,128]{2,1,0:T(8,128)S(1)} %get-tuple-element.73), channel_id=1, replica_groups=mesh['ax'=32,'az'=8] {'ax'}, dimensions={0} | all-to-all | bytes 262144 | tf_op jit(solution)/shard_map/all_to_all | solution.py:373
  118.8 12.1 %all_to_all.11.gathered = f32[8,8,128]{2,1,0:T(8,128)S(1)} all-to-all(f32[8,8,128]{2,1,0:T(8,128)S(1)} %broadcast_in_dim.2), channel_id=1, replica_groups=mesh['ax'=32,'az'=8] {'az'}, dimensions={0} | all-to-all | bytes 65536 | tf_op jit(solution)/shard_map/all_to_all | solution.py:375
  130.8 2.1 %copy-done.1 = bf16[5,192,2048]{2,1,0:T(8,128)(2,1)S(1)} copy-done((bf16[5,192,2048]{2,1,0:T(8,128)(2,1)S(1)}, bf16[5,192,2048]{2,1,0:T(8,128)(2,1)}, u32[]{:S(2)}) %copy-start.1) | copy-done | bytes 3932184
  133.0 7.0 %shard_map.104 = (f32[8,16,2,5,2,8,128]{6,5,4,3,2,1,0:T(8,128)}, f32[8,16,16]{2,1,0:T(8,128)}) custom-call(f32[8,8,128]{2,1,0:T(8,128)S(1)} %all_to_all.11.gathered, f32[8,256]{1,0:T(8,128)S(1)} %copy-done.7, bf16[5,192,2048]{2,1,0:T(8,128)(2,1)S(1)} %copy-done.1), custom_call_target="tpu_custom_call" | custom-call | tf_op jit(solution)/shard_map/pallas_call | solution.py:315
  (80 shorter events, 37.8 us)
Async XLA Ops:
  1.8 14.6 %collective-permute-start = (f32[640,128]{1,0:T(8,128)S(1)}, f32[640,128]{1,0:T(8,128)S(1)}, u32[]{:S(2)}, u32[]{:S(2)}) collective-permute-start(f32[640,128]{1,0:T(8,128)S(1)} %get-tuple-element.40.refs_0_.refs_1_.refs_8_), channel_id=1, source_target_pairs={{8,16},{24,32},{40,48},{56,64},{72,80},{88,96},{104,112},{120,128}... | collective-permute-start | bytes 983048 | tf_op jit(solution)/shard_map/ppermute | solution.py:355
  6.4 15.0 %collective-permute-start.3 = (f32[640,128]{1,0:T(8,128)S(1)}, f32[640,128]{1,0:T(8,128)S(1)}, u32[]{:S(2)}, u32[]{:S(2)}) collective-permute-start(f32[640,128]{1,0:T(8,128)S(1)} %get-tuple-element.41.refs_1_.refs_0_.refs_8_), channel_id=1, source_target_pairs={{0,8},{8,0},{16,24},{24,16},{32,40},{40,32},{48,56},{56,48},{64,72... | collective-permute-start | bytes 983048 | tf_op jit(solution)/shard_map/ppermute | solution.py:356
  6.5 9.9 %collective-permute-start.1 = (f32[160,128]{1,0:T(8,128)S(1)}, f32[160,128]{1,0:T(8,128)S(1)}, u32[]{:S(2)}, u32[]{:S(2)}) collective-permute-start(f32[160,128]{1,0:T(8,128)S(1)} %get-tuple-element.42), channel_id=1, source_target_pairs={{0,1},{1,0},{2,3},{3,2},{4,5},{5,4},{6,7},{7,6},{8,9},{9,8},{10,11... | collective-permute-start | bytes 245768 | tf_op jit(solution)/shard_map/ppermute | solution.py:357
  8.2 8.2 %collective-permute-start.2 = (f32[160,128]{1,0:T(8,128)S(1)}, f32[160,128]{1,0:T(8,128)S(1)}, u32[]{:S(2)}, u32[]{:S(2)}) collective-permute-start(f32[160,128]{1,0:T(8,128)S(1)} %get-tuple-element.43), channel_id=1, source_target_pairs={{1,2},{3,4},{5,6},{7,0},{2,1},{4,3},{6,5},{0,7},{9,10},{11,12},{13... | collective-permute-start | bytes 245768 | tf_op jit(solution)/shard_map/ppermute | solution.py:358
  17.3 10.2 %collective-permute-start.4 = (f32[640,128]{1,0:T(8,128)S(1)}, f32[640,128]{1,0:T(8,128)S(1)}, u32[]{:S(2)}, u32[]{:S(2)}) collective-permute-start(f32[640,128]{1,0:T(8,128)S(1)} %shard_map.87.done.refs_0_.refs_1_.refs_9_), channel_id=1, source_target_pairs={{8,16},{24,32},{40,48},{56,64},{72,80},{88,96},{104,112},{120,128}... | collective-permute-start | bytes 983048 | tf_op jit(solution)/shard_map/ppermute | solution.py:355
  22.3 10.1 %collective-permute-start.7 = (f32[640,128]{1,0:T(8,128)S(1)}, f32[640,128]{1,0:T(8,128)S(1)}, u32[]{:S(2)}, u32[]{:S(2)}) collective-permute-start(f32[640,128]{1,0:T(8,128)S(1)} %get-tuple-element.50.refs_1_.refs_0_.refs_9_), channel_id=1, source_target_pairs={{0,8},{8,0},{16,24},{24,16},{32,40},{40,32},{48,56},{56,48},{64,72... | collective-permute-start | bytes 983048 | tf_op jit(solution)/shard_map/ppermute | solution.py:356
  22.5 5.0 %collective-permute-start.6 = (f32[160,128]{1,0:T(8,128)S(1)}, f32[160,128]{1,0:T(8,128)S(1)}, u32[]{:S(2)}, u32[]{:S(2)}) collective-permute-start(f32[160,128]{1,0:T(8,128)S(1)} %get-tuple-element.52), channel_id=1, source_target_pairs={{1,2},{3,4},{5,6},{7,0},{2,1},{4,3},{6,5},{0,7},{9,10},{11,12},{13... | collective-permute-start | bytes 245768 | tf_op jit(solution)/shard_map/ppermute | solution.py:358
  28.4 10.0 %collective-permute-start.8 = (f32[640,128]{1,0:T(8,128)S(1)}, f32[640,128]{1,0:T(8,128)S(1)}, u32[]{:S(2)}, u32[]{:S(2)}) collective-permute-start(f32[640,128]{1,0:T(8,128)S(1)} %shard_map.89.done.refs_0_.refs_1_.refs_10_), channel_id=1, source_target_pairs={{8,16},{24,32},{40,48},{56,64},{72,80},{88,96},{104,112},{120,128}... | collective-permute-start | bytes 983048 | tf_op jit(solution)/shard_map/ppermute | solution.py:355
  33.3 10.5 %collective-permute-start.11 = (f32[640,128]{1,0:T(8,128)S(1)}, f32[640,128]{1,0:T(8,128)S(1)}, u32[]{:S(2)}, u32[]{:S(2)}) collective-permute-start(f32[640,128]{1,0:T(8,128)S(1)} %get-tuple-element.53.refs_1_.refs_0_.refs_10_), channel_id=1, source_target_pairs={{0,8},{8,0},{16,24},{24,16},{32,40},{40,32},{48,56},{56,48},{64,72... | collective-permute-start | bytes 983048 | tf_op jit(solution)/shard_map/ppermute | solution.py:356
  33.9 4.5 %collective-permute-start.10 = (f32[160,128]{1,0:T(8,128)S(1)}, f32[160,128]{1,0:T(8,128)S(1)}, u32[]{:S(2)}, u32[]{:S(2)}) collective-permute-start(f32[160,128]{1,0:T(8,128)S(1)} %get-tuple-element.55), channel_id=1, source_target_pairs={{1,2},{3,4},{5,6},{7,0},{2,1},{4,3},{6,5},{0,7},{9,10},{11,12},{13... | collective-permute-start | bytes 245768 | tf_op jit(solution)/shard_map/ppermute | solution.py:358
  39.3 10.2 %collective-permute-start.12 = (f32[640,128]{1,0:T(8,128)S(1)}, f32[640,128]{1,0:T(8,128)S(1)}, u32[]{:S(2)}, u32[]{:S(2)}) collective-permute-start(f32[640,128]{1,0:T(8,128)S(1)} %shard_map.91.done.refs_0_.refs_1_), channel_id=1, source_target_pairs={{8,16},{24,32},{40,48},{56,64},{72,80},{88,96},{104,112},{120,128}... | collective-permute-start | bytes 983048 | tf_op jit(solution)/shard_map/ppermute | solution.py:355
  44.7 11.2 %collective-permute-start.15 = (f32[640,128]{1,0:T(8,128)S(1)}, f32[640,128]{1,0:T(8,128)S(1)}, u32[]{:S(2)}, u32[]{:S(2)}) collective-permute-start(f32[640,128]{1,0:T(8,128)S(1)} %get-tuple-element.56.refs_1_.refs_0_), channel_id=1, source_target_pairs={{0,8},{8,0},{16,24},{24,16},{32,40},{40,32},{48,56},{56,48},{64,72... | collective-permute-start | bytes 983048 | tf_op jit(solution)/shard_map/ppermute | solution.py:356
  45.0 4.6 %collective-permute-start.14 = (f32[160,128]{1,0:T(8,128)S(1)}, f32[160,128]{1,0:T(8,128)S(1)}, u32[]{:S(2)}, u32[]{:S(2)}) collective-permute-start(f32[160,128]{1,0:T(8,128)S(1)} %get-tuple-element.58), channel_id=1, source_target_pairs={{1,2},{3,4},{5,6},{7,0},{2,1},{4,3},{6,5},{0,7},{9,10},{11,12},{13... | collective-permute-start | bytes 245768 | tf_op jit(solution)/shard_map/ppermute | solution.py:358
  50.4 11.6 %collective-permute-start.16 = (f32[640,128]{1,0:T(8,128)S(1)}, f32[640,128]{1,0:T(8,128)S(1)}, u32[]{:S(2)}, u32[]{:S(2)}) collective-permute-start(f32[640,128]{1,0:T(8,128)S(1)} %shard_map.93.done.refs_0_.refs_1_.refs_8_), channel_id=1, source_target_pairs={{8,16},{24,32},{40,48},{56,64},{72,80},{88,96},{104,112},{120,128}... | collective-permute-start | bytes 983048 | tf_op jit(solution)/shard_map/ppermute | solution.py:355
  56.9 10.6 %collective-permute-start.19 = (f32[640,128]{1,0:T(8,128)S(1)}, f32[640,128]{1,0:T(8,128)S(1)}, u32[]{:S(2)}, u32[]{:S(2)}) collective-permute-start(f32[640,128]{1,0:T(8,128)S(1)} %get-tuple-element.59.refs_1_.refs_0_.refs_8_), channel_id=1, source_target_pairs={{0,8},{8,0},{16,24},{24,16},{32,40},{40,32},{48,56},{56,48},{64,72... | collective-permute-start | bytes 983048 | tf_op jit(solution)/shard_map/ppermute | solution.py:356
  57.5 4.5 %collective-permute-start.18 = (f32[160,128]{1,0:T(8,128)S(1)}, f32[160,128]{1,0:T(8,128)S(1)}, u32[]{:S(2)}, u32[]{:S(2)}) collective-permute-start(f32[160,128]{1,0:T(8,128)S(1)} %get-tuple-element.61), channel_id=1, source_target_pairs={{1,2},{3,4},{5,6},{7,0},{2,1},{4,3},{6,5},{0,7},{9,10},{11,12},{13... | collective-permute-start | bytes 245768 | tf_op jit(solution)/shard_map/ppermute | solution.py:358
  62.9 10.7 %collective-permute-start.20 = (f32[640,128]{1,0:T(8,128)S(1)}, f32[640,128]{1,0:T(8,128)S(1)}, u32[]{:S(2)}, u32[]{:S(2)}) collective-permute-start(f32[640,128]{1,0:T(8,128)S(1)} %shard_map.95.done.refs_0_.refs_1_.refs_9_), channel_id=1, source_target_pairs={{8,16},{24,32},{40,48},{56,64},{72,80},{88,96},{104,112},{120,128}... | collective-permute-start | bytes 983048 | tf_op jit(solution)/shard_map/ppermute | solution.py:355
  68.4 10.7 %collective-permute-start.23 = (f32[640,128]{1,0:T(8,128)S(1)}, f32[640,128]{1,0:T(8,128)S(1)}, u32[]{:S(2)}, u32[]{:S(2)}) collective-permute-start(f32[640,128]{1,0:T(8,128)S(1)} %get-tuple-element.62.refs_1_.refs_0_.refs_9_), channel_id=1, source_target_pairs={{0,8},{8,0},{16,24},{24,16},{32,40},{40,32},{48,56},{56,48},{64,72... | collective-permute-start | bytes 983048 | tf_op jit(solution)/shard_map/ppermute | solution.py:356
  69.0 4.5 %collective-permute-start.22 = (f32[160,128]{1,0:T(8,128)S(1)}, f32[160,128]{1,0:T(8,128)S(1)}, u32[]{:S(2)}, u32[]{:S(2)}) collective-permute-start(f32[160,128]{1,0:T(8,128)S(1)} %get-tuple-element.64), channel_id=1, source_target_pairs={{1,2},{3,4},{5,6},{7,0},{2,1},{4,3},{6,5},{0,7},{9,10},{11,12},{13... | collective-permute-start | bytes 245768 | tf_op jit(solution)/shard_map/ppermute | solution.py:358
  74.4 10.7 %collective-permute-start.24 = (f32[640,128]{1,0:T(8,128)S(1)}, f32[640,128]{1,0:T(8,128)S(1)}, u32[]{:S(2)}, u32[]{:S(2)}) collective-permute-start(f32[640,128]{1,0:T(8,128)S(1)} %shard_map.97.done.refs_0_.refs_1_.refs_10_), channel_id=1, source_target_pairs={{8,16},{24,32},{40,48},{56,64},{72,80},{88,96},{104,112},{120,128}... | collective-permute-start | bytes 983048 | tf_op jit(solution)/shard_map/ppermute | solution.py:355
  80.0 10.8 %collective-permute-start.27 = (f32[640,128]{1,0:T(8,128)S(1)}, f32[640,128]{1,0:T(8,128)S(1)}, u32[]{:S(2)}, u32[]{:S(2)}) collective-permute-start(f32[640,128]{1,0:T(8,128)S(1)} %get-tuple-element.65.refs_1_.refs_0_.refs_10_), channel_id=1, source_target_pairs={{0,8},{8,0},{16,24},{24,16},{32,40},{40,32},{48,56},{56,48},{64,72... | collective-permute-start | bytes 983048 | tf_op jit(solution)/shard_map/ppermute | solution.py:356
  86.0 10.5 %collective-permute-start.28 = (f32[640,128]{1,0:T(8,128)S(1)}, f32[640,128]{1,0:T(8,128)S(1)}, u32[]{:S(2)}, u32[]{:S(2)}) collective-permute-start(f32[640,128]{1,0:T(8,128)S(1)} %shard_map.99.done.refs_0_.refs_1_), channel_id=1, source_target_pairs={{8,16},{24,32},{40,48},{56,64},{72,80},{88,96},{104,112},{120,128}... | collective-permute-start | bytes 983048 | tf_op jit(solution)/shard_map/ppermute | solution.py:355
  91.8 5.7 %collective-permute-start.31 = (f32[640,128]{1,0:T(8,128)S(1)}, f32[640,128]{1,0:T(8,128)S(1)}, u32[]{:S(2)}, u32[]{:S(2)}) collective-permute-start(f32[640,128]{1,0:T(8,128)S(1)} %get-tuple-element.68.refs_1_.refs_0_), channel_id=1, source_target_pairs={{0,8},{8,0},{16,24},{24,16},{32,40},{40,32},{48,56},{56,48},{64,72... | collective-permute-start | bytes 983048 | tf_op jit(solution)/shard_map/ppermute | solution.py:356
  92.0 4.6 %collective-permute-start.30 = (f32[160,128]{1,0:T(8,128)S(1)}, f32[160,128]{1,0:T(8,128)S(1)}, u32[]{:S(2)}, u32[]{:S(2)}) collective-permute-start(f32[160,128]{1,0:T(8,128)S(1)} %get-tuple-element.70), channel_id=1, source_target_pairs={{1,2},{3,4},{5,6},{7,0},{2,1},{4,3},{6,5},{0,7},{9,10},{11,12},{13... | collective-permute-start | bytes 245768 | tf_op jit(solution)/shard_map/ppermute | solution.py:358
  (16 other events, 112.9 us)
where the time goes:
time: 141 us; the launch traced here: 140 us
  starting transfers between devices  61.8 us (44%)
  blocking collectives  28 us (20%)
  Pallas kernels  24 us (17%)
  waiting for transfers between devices  16.6 us (12%)
  local copies, waits for them, and re-layouts  8.53 us (6%)
    ppermute x8, starting transfers between devices, on_device(): from_chip = lax.ppermute(outer, 'ax', chip)  36.7 us
    ppermute x8, starting transfers between devices, on_device(): r2 = lax.ppermute(second, 'az', z2)  20.3 us
    all_to_all x1, blocking collectives, on_device(): gathered = lax.all_to_all(packed, 'ax', 0, 0, tiled=True)  16 us
    all_to_all x1, blocking collectives, on_device(): gathered = lax.all_to_all(partial, 'az', 0, 0, tiled=True)  12.1 us
    unnamed x16, local copies, waits for them, and re-layouts  8.53 us
    ppermute x8, waiting for transfers between devices, on_device(): r2 = lax.ppermute(second, 'az', z2)  8.45 us
    ppermute x8, waiting for transfers between devices, on_device(): r1 = lax.ppermute(first, 'az', z1)  8.08 us
    pallas_call x8, Pallas kernels, inner_layer(): call(body, [((ROWS, 128), F32), ((160, 128), F32), ((160, 128), F32)], 1...  8.04 us
  transfers between devices with their start and end apart: 32, of which 14 were waited for; matrix products, arithmetic and copies ran while one was open for 0% of the time, Pallas kernels for 10%

commit v1 on v0

--- a/solution.py
+++ b/solution.py
@@ -18,6 +18,7 @@
 F32, BF16 = jnp.float32, jnp.bfloat16
 VMEM = pl.BlockSpec(memory_space=pltpu.VMEM)
 LIMIT = 48 << 20
+UNROLL = 4
 
 
 def frequencies():
@@ -95,55 +96,77 @@
         sign = -sign
     sub = lax.broadcasted_iota(jnp.int32, (8, 128), 0)
     lane = lax.broadcasted_iota(jnp.int32, (8, 128), 1)
-    row0, row7, lane0, lane127 = sub == 0, sub == 7, lane == 0, lane == 127
+    row0, row7 = sub == 0, sub == 7
+    from_low = jnp.where(lane == 0, 0.0, viscous)
+    from_high = jnp.where(lane == 127, 0.0, viscous)
     pick = (sub < 4) == (odd_z == 1)
     base = 80 if inner else 0
     adv, swr = speed[0:8, :], speed[8:16, :]
+    c_other, c_recv = viscous + adv, viscous - adv
+    c_minus, c_plus = viscous + swr, viscous - swr
+    edge_of_domain = None
+    if not inner:
+        position = lax.axis_index("ax")
+        inside = jnp.where((position > 0) & (position < 31), 1.0, 0.0)
+        c_recv = c_recv * inside
+        edge_of_domain = sign * inside
+    c_dx = sign if inner else edge_of_domain
     if stage == 1:
         start, (out,) = own, rest[:1]
     elif stage in (2, 3):
         start, (out,) = rest[0], rest[1:2]
     else:
         start, y2, y3, out = rest[:4]
-
-    def one(j, carry):
-        at = pl.multiple_of(j * 40, 8)
-        rows = [pl.ds(at + v * 8, 8) for v in range(NVAR)]
-        y = [own[r, :] for r in rows]
-        dx, dt, rate = [], [], []
-        for v in range(NVAR):
-            a, b = other[rows[v], :], recv[rows[v], :]
-            n = base + j * NVAR + v
-            edge = jnp.where(
-                pick,
-                jnp.broadcast_to(z1[pl.ds(n, 1), :], (8, 128)),
-                jnp.broadcast_to(z2[pl.ds(n, 1), :], (8, 128)),
-            )
-            tm = jnp.where(row0, edge, pltpu.roll(y[v], 1, 0))
-            tp = jnp.where(row7, edge, pltpu.roll(y[v], 7, 0))
-            rm = jnp.where(lane0, 0.0, pltpu.roll(y[v], 1, 1))
-            rp = jnp.where(lane127, 0.0, pltpu.roll(y[v], 127, 1))
-            dx.append(b - a)
-            dt.append(tp - tm)
-            lap = (a + b) + (tm + tp) + (rm + rp)
-            total = viscous * lap + gval * forcing[rows[v], :] - adv * dx[v] - swr * dt[v]
+    group = 2
+
+    def one(block, carry):
+        at = [pl.multiple_of((block * group + g) * 40, 8) for g in range(group)]
+        y = [[own[pl.ds(at[g] + v * 8, 8), :] for v in range(NVAR)] for g in range(group)]
+        press = [{} for _ in range(group)]
+        rate = [{} for _ in range(group)]
+        for v in (4, 1, 2, 0, 3):
+            for g in range(group):
+                rows = pl.ds(at[g] + v * 8, 8)
+                a, b = other[rows, :], recv[rows, :]
+                n = base + (block * group + g) * NVAR + v
+                edge = jnp.where(
+                    pick,
+                    jnp.broadcast_to(z1[pl.ds(n, 1), :], (8, 128)),
+                    jnp.broadcast_to(z2[pl.ds(n, 1), :], (8, 128)),
+                )
+                me = y[g][v]
+                tm = jnp.where(row0, edge, pltpu.roll(me, 1, 0))
+                tp = jnp.where(row7, edge, pltpu.roll(me, 7, 0))
+                if v in (1, 4):
+                    press[g]["x", v] = b * c_dx - a * sign
+                if v in (2, 4):
+                    press[g]["t", v] = 0.5 * (tp - tm)
+                rate[g][v] = (
+                    (c_other * a + c_recv * b)
+                    + (c_minus * tm + c_plus * tp)
+                    + (from_low * pltpu.roll(me, 1, 1) + from_high * pltpu.roll(me, 127, 1))
+                    + gval * forcing[rows, :]
+                )
             for w in range(NVAR):
-                total = total + coupling[(v * NVAR + w) * 8 : (v * NVAR + w) * 8 + 8, :] * y[w]
-            rate.append(total)
-        rate[1] = rate[1] - sign * dx[4]
-        rate[2] = rate[2] - 0.5 * dt[4]
-        rate[4] = rate[4] - (sign * dx[1] + 0.5 * dt[2])
-        for v in range(NVAR):
-            q = y[v] if stage == 1 else start[rows[v], :]
-            if stage < 4:
-                weight = step_size if stage == 3 else 0.5 * step_size
-                out[rows[v], :] = q + weight * rate[v]
-            else:
-                mean = (y2[rows[v], :] - q) + (2.0 * y3[rows[v], :] + y[v])
-                out[rows[v], :] = mean * (1.0 / 3.0) + (step_size / 6.0) * rate[v]
+                c = coupling[(v * NVAR + w) * 8 : (v * NVAR + w) * 8 + 8, :]
+                for g in range(group):
+                    rate[g][v] = rate[g][v] + c * y[g][w]
+        for g in range(group):
+            rate[g][1] = rate[g][1] - press[g]["x", 4]
+            rate[g][2] = rate[g][2] - press[g]["t", 4]
+            rate[g][4] = rate[g][4] - (press[g]["x", 1] + press[g]["t", 2])
+            for v in range(NVAR):
+                rows = pl.ds(at[g] + v * 8, 8)
+                q = y[g][v] if stage == 1 else start[rows, :]
+                if stage < 4:
+                    weight = step_size if stage == 3 else 0.5 * step_size
+                    out[rows, :] = q + weight * rate[g][v]
+                else:
+                    mean = (y2[rows, :] - q) + (2.0 * y3[rows, :] + y[g][v])
+                    out[rows, :] = mean * (1.0 / 3.0) + (step_size / 6.0) * rate[g][v]
         return carry
 
-    lax.fori_loop(0, NFORCE, one, 0, unroll=2)
+    lax.fori_loop(0, NFORCE // group, one, 0, unroll=UNROLL)
 
 
 def outer_layer(stage, gval, *args):
@@ -170,7 +193,7 @@
 
 def swaps():
     core = [(i, i ^ 1) for i in range(32)]
-    chip = [(i, i + 1) for i in range(1, 31, 2)]
+    chip = [(i, (i + 1) % 32) for i in range(1, 32, 2)]
     chip += [(b, a) for a, b in chip]
     z1 = [(i, i ^ 1) for i in range(8)]
     z2 = [(i, (i + 1) % 8) for i in range(1, 8, 2)]
@@ -186,11 +209,25 @@
     return high, mid, low
 
 
-def gram_body(first_out, first_in, last_out, last_in, final, parts, packed, sem):
+def split_rows(ref, first, stride, parts, n, lanes, places):
+    split = three_parts(ref[pl.ds(first, NFORCE, stride=stride), :])
+    for place in places:
+        parts[pl.ds(place * 32 + n * 16, 16), lanes] = split[(0, 1, 2, 0, 1, 0)[place]]
+
+
+def gram_body(first_out, first_in, last_out, last_in, middle, final, packed, parts, sem):
     odd_x, _ = parities()
+    cube = lambda ref: ref.reshape(NFORCE, NVAR, 8, 128)
     copies = [
-        pltpu.make_async_copy(ref, final.at[:, :, at], sem.at[i])
-        for i, (ref, at) in enumerate(((last_out, odd_x), (last_in, 1 - odd_x)))
+        pltpu.make_async_copy(cube(ref), to.at[:, :, at], sem.at[i])
+        for i, (ref, to, at) in enumerate(
+            (
+                (first_out, middle, odd_x),
+                (first_in, middle, 1 - odd_x),
+                (last_out, final, odd_x),
+                (last_in, final, 1 - odd_x),
+            )
+        )
     ]
     for copy in copies:
         copy.start()
@@ -201,11 +238,8 @@
             for t in range(8):
                 lanes = pl.ds(half * 1024 + t * 128, 128)
                 for n, ref in enumerate(pair):
-                    x = ref.reshape(ROWS, 128)[pl.ds(v * 8 + t, NFORCE, stride=40), :]
-                    high, mid, low = three_parts(x)
-                    for place, part in enumerate((high, mid, low, high, mid, high)):
-                        parts[v, pl.ds(place * 32 + n * 16, 16), lanes] = part
-        block = parts[v, 0:96, :]
+                    split_rows(ref, v * 8 + t, 40, parts.at[v], n, lanes, (0, 1, 2))
+        block = parts[v]
         total = total + lax.dot_general(
             block, block, (((1,), (1,)), ((), ())), preferred_element_type=F32
         )
@@ -219,19 +253,15 @@
 
 
 def gram_parts(first_out, first_in, last_out, last_in):
-    cube = lambda x: x.reshape(NFORCE, NVAR, 8, 128)
+    state = ((NFORCE, NVAR, 2, 8, 128), F32)
     return call(
         gram_body,
-        [
-            ((NFORCE, NVAR, 2, 8, 128), F32),
-            ((NVAR, 192, 2048), BF16),
-            ((32, 8, 128), F32),
-        ],
+        [state, state, ((32, 8, 128), F32)],
         1 << 22,
         in_specs=[VMEM] * 4,
-        out_specs=[pl.BlockSpec(memory_space=pl.ANY), VMEM, VMEM],
-        scratch_shapes=[pltpu.SemaphoreType.DMA((2,))],
-    )(*map(cube, (first_out, first_in, last_out, last_in)))
+        out_specs=[pl.BlockSpec(memory_space=pl.ANY)] * 2 + [VMEM],
+        scratch_shapes=[pltpu.VMEM((NVAR, 96, 2048), BF16), pltpu.SemaphoreType.DMA((4,))],
+    )(first_out, first_in, last_out, last_in)
 
 
 def lane_tables():
@@ -294,24 +324,29 @@
     upper[...] = work[pl.ds(0, 128, stride=2), :][:, 64:80].reshape(NFREQ, NFORCE, NFORCE)
 
 
-def basis_body(gathered, table, parts, basis, upper, weights, work):
+def basis_body(gathered, table, middle, final, basis, upper, weights, work, parts):
+    for n, ref in enumerate((middle, final)):
+        for x in range(2):
+            for t in range(8):
+                lanes = pl.ds(x * 1024 + t * 128, 128)
+                split_rows(ref.reshape(256, 128), x * 8 + t, 16, parts, n, lanes, range(6))
+
     @pl.when(pl.program_id(0) == 0)
     def _():
         factor(gathered, table, weights, upper, work)
 
-    odd_x, _ = parities()
     flat = basis.reshape(256 * 16, 128)
-    for half in range(2):
-        at = odd_x if half == 0 else 1 - odd_x
+    for x in range(2):
         for t in range(0, 8, 2):
-            lanes = pl.ds(half * 1024 + t * 128, 256)
-            block = jnp.dot(weights[...], parts[0, :, lanes], preferred_element_type=F32)
+            lanes = pl.ds(x * 1024 + t * 128, 256)
+            block = jnp.dot(weights[...], parts[:, lanes], preferred_element_type=F32)
             for u in range(2):
-                flat[pl.ds(at * 8 + t + u, 256, stride=16), :] = block[:, u * 128 : u * 128 + 128]
-
-
-def basis_of(gathered, parts):
+                flat[pl.ds(x * 8 + t + u, 256, stride=16), :] = block[:, u * 128 : u * 128 + 128]
+
+
+def basis_of(gathered, middle, final):
     whole = lambda *shape: pl.BlockSpec(shape, lambda v: (0,) * len(shape))
+    field = pl.BlockSpec((NFORCE, 1, 2, 8, 128), lambda v: (0, v, 0, 0, 0))
     return pl.pallas_call(
         basis_body,
         grid=(NVAR,),
@@ -319,18 +354,18 @@
             jax.ShapeDtypeStruct((NFREQ, NFORCE, 2, NVAR, 2, 8, 128), F32),
             jax.ShapeDtypeStruct((NFREQ, NFORCE, NFORCE), F32),
         ],
-        in_specs=[
-            whole(8, 8, 128),
-            whole(8, 256),
-            pl.BlockSpec((1, 192, 2048), lambda v: (v, 0, 0)),
-        ],
+        in_specs=[whole(8, 8, 128), whole(8, 256), field, field],
         out_specs=[
             pl.BlockSpec((NFREQ, NFORCE, 2, 1, 2, 8, 128), lambda v: (0, 0, 0, v, 0, 0, 0)),
             whole(NFREQ, NFORCE, NFORCE),
         ],
-        scratch_shapes=[pltpu.VMEM((256, 192), BF16), pltpu.VMEM((256, 128), F32)],
+        scratch_shapes=[
+            pltpu.VMEM((256, 192), BF16),
+            pltpu.VMEM((256, 128), F32),
+            pltpu.VMEM((192, 2048), BF16),
+        ],
         compiler_params=pltpu.CompilerParams(vmem_limit_bytes=LIMIT),
-    )(gathered, jnp.asarray(lane_tables()), parts)
+    )(gathered, jnp.asarray(lane_tables()), middle, final)
 
 
 def on_device(initial_state, forcing, axial_speed, swirl_speed, coupling):
@@ -369,11 +404,11 @@
             outer, inner = new_outer, new_inner
             history.append((outer, inner))
         kept.append((outer, inner))
-    final, parts, packed = gram_parts(*kept[0], *kept[1])
+    middle, final, packed = gram_parts(*kept[0], *kept[1])
     gathered = lax.all_to_all(packed, "ax", 0, 0, tiled=True)
     partial = jnp.broadcast_to(jnp.sum(gathered, axis=0)[None], (8, 8, 128))
     gathered = lax.all_to_all(partial, "az", 0, 0, tiled=True)
-    basis, upper = basis_of(gathered, parts)
+    basis, upper = basis_of(gathered, middle, final)
     return final, basis, upper
 
 

time: 141 us -> 127 us (0.901)
  Pallas kernels: 24 us -> 17.7 us
  blocking collectives: 28 us -> 24.3 us
  local copies, waits for them, and re-layouts: 8.53 us -> 5.59 us
  starting transfers between devices: 61.8 us -> 60.1 us
    ppermute x8, starting transfers between devices: 36.7 us -> 3.42 us  [on_device(): from_chip = lax.ppermute(outer, 'ax', chip)]
    ppermute x8, starting transfers between devices: 20.3 us -> 36.9 us  [on_device(): r2 = lax.ppermute(second, 'az', z2)]
    ppermute x8, starting transfers between devices: 0.92 us -> 17 us  [on_device(): from_core = lax.ppermute(inner, 'ax', core)]
    ppermute x8, waiting for transfers between devices: 8.45 us -> 17.6 us  [on_device(): r2 = lax.ppermute(second, 'az', z2)]
    ppermute x8, waiting for transfers between devices: 8.08 us -> 0.02 us  [on_device(): r1 = lax.ppermute(first, 'az', z1)]
    all_to_all x1, blocking collectives: 16 us -> 12 us  [on_device(): gathered = lax.all_to_all(packed, 'ax', 0, 0, tiled=True)]
    pallas_call x8, Pallas kernels: 8.04 us -> 4.71 us  [inner_layer(): call(body, [((ROWS, 128), F32), ((160, 128), F32), ((160, 128), F32)], 1...]
    pallas_call x8, Pallas kernels: 7.04 us -> 3.76 us  [outer_layer(): call(body, [((ROWS, 128), F32)], 1 << 20, in_specs=[VMEM] * len(args), ou...]
  transfers between devices with their start and end apart: 32 -> 32, of which waited for: 14 -> 7; matrix products, arithmetic and copies ran while one was open for 0% -> 0% of each run, Pallas kernels for 10% -> 6%
where the time goes in v1:
time: 127 us; the launch traced here: 126 us
  starting transfers between devices  60.1 us (47%)
  blocking collectives  24.3 us (19%)
  Pallas kernels  17.7 us (14%)
  waiting for transfers between devices  17.7 us (14%)
  local copies, waits for them, and re-layouts  5.59 us (4%)
    ppermute x8, starting transfers between devices, on_device(): r2 = lax.ppermute(second, 'az', z2)  36.9 us
    ppermute x8, waiting for transfers between devices, on_device(): r2 = lax.ppermute(second, 'az', z2)  17.6 us
    ppermute x8, starting transfers between devices, on_device(): from_core = lax.ppermute(inner, 'ax', core)  17 us
    all_to_all x1, blocking collectives, on_device(): gathered = lax.all_to_all(partial, 'az', 0, 0, tiled=True)  12.3 us
    all_to_all x1, blocking collectives, on_device(): gathered = lax.all_to_all(packed, 'ax', 0, 0, tiled=True)  12 us
    pallas_call x1, Pallas kernels, basis_of(): pl.pallas_call(basis_body, grid=(NVAR,), out_shape=[jax.ShapeDtypeStruct(...  7.63 us
    unnamed x14, local copies, waits for them, and re-layouts  5.58 us
    pallas_call x8, Pallas kernels, inner_layer(): call(body, [((ROWS, 128), F32), ((160, 128), F32), ((160, 128), F32)], 1...  4.71 us
  transfers between devices with their start and end apart: 32, of which 7 were waited for; matrix products, arithmetic and copies ran while one was open for 0% of the time, Pallas kernels for 6%

profile of v1, /device:TPU:1, one launch (start us, length us, event | category | flops | bytes accessed | tf_op | source)
XLA Modules:
  0.0 126.4 jit_solution(4485376448848943664)
XLA Ops:
  1.8 2.8 %collective-permute-start = (f32[640,128]{1,0:T(8,128)S(1)}, f32[640,128]{1,0:T(8,128)S(1)}, u32[]{:S(2)}, u32[]{:S(2)}) collective-permute-start(f32[640,128]{1,0:T(8,128)S(1)} %get-tuple-element.40.refs_0_.refs_1_.refs_8_), channel_id=1, source_target_pairs={{8,16},{24,32},{40,48},{56,64},{72,80},{88,96},{104,112},{120,128}... | collective-permute-start | bytes 983048 | tf_op jit(solution)/shard_map/ppermute | solution.py:390
  4.6 3.5 %collective-permute-start.3 = (f32[640,128]{1,0:T(8,128)S(1)}, f32[640,128]{1,0:T(8,128)S(1)}, u32[]{:S(2)}, u32[]{:S(2)}) collective-permute-start(f32[640,128]{1,0:T(8,128)S(1)} %get-tuple-element.41.refs_1_.refs_0_.refs_8_), channel_id=1, source_target_pairs={{0,8},{8,0},{16,24},{24,16},{32,40},{40,32},{48,56},{56,48},{64,72... | collective-permute-start | bytes 983048 | tf_op jit(solution)/shard_map/ppermute | solution.py:391
  9.7 4.7 %collective-permute-start.2 = (f32[160,128]{1,0:T(8,128)S(1)}, f32[160,128]{1,0:T(8,128)S(1)}, u32[]{:S(2)}, u32[]{:S(2)}) collective-permute-start(f32[160,128]{1,0:T(8,128)S(1)} %get-tuple-element.43), channel_id=1, source_target_pairs={{1,2},{3,4},{5,6},{7,0},{2,1},{4,3},{6,5},{0,7},{9,10},{11,12},{13... | collective-permute-start | bytes 245768 | tf_op jit(solution)/shard_map/ppermute | solution.py:393
  20.6 4.7 %collective-permute-start.6 = (f32[160,128]{1,0:T(8,128)S(1)}, f32[160,128]{1,0:T(8,128)S(1)}, u32[]{:S(2)}, u32[]{:S(2)}) collective-permute-start(f32[160,128]{1,0:T(8,128)S(1)} %get-tuple-element.52), channel_id=1, source_target_pairs={{1,2},{3,4},{5,6},{7,0},{2,1},{4,3},{6,5},{0,7},{9,10},{11,12},{13... | collective-permute-start | bytes 245768 | tf_op jit(solution)/shard_map/ppermute | solution.py:393
  25.3 2.5 %collective-permute-done.6.refs_4_ = f32[160,128]{1,0:T(8,128)S(1)} collective-permute-done((f32[160,128]{1,0:T(8,128)S(1)}, f32[160,128]{1,0:T(8,128)S(1)}, u32[]{:S(2)}, u32[]{:S(2)}) %collective-permute-start.6) | collective-permute-done | bytes 81952 | tf_op jit(solution)/shard_map/ppermute | solution.py:393
  31.0 4.7 %collective-permute-start.10 = (f32[160,128]{1,0:T(8,128)S(1)}, f32[160,128]{1,0:T(8,128)S(1)}, u32[]{:S(2)}, u32[]{:S(2)}) collective-permute-start(f32[160,128]{1,0:T(8,128)S(1)} %get-tuple-element.55), channel_id=1, source_target_pairs={{1,2},{3,4},{5,6},{7,0},{2,1},{4,3},{6,5},{0,7},{9,10},{11,12},{13... | collective-permute-start | bytes 245768 | tf_op jit(solution)/shard_map/ppermute | solution.py:393
  35.7 2.5 %collective-permute-done.10.refs_4_ = f32[160,128]{1,0:T(8,128)S(1)} collective-permute-done((f32[160,128]{1,0:T(8,128)S(1)}, f32[160,128]{1,0:T(8,128)S(1)}, u32[]{:S(2)}, u32[]{:S(2)}) %collective-permute-start.10) | collective-permute-done | bytes 81952 | tf_op jit(solution)/shard_map/ppermute | solution.py:393
  41.4 4.7 %collective-permute-start.14 = (f32[160,128]{1,0:T(8,128)S(1)}, f32[160,128]{1,0:T(8,128)S(1)}, u32[]{:S(2)}, u32[]{:S(2)}) collective-permute-start(f32[160,128]{1,0:T(8,128)S(1)} %get-tuple-element.58), channel_id=1, source_target_pairs={{1,2},{3,4},{5,6},{7,0},{2,1},{4,3},{6,5},{0,7},{9,10},{11,12},{13... | collective-permute-start | bytes 245768 | tf_op jit(solution)/shard_map/ppermute | solution.py:393
  46.0 2.5 %collective-permute-done.14.refs_4_ = f32[160,128]{1,0:T(8,128)S(1)} collective-permute-done((f32[160,128]{1,0:T(8,128)S(1)}, f32[160,128]{1,0:T(8,128)S(1)}, u32[]{:S(2)}, u32[]{:S(2)}) %collective-permute-start.14) | collective-permute-done | bytes 81952 | tf_op jit(solution)/shard_map/ppermute | solution.py:393
  49.8 2.2 %collective-permute-start.19 = (f32[640,128]{1,0:T(8,128)S(1)}, f32[640,128]{1,0:T(8,128)S(1)}, u32[]{:S(2)}, u32[]{:S(2)}) collective-permute-start(f32[640,128]{1,0:T(8,128)S(1)} %get-tuple-element.59.refs_1_.refs_0_.refs_8_.first_in), channel_id=1, source_target_pairs={{0,8},{8,0},{16,24},{24,16},{32,40},{40,32},{48,56},{56,48},{64,72... | collective-permute-start | bytes 983048 | tf_op jit(solution)/shard_map/ppermute | solution.py:391
  52.1 4.7 %collective-permute-start.18 = (f32[160,128]{1,0:T(8,128)S(1)}, f32[160,128]{1,0:T(8,128)S(1)}, u32[]{:S(2)}, u32[]{:S(2)}) collective-permute-start(f32[160,128]{1,0:T(8,128)S(1)} %get-tuple-element.61), channel_id=1, source_target_pairs={{1,2},{3,4},{5,6},{7,0},{2,1},{4,3},{6,5},{0,7},{9,10},{11,12},{13... | collective-permute-start | bytes 245768 | tf_op jit(solution)/shard_map/ppermute | solution.py:393
  56.7 2.5 %collective-permute-done.18.refs_4_ = f32[160,128]{1,0:T(8,128)S(1)} collective-permute-done((f32[160,128]{1,0:T(8,128)S(1)}, f32[160,128]{1,0:T(8,128)S(1)}, u32[]{:S(2)}, u32[]{:S(2)}) %collective-permute-start.18) | collective-permute-done | bytes 81952 | tf_op jit(solution)/shard_map/ppermute | solution.py:393
  60.3 2.0 %collective-permute-start.23 = (f32[640,128]{1,0:T(8,128)S(1)}, f32[640,128]{1,0:T(8,128)S(1)}, u32[]{:S(2)}, u32[]{:S(2)}) collective-permute-start(f32[640,128]{1,0:T(8,128)S(1)} %get-tuple-element.62.refs_1_.refs_0_.refs_9_), channel_id=1, source_target_pairs={{0,8},{8,0},{16,24},{24,16},{32,40},{40,32},{48,56},{56,48},{64,72... | collective-permute-start | bytes 983048 | tf_op jit(solution)/shard_map/ppermute | solution.py:391
  62.3 4.5 %collective-permute-start.22 = (f32[160,128]{1,0:T(8,128)S(1)}, f32[160,128]{1,0:T(8,128)S(1)}, u32[]{:S(2)}, u32[]{:S(2)}) collective-permute-start(f32[160,128]{1,0:T(8,128)S(1)} %get-tuple-element.64), channel_id=1, source_target_pairs={{1,2},{3,4},{5,6},{7,0},{2,1},{4,3},{6,5},{0,7},{9,10},{11,12},{13... | collective-permute-start | bytes 245768 | tf_op jit(solution)/shard_map/ppermute | solution.py:393
  66.8 2.5 %collective-permute-done.22.refs_4_ = f32[160,128]{1,0:T(8,128)S(1)} collective-permute-done((f32[160,128]{1,0:T(8,128)S(1)}, f32[160,128]{1,0:T(8,128)S(1)}, u32[]{:S(2)}, u32[]{:S(2)}) %collective-permute-start.22) | collective-permute-done | bytes 81952 | tf_op jit(solution)/shard_map/ppermute | solution.py:393
  70.4 2.3 %collective-permute-start.27 = (f32[640,128]{1,0:T(8,128)S(1)}, f32[640,128]{1,0:T(8,128)S(1)}, u32[]{:S(2)}, u32[]{:S(2)}) collective-permute-start(f32[640,128]{1,0:T(8,128)S(1)} %get-tuple-element.65.refs_1_.refs_0_.refs_10_), channel_id=1, source_target_pairs={{0,8},{8,0},{16,24},{24,16},{32,40},{40,32},{48,56},{56,48},{64,72... | collective-permute-start | bytes 983048 | tf_op jit(solution)/shard_map/ppermute | solution.py:391
  72.7 4.5 %collective-permute-start.26 = (f32[160,128]{1,0:T(8,128)S(1)}, f32[160,128]{1,0:T(8,128)S(1)}, u32[]{:S(2)}, u32[]{:S(2)}) collective-permute-start(f32[160,128]{1,0:T(8,128)S(1)} %get-tuple-element.67), channel_id=1, source_target_pairs={{1,2},{3,4},{5,6},{7,0},{2,1},{4,3},{6,5},{0,7},{9,10},{11,12},{13... | collective-permute-start | bytes 245768 | tf_op jit(solution)/shard_map/ppermute | solution.py:393
  77.2 2.5 %collective-permute-done.26.refs_4_ = f32[160,128]{1,0:T(8,128)S(1)} collective-permute-done((f32[160,128]{1,0:T(8,128)S(1)}, f32[160,128]{1,0:T(8,128)S(1)}, u32[]{:S(2)}, u32[]{:S(2)}) %collective-permute-start.26) | collective-permute-done | bytes 81952 | tf_op jit(solution)/shard_map/ppermute | solution.py:393
  80.8 2.2 %collective-permute-start.31 = (f32[640,128]{1,0:T(8,128)S(1)}, f32[640,128]{1,0:T(8,128)S(1)}, u32[]{:S(2)}, u32[]{:S(2)}) collective-permute-start(f32[640,128]{1,0:T(8,128)S(1)} %get-tuple-element.68.refs_1_.refs_0_), channel_id=1, source_target_pairs={{0,8},{8,0},{16,24},{24,16},{32,40},{40,32},{48,56},{56,48},{64,72... | collective-permute-start | bytes 983048 | tf_op jit(solution)/shard_map/ppermute | solution.py:391
  83.0 4.5 %collective-permute-start.30 = (f32[160,128]{1,0:T(8,128)S(1)}, f32[160,128]{1,0:T(8,128)S(1)}, u32[]{:S(2)}, u32[]{:S(2)}) collective-permute-start(f32[160,128]{1,0:T(8,128)S(1)} %get-tuple-element.70), channel_id=1, source_target_pairs={{1,2},{3,4},{5,6},{7,0},{2,1},{4,3},{6,5},{0,7},{9,10},{11,12},{13... | collective-permute-start | bytes 245768 | tf_op jit(solution)/shard_map/ppermute | solution.py:393
  87.5 2.5 %collective-permute-done.30.refs_4_ = f32[160,128]{1,0:T(8,128)S(1)} collective-permute-done((f32[160,128]{1,0:T(8,128)S(1)}, f32[160,128]{1,0:T(8,128)S(1)}, u32[]{:S(2)}, u32[]{:S(2)}) %collective-permute-start.30) | collective-permute-done | bytes 81952 | tf_op jit(solution)/shard_map/ppermute | solution.py:393
  93.3 12.0 %all_to_all.10 = f32[32,8,128]{2,1,0:T(8,128)S(1)} all-to-all(f32[32,8,128]{2,1,0:T(8,128)S(1)} %get-tuple-element.73), channel_id=1, replica_groups=mesh['ax'=32,'az'=8] {'ax'}, dimensions={0} | all-to-all | bytes 262144 | tf_op jit(solution)/shard_map/all_to_all | solution.py:408
  105.4 12.3 %all_to_all.11.gathered = f32[8,8,128]{2,1,0:T(8,128)S(1)} all-to-all(f32[8,8,128]{2,1,0:T(8,128)S(1)} %broadcast_in_dim.2), channel_id=1, replica_groups=mesh['ax'=32,'az'=8] {'az'}, dimensions={0} | all-to-all | bytes 65536 | tf_op jit(solution)/shard_map/all_to_all | solution.py:410
  118.7 7.6 %shard_map.104 = (f32[8,16,2,5,2,8,128]{6,5,4,3,2,1,0:T(8,128)}, f32[8,16,16]{2,1,0:T(8,128)}) custom-call(f32[8,8,128]{2,1,0:T(8,128)S(1)} %all_to_all.11.gathered, f32[8,256]{1,0:T(8,128)S(1)} %copy-done.6, f32[16,5,2,8,128]{4,3,2,1,0:T(8,128)S(1)} %get-tuple-element.74.middle, f32[16,5,2,8,128]{4,3,2,1,0:T(8,128)S(1)} %copy-done.1), custom_call_target="tpu_custom_call" | custom-call | tf_op jit(solution)/shard_map/pallas_call | solution.py:350
  (78 shorter events, 24.1 us)
Async XLA Ops:
  1.8 16.1 %collective-permute-start = (f32[640,128]{1,0:T(8,128)S(1)}, f32[640,128]{1,0:T(8,128)S(1)}, u32[]{:S(2)}, u32[]{:S(2)}) collective-permute-start(f32[640,128]{1,0:T(8,128)S(1)} %get-tuple-element.40.refs_0_.refs_1_.refs_8_), channel_id=1, source_target_pairs={{8,16},{24,32},{40,48},{56,64},{72,80},{88,96},{104,112},{120,128}... | collective-permute-start | bytes 983048 | tf_op jit(solution)/shard_map/ppermute | solution.py:390
  4.6 13.9 %collective-permute-start.3 = (f32[640,128]{1,0:T(8,128)S(1)}, f32[640,128]{1,0:T(8,128)S(1)}, u32[]{:S(2)}, u32[]{:S(2)}) collective-permute-start(f32[640,128]{1,0:T(8,128)S(1)} %get-tuple-element.41.refs_1_.refs_0_.refs_8_), channel_id=1, source_target_pairs={{0,8},{8,0},{16,24},{24,16},{32,40},{40,32},{48,56},{56,48},{64,72... | collective-permute-start | bytes 983048 | tf_op jit(solution)/shard_map/ppermute | solution.py:391
  8.0 9.8 %collective-permute-start.1 = (f32[160,128]{1,0:T(8,128)S(1)}, f32[160,128]{1,0:T(8,128)S(1)}, u32[]{:S(2)}, u32[]{:S(2)}) collective-permute-start(f32[160,128]{1,0:T(8,128)S(1)} %get-tuple-element.42), channel_id=1, source_target_pairs={{0,1},{1,0},{2,3},{3,2},{4,5},{5,4},{6,7},{7,6},{8,9},{9,8},{10,11... | collective-permute-start | bytes 245768 | tf_op jit(solution)/shard_map/ppermute | solution.py:392
  9.7 8.2 %collective-permute-start.2 = (f32[160,128]{1,0:T(8,128)S(1)}, f32[160,128]{1,0:T(8,128)S(1)}, u32[]{:S(2)}, u32[]{:S(2)}) collective-permute-start(f32[160,128]{1,0:T(8,128)S(1)} %get-tuple-element.43), channel_id=1, source_target_pairs={{1,2},{3,4},{5,6},{7,0},{2,1},{4,3},{6,5},{0,7},{9,10},{11,12},{13... | collective-permute-start | bytes 245768 | tf_op jit(solution)/shard_map/ppermute | solution.py:393
  18.3 9.5 %collective-permute-start.4 = (f32[640,128]{1,0:T(8,128)S(1)}, f32[640,128]{1,0:T(8,128)S(1)}, u32[]{:S(2)}, u32[]{:S(2)}) collective-permute-start(f32[640,128]{1,0:T(8,128)S(1)} %shard_map.87.done.refs_0_.refs_1_.refs_9_), channel_id=1, source_target_pairs={{8,16},{24,32},{40,48},{56,64},{72,80},{88,96},{104,112},{120,128}... | collective-permute-start | bytes 983048 | tf_op jit(solution)/shard_map/ppermute | solution.py:390
  18.9 9.4 %collective-permute-start.7 = (f32[640,128]{1,0:T(8,128)S(1)}, f32[640,128]{1,0:T(8,128)S(1)}, u32[]{:S(2)}, u32[]{:S(2)}) collective-permute-start(f32[640,128]{1,0:T(8,128)S(1)} %get-tuple-element.50.refs_1_.refs_0_.refs_9_), channel_id=1, source_target_pairs={{0,8},{8,0},{16,24},{24,16},{32,40},{40,32},{48,56},{56,48},{64,72... | collective-permute-start | bytes 983048 | tf_op jit(solution)/shard_map/ppermute | solution.py:391
  20.6 7.2 %collective-permute-start.6 = (f32[160,128]{1,0:T(8,128)S(1)}, f32[160,128]{1,0:T(8,128)S(1)}, u32[]{:S(2)}, u32[]{:S(2)}) collective-permute-start(f32[160,128]{1,0:T(8,128)S(1)} %get-tuple-element.52), channel_id=1, source_target_pairs={{1,2},{3,4},{5,6},{7,0},{2,1},{4,3},{6,5},{0,7},{9,10},{11,12},{13... | collective-permute-start | bytes 245768 | tf_op jit(solution)/shard_map/ppermute | solution.py:393
  28.3 9.9 %collective-permute-start.8 = (f32[640,128]{1,0:T(8,128)S(1)}, f32[640,128]{1,0:T(8,128)S(1)}, u32[]{:S(2)}, u32[]{:S(2)}) collective-permute-start(f32[640,128]{1,0:T(8,128)S(1)} %shard_map.89.done.refs_0_.refs_1_.refs_10_), channel_id=1, source_target_pairs={{8,16},{24,32},{40,48},{56,64},{72,80},{88,96},{104,112},{120,128}... | collective-permute-start | bytes 983048 | tf_op jit(solution)/shard_map/ppermute | solution.py:390
  28.9 9.9 %collective-permute-start.11 = (f32[640,128]{1,0:T(8,128)S(1)}, f32[640,128]{1,0:T(8,128)S(1)}, u32[]{:S(2)}, u32[]{:S(2)}) collective-permute-start(f32[640,128]{1,0:T(8,128)S(1)} %get-tuple-element.53.refs_1_.refs_0_.refs_10_), channel_id=1, source_target_pairs={{0,8},{8,0},{16,24},{24,16},{32,40},{40,32},{48,56},{56,48},{64,72... | collective-permute-start | bytes 983048 | tf_op jit(solution)/shard_map/ppermute | solution.py:391
  31.0 7.2 %collective-permute-start.10 = (f32[160,128]{1,0:T(8,128)S(1)}, f32[160,128]{1,0:T(8,128)S(1)}, u32[]{:S(2)}, u32[]{:S(2)}) collective-permute-start(f32[160,128]{1,0:T(8,128)S(1)} %get-tuple-element.55), channel_id=1, source_target_pairs={{1,2},{3,4},{5,6},{7,0},{2,1},{4,3},{6,5},{0,7},{9,10},{11,12},{13... | collective-permute-start | bytes 245768 | tf_op jit(solution)/shard_map/ppermute | solution.py:393
  38.7 9.9 %collective-permute-start.12 = (f32[640,128]{1,0:T(8,128)S(1)}, f32[640,128]{1,0:T(8,128)S(1)}, u32[]{:S(2)}, u32[]{:S(2)}) collective-permute-start(f32[640,128]{1,0:T(8,128)S(1)} %shard_map.91.done.refs_0_.refs_1_), channel_id=1, source_target_pairs={{8,16},{24,32},{40,48},{56,64},{72,80},{88,96},{104,112},{120,128}... | collective-permute-start | bytes 983048 | tf_op jit(solution)/shard_map/ppermute | solution.py:390
  39.3 9.9 %collective-permute-start.15 = (f32[640,128]{1,0:T(8,128)S(1)}, f32[640,128]{1,0:T(8,128)S(1)}, u32[]{:S(2)}, u32[]{:S(2)}) collective-permute-start(f32[640,128]{1,0:T(8,128)S(1)} %get-tuple-element.56.refs_1_.refs_0_), channel_id=1, source_target_pairs={{0,8},{8,0},{16,24},{24,16},{32,40},{40,32},{48,56},{56,48},{64,72... | collective-permute-start | bytes 983048 | tf_op jit(solution)/shard_map/ppermute | solution.py:391
  41.4 7.2 %collective-permute-start.14 = (f32[160,128]{1,0:T(8,128)S(1)}, f32[160,128]{1,0:T(8,128)S(1)}, u32[]{:S(2)}, u32[]{:S(2)}) collective-permute-start(f32[160,128]{1,0:T(8,128)S(1)} %get-tuple-element.58), channel_id=1, source_target_pairs={{1,2},{3,4},{5,6},{7,0},{2,1},{4,3},{6,5},{0,7},{9,10},{11,12},{13... | collective-permute-start | bytes 245768 | tf_op jit(solution)/shard_map/ppermute | solution.py:393
  49.1 10.2 %collective-permute-start.16 = (f32[640,128]{1,0:T(8,128)S(1)}, f32[640,128]{1,0:T(8,128)S(1)}, u32[]{:S(2)}, u32[]{:S(2)}) collective-permute-start(f32[640,128]{1,0:T(8,128)S(1)} %shard_map.93.done.refs_0_.refs_1_.refs_8_.first_out), channel_id=1, source_target_pairs={{8,16},{24,32},{40,48},{56,64},{72,80},{88,96},{104,112},{120,128}... | collective-permute-start | bytes 983048 | tf_op jit(solution)/shard_map/ppermute | solution.py:390
  49.8 10.0 %collective-permute-start.19 = (f32[640,128]{1,0:T(8,128)S(1)}, f32[640,128]{1,0:T(8,128)S(1)}, u32[]{:S(2)}, u32[]{:S(2)}) collective-permute-start(f32[640,128]{1,0:T(8,128)S(1)} %get-tuple-element.59.refs_1_.refs_0_.refs_8_.first_in), channel_id=1, source_target_pairs={{0,8},{8,0},{16,24},{24,16},{32,40},{40,32},{48,56},{56,48},{64,72... | collective-permute-start | bytes 983048 | tf_op jit(solution)/shard_map/ppermute | solution.py:391
  52.1 7.2 %collective-permute-start.18 = (f32[160,128]{1,0:T(8,128)S(1)}, f32[160,128]{1,0:T(8,128)S(1)}, u32[]{:S(2)}, u32[]{:S(2)}) collective-permute-start(f32[160,128]{1,0:T(8,128)S(1)} %get-tuple-element.61), channel_id=1, source_target_pairs={{1,2},{3,4},{5,6},{7,0},{2,1},{4,3},{6,5},{0,7},{9,10},{11,12},{13... | collective-permute-start | bytes 245768 | tf_op jit(solution)/shard_map/ppermute | solution.py:393
  59.7 9.6 %collective-permute-start.20 = (f32[640,128]{1,0:T(8,128)S(1)}, f32[640,128]{1,0:T(8,128)S(1)}, u32[]{:S(2)}, u32[]{:S(2)}) collective-permute-start(f32[640,128]{1,0:T(8,128)S(1)} %shard_map.95.done.refs_0_.refs_1_.refs_9_), channel_id=1, source_target_pairs={{8,16},{24,32},{40,48},{56,64},{72,80},{88,96},{104,112},{120,128}... | collective-permute-start | bytes 983048 | tf_op jit(solution)/shard_map/ppermute | solution.py:390
  60.3 9.6 %collective-permute-start.23 = (f32[640,128]{1,0:T(8,128)S(1)}, f32[640,128]{1,0:T(8,128)S(1)}, u32[]{:S(2)}, u32[]{:S(2)}) collective-permute-start(f32[640,128]{1,0:T(8,128)S(1)} %get-tuple-element.62.refs_1_.refs_0_.refs_9_), channel_id=1, source_target_pairs={{0,8},{8,0},{16,24},{24,16},{32,40},{40,32},{48,56},{56,48},{64,72... | collective-permute-start | bytes 983048 | tf_op jit(solution)/shard_map/ppermute | solution.py:391
  62.3 7.1 %collective-permute-start.22 = (f32[160,128]{1,0:T(8,128)S(1)}, f32[160,128]{1,0:T(8,128)S(1)}, u32[]{:S(2)}, u32[]{:S(2)}) collective-permute-start(f32[160,128]{1,0:T(8,128)S(1)} %get-tuple-element.64), channel_id=1, source_target_pairs={{1,2},{3,4},{5,6},{7,0},{2,1},{4,3},{6,5},{0,7},{9,10},{11,12},{13... | collective-permute-start | bytes 245768 | tf_op jit(solution)/shard_map/ppermute | solution.py:393
  69.8 9.9 %collective-permute-start.24 = (f32[640,128]{1,0:T(8,128)S(1)}, f32[640,128]{1,0:T(8,128)S(1)}, u32[]{:S(2)}, u32[]{:S(2)}) collective-permute-start(f32[640,128]{1,0:T(8,128)S(1)} %shard_map.97.done.refs_0_.refs_1_.refs_10_), channel_id=1, source_target_pairs={{8,16},{24,32},{40,48},{56,64},{72,80},{88,96},{104,112},{120,128}... | collective-permute-start | bytes 983048 | tf_op jit(solution)/shard_map/ppermute | solution.py:390
  70.4 9.9 %collective-permute-start.27 = (f32[640,128]{1,0:T(8,128)S(1)}, f32[640,128]{1,0:T(8,128)S(1)}, u32[]{:S(2)}, u32[]{:S(2)}) collective-permute-start(f32[640,128]{1,0:T(8,128)S(1)} %get-tuple-element.65.refs_1_.refs_0_.refs_10_), channel_id=1, source_target_pairs={{0,8},{8,0},{16,24},{24,16},{32,40},{40,32},{48,56},{56,48},{64,72... | collective-permute-start | bytes 983048 | tf_op jit(solution)/shard_map/ppermute | solution.py:391
  72.7 7.1 %collective-permute-start.26 = (f32[160,128]{1,0:T(8,128)S(1)}, f32[160,128]{1,0:T(8,128)S(1)}, u32[]{:S(2)}, u32[]{:S(2)}) collective-permute-start(f32[160,128]{1,0:T(8,128)S(1)} %get-tuple-element.67), channel_id=1, source_target_pairs={{1,2},{3,4},{5,6},{7,0},{2,1},{4,3},{6,5},{0,7},{9,10},{11,12},{13... | collective-permute-start | bytes 245768 | tf_op jit(solution)/shard_map/ppermute | solution.py:393
  80.2 9.9 %collective-permute-start.28 = (f32[640,128]{1,0:T(8,128)S(1)}, f32[640,128]{1,0:T(8,128)S(1)}, u32[]{:S(2)}, u32[]{:S(2)}) collective-permute-start(f32[640,128]{1,0:T(8,128)S(1)} %shard_map.99.done.refs_0_.refs_1_), channel_id=1, source_target_pairs={{8,16},{24,32},{40,48},{56,64},{72,80},{88,96},{104,112},{120,128}... | collective-permute-start | bytes 983048 | tf_op jit(solution)/shard_map/ppermute | solution.py:390
  80.8 9.8 %collective-permute-start.31 = (f32[640,128]{1,0:T(8,128)S(1)}, f32[640,128]{1,0:T(8,128)S(1)}, u32[]{:S(2)}, u32[]{:S(2)}) collective-permute-start(f32[640,128]{1,0:T(8,128)S(1)} %get-tuple-element.68.refs_1_.refs_0_), channel_id=1, source_target_pairs={{0,8},{8,0},{16,24},{24,16},{32,40},{40,32},{48,56},{56,48},{64,72... | collective-permute-start | bytes 983048 | tf_op jit(solution)/shard_map/ppermute | solution.py:391
  (15 other events, 113.9 us)

commit v2 on v1

--- a/solution.py
+++ b/solution.py
@@ -17,6 +17,7 @@
 viscous = 0.1
 F32, BF16 = jnp.float32, jnp.bfloat16
 VMEM = pl.BlockSpec(memory_space=pltpu.VMEM)
+HBM = pl.BlockSpec(memory_space=pltpu.MemorySpace.HBM)
 LIMIT = 48 << 20
 UNROLL = 4
 
@@ -30,7 +31,10 @@
 
 
 def call(body, outs, cost, **kw):
-    shapes = [jax.ShapeDtypeStruct(s, d) for s, d in outs]
+    shapes = [
+        pltpu.MemorySpace.HBM(s, d) if spec is HBM else jax.ShapeDtypeStruct(s, d)
+        for (s, d), spec in zip(outs, kw["out_specs"], strict=True)
+    ]
     return pl.pallas_call(
         body,
         out_shape=shapes,
@@ -53,39 +57,46 @@
         second[where, :] = jnp.where(odd == 0, low, high)
 
 
-def split_state(state, outer, inner, first, second):
+def run_copies(pairs, sem):
+    copies = [pltpu.make_async_copy(a, b, sem.at[i]) for i, (a, b) in enumerate(pairs)]
+    for copy in copies:
+        copy.start()
+    return copies
+
+
+def halves(array, odd_x, outer, inner, pieces):
+    size = NFORCE // pieces
+    pairs = []
+    for at, ref in ((odd_x, outer), (1 - odd_x, inner)):
+        for i in range(pieces):
+            part = pl.ds(i * size, size)
+            pairs.append((array.at[part, :, at], ref.reshape(NFORCE, NVAR, 8, 128).at[part]))
+    return pairs
+
+
+def split_state(state, outer, inner, first, second, sem):
     odd_x, odd_z = parities()
-
-    def one(j, carry):
-        for v in range(NVAR):
-            rows = pl.ds(pl.multiple_of(j * 40 + v * 8, 8), 8)
-            outer[rows, :] = state[j, v, odd_x]
-            inner[rows, :] = state[j, v, 1 - odd_x]
-        return carry
-
-    lax.fori_loop(0, NFORCE, one, 0, unroll=4)
+    for copy in run_copies(halves(state, odd_x, outer, inner, 4), sem):
+        copy.wait()
     pack_rows(outer, inner, odd_z, first, second)
 
 
-def split_fixed(forcing, axial, swirl, coupling, f_out, f_in, c_out, c_in, s_out, s_in):
+def split_fixed(forcing, axial, swirl, coupling, f_out, f_in, c_out, c_in, s_out, s_in, c_all, a_all, w_all, sem):
     odd_x, _ = parities()
     sign = jnp.where(odd_x == 0, 1.0, -1.0)
-
-    def one(j, carry):
-        for v in range(NVAR):
-            rows = pl.ds(pl.multiple_of(j * 40 + v * 8, 8), 8)
-            f_out[rows, :] = forcing[j, v, odd_x]
-            f_in[rows, :] = forcing[j, v, 1 - odd_x]
-        return carry
-
-    lax.fori_loop(0, NFORCE, one, 0, unroll=4)
+    pairs = [(coupling, c_all), (axial, a_all), (swirl, w_all)]
+    copies = run_copies(pairs + halves(forcing, odd_x, f_out, f_in, 4), sem)
+    for copy in copies[:3]:
+        copy.wait()
     for layer, c, s, toward in ((odd_x, c_out, s_out, -sign), (1 - odd_x, c_in, s_in, sign)):
         for v in range(NVAR):
             for w in range(NVAR):
                 shift = 6.0 * viscous if v == w else 0.0
-                c[pl.ds((v * NVAR + w) * 8, 8), :] = coupling[v, w, layer] - shift
-        s[0:8, :] = axial[layer] * (0.5 * toward)
-        s[8:16, :] = swirl[layer] * 0.5
+                c[pl.ds((v * NVAR + w) * 8, 8), :] = c_all[v, w, layer] - shift
+        s[0:8, :] = a_all[layer] * (0.5 * toward)
+        s[8:16, :] = w_all[layer] * 0.5
+    for copy in copies[3:]:
+        copy.wait()
 
 
 def layer_body(inner, stage, gval, refs):
@@ -176,6 +187,13 @@
     return call(body, [((ROWS, 128), F32)], 1 << 20, in_specs=[VMEM] * len(args), out_specs=[VMEM])(*args)[0]
 
 
+def last_layer(stage, gval, *args):
+    def body(*refs):
+        layer_body(True, stage, gval, refs)
+
+    return call(body, [((ROWS, 128), F32)], 1 << 20, in_specs=[VMEM] * len(args), out_specs=[VMEM])(*args)[0]
+
+
 def inner_layer(stage, gval, new_outer, *args):
     def body(done, *refs):
         layer_body(True, stage, gval, refs)
@@ -193,8 +211,10 @@
 
 def swaps():
     core = [(i, i ^ 1) for i in range(32)]
-    chip = [(i, (i + 1) % 32) for i in range(1, 32, 2)]
-    chip += [(b, a) for a, b in chip]
+    pairs = [(i, i + 1) for i in range(1, 31, 2)]
+    pairs += [(b, a) for a, b in pairs]
+    chip = [(a * 8 + z, b * 8 + z) for a, b in pairs for z in range(8)]
+    chip += [(e * 8 + z, e * 8 + (z ^ 1)) for e in (0, 31) for z in range(8)]
     z1 = [(i, i ^ 1) for i in range(8)]
     z2 = [(i, (i + 1) % 8) for i in range(1, 8, 2)]
     z2 += [(b, a) for a, b in z2]
@@ -259,7 +279,7 @@
         [state, state, ((32, 8, 128), F32)],
         1 << 22,
         in_specs=[VMEM] * 4,
-        out_specs=[pl.BlockSpec(memory_space=pl.ANY)] * 2 + [VMEM],
+        out_specs=[HBM] * 2 + [VMEM],
         scratch_shapes=[pltpu.VMEM((NVAR, 96, 2048), BF16), pltpu.SemaphoreType.DMA((4,))],
     )(first_out, first_in, last_out, last_in)
 
@@ -324,60 +344,96 @@
     upper[...] = work[pl.ds(0, 128, stride=2), :][:, 64:80].reshape(NFREQ, NFORCE, NFORCE)
 
 
-def basis_body(gathered, table, middle, final, basis, upper, weights, work, parts):
-    for n, ref in enumerate((middle, final)):
+def basis_body(gathered, table, middle, final, basis, upper, states, weights, work, parts, blocks, sem_in, sem_out):
+    arriving = [
+        [
+            pltpu.make_async_copy(ref.at[:, v], states.at[n, v], sem_in.at[n, v])
+            for n, ref in enumerate((middle, final))
+        ]
+        for v in range(NVAR)
+    ]
+    for pair in arriving:
+        for copy in pair:
+            copy.start()
+    factor(gathered, table, weights, upper, work)
+    leaving = []
+    for v in range(NVAR):
+        for n, copy in enumerate(arriving[v]):
+            copy.wait()
+            rows = states.at[n, v].reshape(256, 128)
+            for x in range(2):
+                for t in range(8):
+                    lanes = pl.ds(x * 1024 + t * 128, 128)
+                    split_rows(rows, x * 8 + t, 16, parts, n, lanes, range(6))
+        flat = blocks.at[v].reshape(256 * 24, 128)
         for x in range(2):
-            for t in range(8):
-                lanes = pl.ds(x * 1024 + t * 128, 128)
-                split_rows(ref.reshape(256, 128), x * 8 + t, 16, parts, n, lanes, range(6))
-
-    @pl.when(pl.program_id(0) == 0)
-    def _():
-        factor(gathered, table, weights, upper, work)
-
-    flat = basis.reshape(256 * 16, 128)
-    for x in range(2):
-        for t in range(0, 8, 2):
-            lanes = pl.ds(x * 1024 + t * 128, 256)
-            block = jnp.dot(weights[...], parts[:, lanes], preferred_element_type=F32)
-            for u in range(2):
-                flat[pl.ds(x * 8 + t + u, 256, stride=16), :] = block[:, u * 128 : u * 128 + 128]
+            for t in range(0, 8, 2):
+                lanes = pl.ds(x * 1024 + t * 128, 256)
+                block = jnp.dot(weights[...], parts[:, lanes], preferred_element_type=F32)
+                for u in range(2):
+                    flat[pl.ds(x * 8 + t + u, 256, stride=24), :] = block[:, u * 128 : u * 128 + 128]
+        for part in range(2):
+            k = pl.ds(part * 4, 4)
+            copy = pltpu.make_async_copy(
+                blocks.at[v, k, :, :, pl.ds(0, 2)], basis.at[k, :, :, v], sem_out.at[v, part]
+            )
+            copy.start()
+            leaving.append(copy)
+    for copy in leaving:
+        copy.wait()
 
 
 def basis_of(gathered, middle, final):
-    whole = lambda *shape: pl.BlockSpec(shape, lambda v: (0,) * len(shape))
-    field = pl.BlockSpec((NFORCE, 1, 2, 8, 128), lambda v: (0, v, 0, 0, 0))
-    return pl.pallas_call(
+    return call(
         basis_body,
-        grid=(NVAR,),
-        out_shape=[
-            jax.ShapeDtypeStruct((NFREQ, NFORCE, 2, NVAR, 2, 8, 128), F32),
-            jax.ShapeDtypeStruct((NFREQ, NFORCE, NFORCE), F32),
+        [
+            ((NFREQ, NFORCE, 2, NVAR, 2, 8, 128), F32),
+            ((NFREQ, NFORCE, NFORCE), F32),
         ],
-        in_specs=[whole(8, 8, 128), whole(8, 256), field, field],
-        out_specs=[
-            pl.BlockSpec((NFREQ, NFORCE, 2, 1, 2, 8, 128), lambda v: (0, 0, 0, v, 0, 0, 0)),
-            whole(NFREQ, NFORCE, NFORCE),
-        ],
+        1 << 24,
+        in_specs=[VMEM, VMEM, HBM, HBM],
+        out_specs=[HBM, VMEM],
         scratch_shapes=[
+            pltpu.VMEM((2, NVAR, NFORCE, 2, 8, 128), F32),
             pltpu.VMEM((256, 192), BF16),
             pltpu.VMEM((256, 128), F32),
             pltpu.VMEM((192, 2048), BF16),
+            pltpu.VMEM((NVAR, NFREQ, NFORCE, 2, 3, 8, 128), F32),
+            pltpu.SemaphoreType.DMA((2, NVAR)),
+            pltpu.SemaphoreType.DMA((NVAR, 2)),
         ],
-        compiler_params=pltpu.CompilerParams(vmem_limit_bytes=LIMIT),
-    )(gathered, jnp.asarray(lane_tables()), middle, final)
+    )(gathered, jnp.asarray(lane_tables()), *in_hbm(middle, final))
+
+
+def in_hbm(*arrays):
+    return [pltpu.with_memory_space_constraint(a, pltpu.MemorySpace.HBM) for a in arrays]
 
 
 def on_device(initial_state, forcing, axial_speed, swirl_speed, coupling):
     core, chip, z1, z2 = swaps()
     layer, rows = ((ROWS, 128), F32), ((160, 128), F32)
     outer, inner, first, second = call(
-        split_state, [layer, layer, rows, rows], 1 << 20, in_specs=[VMEM], out_specs=[VMEM] * 4
-    )(initial_state)
+        split_state,
+        [layer, layer, rows, rows],
+        1 << 20,
+        in_specs=[HBM],
+        out_specs=[VMEM] * 4,
+        scratch_shapes=[pltpu.SemaphoreType.DMA((8,))],
+    )(*in_hbm(initial_state))
     c, s = ((200, 128), F32), ((16, 128), F32)
     f_out, f_in, c_out, c_in, s_out, s_in = call(
-        split_fixed, [layer, layer, c, c, s, s], 1 << 20, in_specs=[VMEM] * 4, out_specs=[VMEM] * 6
-    )(forcing, axial_speed, swirl_speed, coupling)
+        split_fixed,
+        [layer, layer, c, c, s, s],
+        1 << 20,
+        in_specs=[HBM] * 4,
+        out_specs=[VMEM] * 6,
+        scratch_shapes=[
+            pltpu.VMEM((NVAR, NVAR, 2, 8, 128), F32),
+            pltpu.VMEM((2, 8, 128), F32),
+            pltpu.VMEM((2, 8, 128), F32),
+            pltpu.SemaphoreType.DMA((11,)),
+        ],
+    )(*in_hbm(forcing, axial_speed, swirl_speed, coupling))
 
     kept = []
     for step in range(STEPS):
@@ -387,7 +443,7 @@
         history = []
         for stage in range(1, 5):
             gval = forcing_time(times[stage - 1])
-            from_chip = lax.ppermute(outer, "ax", chip)
+            from_chip = lax.ppermute(outer, ("ax", "az"), chip)
             from_core = lax.ppermute(inner, "ax", core)
             r1 = lax.ppermute(first, "az", z1)
             r2 = lax.ppermute(second, "az", z2)
@@ -398,9 +454,11 @@
             else:
                 more = tuple((base[i], history[0][i], history[1][i]) for i in range(2))
             new_outer = outer_layer(stage, gval, outer, inner, from_chip, r1, r2, f_out, c_out, s_out, *more[0])
-            new_inner, first, second = inner_layer(
-                stage, gval, new_outer, inner, outer, from_core, r1, r2, f_in, c_in, s_in, *more[1]
-            )
+            here = (inner, outer, from_core, r1, r2, f_in, c_in, s_in, *more[1])
+            if step == STEPS - 1 and stage == 4:
+                new_inner = last_layer(stage, gval, *here)
+            else:
+                new_inner, first, second = inner_layer(stage, gval, new_outer, *here)
             outer, inner = new_outer, new_inner
             history.append((outer, inner))
         kept.append((outer, inner))

time: 127 us -> 116 us (0.913)
  starting transfers between devices: 60.1 us -> 50.6 us
  local copies, waits for them, and re-layouts: 5.59 us -> 0.01 us
  blocking collectives: 24.3 us -> 27.4 us
    ppermute x8, starting transfers between devices: 17 us -> 4.99 us  [on_device(): from_core = lax.ppermute(inner, 'ax', core)]
    ppermute x8, starting transfers between devices: 36.9 us -> 26 us  [on_device(): r2 = lax.ppermute(second, 'az', z2)]
    ppermute x8, starting transfers between devices: 2.76 us -> 10.8 us  [on_device(): r1 = lax.ppermute(first, 'az', z1)]
    unnamed x14 -> x2, local copies, waits for them, and re-layouts: 5.58 us -> 0.01 us
    ppermute x8, starting transfers between devices: 3.42 us -> 8.86 us  [on_device(): from_chip = lax.ppermute(outer, ('ax', 'az'), chip)]
    all_to_all x1, blocking collectives: 12 us -> 15.3 us  [on_device(): gathered = lax.all_to_all(packed, 'ax', 0, 0, tiled=True)]
    pallas_call x3 -> x4, Pallas kernels: 7.78 us -> 9.93 us  [the longest x1 6.78 us: basis_of(): call(basis_body, [((NFREQ, NFORCE, 2, NVAR, 2, 8, 128), F32), ((NFREQ, NF...]
    ppermute x8, waiting for transfers between devices: 17.6 us -> 16 us  [on_device(): r2 = lax.ppermute(second, 'az', z2)]
  transfers between devices with their start and end apart: 32 -> 32, of which waited for: 7 -> 13; matrix products, arithmetic and copies ran while one was open for 0% -> 0% of each run, Pallas kernels for 6% -> 7%
where the time goes in v2:
time: 116 us
  starting transfers between devices  50.6 us (44%)
  blocking collectives  27.4 us (24%)
  Pallas kernels  18.9 us (16%)
  waiting for transfers between devices  18 us (16%)
    ppermute x8, starting transfers between devices, on_device(): r2 = lax.ppermute(second, 'az', z2)  26 us
    ppermute x8, waiting for transfers between devices, on_device(): r2 = lax.ppermute(second, 'az', z2)  16 us
    all_to_all x1, blocking collectives, on_device(): gathered = lax.all_to_all(packed, 'ax', 0, 0, tiled=True)  15.3 us
    all_to_all x1, blocking collectives, on_device(): gathered = lax.all_to_all(partial, 'az', 0, 0, tiled=True)  12.1 us
    ppermute x8, starting transfers between devices, on_device(): r1 = lax.ppermute(first, 'az', z1)  10.8 us
    ppermute x8, starting transfers between devices, on_device(): from_chip = lax.ppermute(outer, ('ax', 'az'), chip)  8.86 us
    pallas_call x1, Pallas kernels, basis_of(): call(basis_body, [((NFREQ, NFORCE, 2, NVAR, 2, 8, 128), F32), ((NFREQ, NF...  6.78 us
    ppermute x8, starting transfers between devices, on_device(): from_core = lax.ppermute(inner, 'ax', core)  4.99 us
  transfers between devices with their start and end apart: 32, of which 13 were waited for; matrix products, arithmetic and copies ran while one was open for 0% of the time, Pallas kernels for 7%

profile of v2, /device:TPU:1, one launch (start us, length us, event | category | flops | bytes accessed | tf_op | source)
XLA Modules:
  0.0 116.0 jit_solution(13003550521910272452)
XLA Ops:
  1.9 2.8 %collective-permute-start = (f32[640,128]{1,0:T(8,128)S(1)}, f32[640,128]{1,0:T(8,128)S(1)}, u32[]{:S(2)}, u32[]{:S(2)}) collective-permute-start(f32[640,128]{1,0:T(8,128)S(1)} %get-tuple-element.39.refs_0_.refs_1_.refs_8_), channel_id=1, source_target_pairs={{8,16},{9,17},{10,18},{11,19},{12,20},{13,21},{14,22},{15,23},{24,... | collective-permute-start | bytes 983048 | tf_op jit(solution)/shard_map/ppermute | solution.py:446
  7.0 4.0 %collective-permute-start.2 = (f32[160,128]{1,0:T(8,128)S(1)}, f32[160,128]{1,0:T(8,128)S(1)}, u32[]{:S(2)}, u32[]{:S(2)}) collective-permute-start(f32[160,128]{1,0:T(8,128)S(1)} %get-tuple-element.42), channel_id=1, source_target_pairs={{1,2},{3,4},{5,6},{7,0},{2,1},{4,3},{6,5},{0,7},{9,10},{11,12},{13... | collective-permute-start | bytes 245768 | tf_op jit(solution)/shard_map/ppermute | solution.py:449
  13.3 2.9 %collective-permute-start.4 = (f32[640,128]{1,0:T(8,128)S(1)}, f32[640,128]{1,0:T(8,128)S(1)}, u32[]{:S(2)}, u32[]{:S(2)}) collective-permute-start(f32[640,128]{1,0:T(8,128)S(1)} %shard_map.87.done.refs_0_.refs_1_.refs_9_), channel_id=1, source_target_pairs={{8,16},{9,17},{10,18},{11,19},{12,20},{13,21},{14,22},{15,23},{24,... | collective-permute-start | bytes 983048 | tf_op jit(solution)/shard_map/ppermute | solution.py:446
  17.4 3.4 %collective-permute-start.6 = (f32[160,128]{1,0:T(8,128)S(1)}, f32[160,128]{1,0:T(8,128)S(1)}, u32[]{:S(2)}, u32[]{:S(2)}) collective-permute-start(f32[160,128]{1,0:T(8,128)S(1)} %get-tuple-element.51), channel_id=1, source_target_pairs={{1,2},{3,4},{5,6},{7,0},{2,1},{4,3},{6,5},{0,7},{9,10},{11,12},{13... | collective-permute-start | bytes 245768 | tf_op jit(solution)/shard_map/ppermute | solution.py:449
  21.4 1.9 %collective-permute-done.6.refs_4_ = f32[160,128]{1,0:T(8,128)S(1)} collective-permute-done((f32[160,128]{1,0:T(8,128)S(1)}, f32[160,128]{1,0:T(8,128)S(1)}, u32[]{:S(2)}, u32[]{:S(2)}) %collective-permute-start.6) | collective-permute-done | bytes 81952 | tf_op jit(solution)/shard_map/ppermute | solution.py:449
  25.4 1.7 %collective-permute-start.9 = (f32[160,128]{1,0:T(8,128)S(1)}, f32[160,128]{1,0:T(8,128)S(1)}, u32[]{:S(2)}, u32[]{:S(2)}) collective-permute-start(f32[160,128]{1,0:T(8,128)S(1)} %get-tuple-element.53), channel_id=1, source_target_pairs={{0,1},{1,0},{2,3},{3,2},{4,5},{5,4},{6,7},{7,6},{8,9},{9,8},{10,11... | collective-permute-start | bytes 245768 | tf_op jit(solution)/shard_map/ppermute | solution.py:448
  27.1 3.1 %collective-permute-start.10 = (f32[160,128]{1,0:T(8,128)S(1)}, f32[160,128]{1,0:T(8,128)S(1)}, u32[]{:S(2)}, u32[]{:S(2)}) collective-permute-start(f32[160,128]{1,0:T(8,128)S(1)} %get-tuple-element.54), channel_id=1, source_target_pairs={{1,2},{3,4},{5,6},{7,0},{2,1},{4,3},{6,5},{0,7},{9,10},{11,12},{13... | collective-permute-start | bytes 245768 | tf_op jit(solution)/shard_map/ppermute | solution.py:449
  30.2 2.5 %collective-permute-done.10.refs_4_ = f32[160,128]{1,0:T(8,128)S(1)} collective-permute-done((f32[160,128]{1,0:T(8,128)S(1)}, f32[160,128]{1,0:T(8,128)S(1)}, u32[]{:S(2)}, u32[]{:S(2)}) %collective-permute-start.10) | collective-permute-done | bytes 81952 | tf_op jit(solution)/shard_map/ppermute | solution.py:449
  34.7 1.7 %collective-permute-start.13 = (f32[160,128]{1,0:T(8,128)S(1)}, f32[160,128]{1,0:T(8,128)S(1)}, u32[]{:S(2)}, u32[]{:S(2)}) collective-permute-start(f32[160,128]{1,0:T(8,128)S(1)} %get-tuple-element.56), channel_id=1, source_target_pairs={{0,1},{1,0},{2,3},{3,2},{4,5},{5,4},{6,7},{7,6},{8,9},{9,8},{10,11... | collective-permute-start | bytes 245768 | tf_op jit(solution)/shard_map/ppermute | solution.py:448
  36.5 3.1 %collective-permute-start.14 = (f32[160,128]{1,0:T(8,128)S(1)}, f32[160,128]{1,0:T(8,128)S(1)}, u32[]{:S(2)}, u32[]{:S(2)}) collective-permute-start(f32[160,128]{1,0:T(8,128)S(1)} %get-tuple-element.57), channel_id=1, source_target_pairs={{1,2},{3,4},{5,6},{7,0},{2,1},{4,3},{6,5},{0,7},{9,10},{11,12},{13... | collective-permute-start | bytes 245768 | tf_op jit(solution)/shard_map/ppermute | solution.py:449
  39.6 2.5 %collective-permute-done.14.refs_4_ = f32[160,128]{1,0:T(8,128)S(1)} collective-permute-done((f32[160,128]{1,0:T(8,128)S(1)}, f32[160,128]{1,0:T(8,128)S(1)}, u32[]{:S(2)}, u32[]{:S(2)}) %collective-permute-start.14) | collective-permute-done | bytes 81952 | tf_op jit(solution)/shard_map/ppermute | solution.py:449
  46.2 3.1 %collective-permute-start.18 = (f32[160,128]{1,0:T(8,128)S(1)}, f32[160,128]{1,0:T(8,128)S(1)}, u32[]{:S(2)}, u32[]{:S(2)}) collective-permute-start(f32[160,128]{1,0:T(8,128)S(1)} %get-tuple-element.60), channel_id=1, source_target_pairs={{1,2},{3,4},{5,6},{7,0},{2,1},{4,3},{6,5},{0,7},{9,10},{11,12},{13... | collective-permute-start | bytes 245768 | tf_op jit(solution)/shard_map/ppermute | solution.py:449
  49.3 2.5 %collective-permute-done.18.refs_4_ = f32[160,128]{1,0:T(8,128)S(1)} collective-permute-done((f32[160,128]{1,0:T(8,128)S(1)}, f32[160,128]{1,0:T(8,128)S(1)}, u32[]{:S(2)}, u32[]{:S(2)}) %collective-permute-start.18) | collective-permute-done | bytes 81952 | tf_op jit(solution)/shard_map/ppermute | solution.py:449
  53.8 1.7 %collective-permute-start.21 = (f32[160,128]{1,0:T(8,128)S(1)}, f32[160,128]{1,0:T(8,128)S(1)}, u32[]{:S(2)}, u32[]{:S(2)}) collective-permute-start(f32[160,128]{1,0:T(8,128)S(1)} %get-tuple-element.62), channel_id=1, source_target_pairs={{0,1},{1,0},{2,3},{3,2},{4,5},{5,4},{6,7},{7,6},{8,9},{9,8},{10,11... | collective-permute-start | bytes 245768 | tf_op jit(solution)/shard_map/ppermute | solution.py:448
  55.6 2.8 %collective-permute-start.22 = (f32[160,128]{1,0:T(8,128)S(1)}, f32[160,128]{1,0:T(8,128)S(1)}, u32[]{:S(2)}, u32[]{:S(2)}) collective-permute-start(f32[160,128]{1,0:T(8,128)S(1)} %get-tuple-element.63), channel_id=1, source_target_pairs={{1,2},{3,4},{5,6},{7,0},{2,1},{4,3},{6,5},{0,7},{9,10},{11,12},{13... | collective-permute-start | bytes 245768 | tf_op jit(solution)/shard_map/ppermute | solution.py:449
  58.4 2.3 %collective-permute-done.22.refs_4_ = f32[160,128]{1,0:T(8,128)S(1)} collective-permute-done((f32[160,128]{1,0:T(8,128)S(1)}, f32[160,128]{1,0:T(8,128)S(1)}, u32[]{:S(2)}, u32[]{:S(2)}) %collective-permute-start.22) | collective-permute-done | bytes 81952 | tf_op jit(solution)/shard_map/ppermute | solution.py:449
  63.2 1.7 %collective-permute-start.25 = (f32[160,128]{1,0:T(8,128)S(1)}, f32[160,128]{1,0:T(8,128)S(1)}, u32[]{:S(2)}, u32[]{:S(2)}) collective-permute-start(f32[160,128]{1,0:T(8,128)S(1)} %get-tuple-element.65), channel_id=1, source_target_pairs={{0,1},{1,0},{2,3},{3,2},{4,5},{5,4},{6,7},{7,6},{8,9},{9,8},{10,11... | collective-permute-start | bytes 245768 | tf_op jit(solution)/shard_map/ppermute | solution.py:448
  64.9 2.8 %collective-permute-start.26 = (f32[160,128]{1,0:T(8,128)S(1)}, f32[160,128]{1,0:T(8,128)S(1)}, u32[]{:S(2)}, u32[]{:S(2)}) collective-permute-start(f32[160,128]{1,0:T(8,128)S(1)} %get-tuple-element.66), channel_id=1, source_target_pairs={{1,2},{3,4},{5,6},{7,0},{2,1},{4,3},{6,5},{0,7},{9,10},{11,12},{13... | collective-permute-start | bytes 245768 | tf_op jit(solution)/shard_map/ppermute | solution.py:449
  67.8 2.3 %collective-permute-done.26.refs_4_ = f32[160,128]{1,0:T(8,128)S(1)} collective-permute-done((f32[160,128]{1,0:T(8,128)S(1)}, f32[160,128]{1,0:T(8,128)S(1)}, u32[]{:S(2)}, u32[]{:S(2)}) %collective-permute-start.26) | collective-permute-done | bytes 81952 | tf_op jit(solution)/shard_map/ppermute | solution.py:449
  72.5 3.6 %collective-permute-start.30 = (f32[160,128]{1,0:T(8,128)S(1)}, f32[160,128]{1,0:T(8,128)S(1)}, u32[]{:S(2)}, u32[]{:S(2)}) collective-permute-start(f32[160,128]{1,0:T(8,128)S(1)} %get-tuple-element.69), channel_id=1, source_target_pairs={{1,2},{3,4},{5,6},{7,0},{2,1},{4,3},{6,5},{0,7},{9,10},{11,12},{13... | collective-permute-start | bytes 245768 | tf_op jit(solution)/shard_map/ppermute | solution.py:449
  79.8 1.8 %shard_map.103 = (f32[16,5,2,8,128]{4,3,2,1,0:T(8,128)}, f32[16,5,2,8,128]{4,3,2,1,0:T(8,128)}, f32[32,8,128]{2,1,0:T(8,128)S(1)}) custom-call(f32[640,128]{1,0:T(8,128)S(1)} %shard_map.93.done.refs_0_.refs_1_.refs_8_.first_out, f32[640,128]{1,0:T(8,128)S(1)} %get-tuple-element.58.refs_1_.refs_0_.refs_8_.first_in, f32[640,128]{1,0:T(8,128)S(1)} %shard_map.101.last_out, ...), custom_call_target="tpu_custom_call" | custom-call | flops 4194304 | bytes 4194304 | tf_op jit(solution)/shard_map/pallas_call | solution.py:277
  81.6 15.3 %all_to_all.10 = f32[32,8,128]{2,1,0:T(8,128)S(1)} all-to-all(f32[32,8,128]{2,1,0:T(8,128)S(1)} %get-tuple-element.71), channel_id=1, replica_groups=mesh['ax'=32,'az'=8] {'ax'}, dimensions={0} | all-to-all | bytes 262144 | tf_op jit(solution)/shard_map/all_to_all | solution.py:466
  97.0 12.1 %all_to_all.11.gathered = f32[8,8,128]{2,1,0:T(8,128)S(1)} all-to-all(f32[8,8,128]{2,1,0:T(8,128)S(1)} %broadcast_in_dim.2), channel_id=1, replica_groups=mesh['ax'=32,'az'=8] {'az'}, dimensions={0} | all-to-all | bytes 65536 | tf_op jit(solution)/shard_map/all_to_all | solution.py:468
  109.1 6.8 %shard_map.104 = (f32[8,16,2,5,2,8,128]{6,5,4,3,2,1,0:T(8,128)}, f32[8,16,16]{2,1,0:T(8,128)}) custom-call(f32[8,8,128]{2,1,0:T(8,128)S(1)} %all_to_all.11.gathered, f32[8,256]{1,0:T(8,128)S(1)} %copy-done, f32[16,5,2,8,128]{4,3,2,1,0:T(8,128)} %get-tuple-element.72.middle, f32[16,5,2,8,128]{4,3,2,1,0:T(8,128)} %get-tuple-element.36.final), custom_call_target="tpu_custom_call" | custom-call | flops 16777216 | bytes 16777216 | tf_op jit(solution)/shard_map/pallas_call | solution.py:387
  (66 shorter events, 26.3 us)
Async XLA Ops:
  1.9 10.9 %collective-permute-start = (f32[640,128]{1,0:T(8,128)S(1)}, f32[640,128]{1,0:T(8,128)S(1)}, u32[]{:S(2)}, u32[]{:S(2)}) collective-permute-start(f32[640,128]{1,0:T(8,128)S(1)} %get-tuple-element.39.refs_0_.refs_1_.refs_8_), channel_id=1, source_target_pairs={{8,16},{9,17},{10,18},{11,19},{12,20},{13,21},{14,22},{15,23},{24,... | collective-permute-start | bytes 983048 | tf_op jit(solution)/shard_map/ppermute | solution.py:446
  4.7 11.5 %collective-permute-start.3 = (f32[640,128]{1,0:T(8,128)S(1)}, f32[640,128]{1,0:T(8,128)S(1)}, u32[]{:S(2)}, u32[]{:S(2)}) collective-permute-start(f32[640,128]{1,0:T(8,128)S(1)} %get-tuple-element.40.refs_1_.refs_0_.refs_8_), channel_id=1, source_target_pairs={{0,8},{8,0},{16,24},{24,16},{32,40},{40,32},{48,56},{56,48},{64,72... | collective-permute-start | bytes 983048 | tf_op jit(solution)/shard_map/ppermute | solution.py:447
  5.4 6.9 %collective-permute-start.1 = (f32[160,128]{1,0:T(8,128)S(1)}, f32[160,128]{1,0:T(8,128)S(1)}, u32[]{:S(2)}, u32[]{:S(2)}) collective-permute-start(f32[160,128]{1,0:T(8,128)S(1)} %get-tuple-element.41), channel_id=1, source_target_pairs={{0,1},{1,0},{2,3},{3,2},{4,5},{5,4},{6,7},{7,6},{8,9},{9,8},{10,11... | collective-permute-start | bytes 245768 | tf_op jit(solution)/shard_map/ppermute | solution.py:448
  7.0 5.8 %collective-permute-start.2 = (f32[160,128]{1,0:T(8,128)S(1)}, f32[160,128]{1,0:T(8,128)S(1)}, u32[]{:S(2)}, u32[]{:S(2)}) collective-permute-start(f32[160,128]{1,0:T(8,128)S(1)} %get-tuple-element.42), channel_id=1, source_target_pairs={{1,2},{3,4},{5,6},{7,0},{2,1},{4,3},{6,5},{0,7},{9,10},{11,12},{13... | collective-permute-start | bytes 245768 | tf_op jit(solution)/shard_map/ppermute | solution.py:449
  13.3 10.0 %collective-permute-start.4 = (f32[640,128]{1,0:T(8,128)S(1)}, f32[640,128]{1,0:T(8,128)S(1)}, u32[]{:S(2)}, u32[]{:S(2)}) collective-permute-start(f32[640,128]{1,0:T(8,128)S(1)} %shard_map.87.done.refs_0_.refs_1_.refs_9_), channel_id=1, source_target_pairs={{8,16},{9,17},{10,18},{11,19},{12,20},{13,21},{14,22},{15,23},{24,... | collective-permute-start | bytes 983048 | tf_op jit(solution)/shard_map/ppermute | solution.py:446
  16.7 8.1 %collective-permute-start.7 = (f32[640,128]{1,0:T(8,128)S(1)}, f32[640,128]{1,0:T(8,128)S(1)}, u32[]{:S(2)}, u32[]{:S(2)}) collective-permute-start(f32[640,128]{1,0:T(8,128)S(1)} %get-tuple-element.49.refs_1_.refs_0_.refs_9_), channel_id=1, source_target_pairs={{0,8},{8,0},{16,24},{24,16},{32,40},{40,32},{48,56},{56,48},{64,72... | collective-permute-start | bytes 983048 | tf_op jit(solution)/shard_map/ppermute | solution.py:447
  17.4 6.0 %collective-permute-start.6 = (f32[160,128]{1,0:T(8,128)S(1)}, f32[160,128]{1,0:T(8,128)S(1)}, u32[]{:S(2)}, u32[]{:S(2)}) collective-permute-start(f32[160,128]{1,0:T(8,128)S(1)} %get-tuple-element.51), channel_id=1, source_target_pairs={{1,2},{3,4},{5,6},{7,0},{2,1},{4,3},{6,5},{0,7},{9,10},{11,12},{13... | collective-permute-start | bytes 245768 | tf_op jit(solution)/shard_map/ppermute | solution.py:449
  23.8 8.9 %collective-permute-start.8 = (f32[640,128]{1,0:T(8,128)S(1)}, f32[640,128]{1,0:T(8,128)S(1)}, u32[]{:S(2)}, u32[]{:S(2)}) collective-permute-start(f32[640,128]{1,0:T(8,128)S(1)} %shard_map.89.done.refs_0_.refs_1_.refs_10_), channel_id=1, source_target_pairs={{8,16},{9,17},{10,18},{11,19},{12,20},{13,21},{14,22},{15,23},{24,... | collective-permute-start | bytes 983048 | tf_op jit(solution)/shard_map/ppermute | solution.py:446
  25.2 8.0 %collective-permute-start.11 = (f32[640,128]{1,0:T(8,128)S(1)}, f32[640,128]{1,0:T(8,128)S(1)}, u32[]{:S(2)}, u32[]{:S(2)}) collective-permute-start(f32[640,128]{1,0:T(8,128)S(1)} %get-tuple-element.52.refs_1_.refs_0_.refs_10_), channel_id=1, source_target_pairs={{0,8},{8,0},{16,24},{24,16},{32,40},{40,32},{48,56},{56,48},{64,72... | collective-permute-start | bytes 983048 | tf_op jit(solution)/shard_map/ppermute | solution.py:447
  27.1 5.6 %collective-permute-start.10 = (f32[160,128]{1,0:T(8,128)S(1)}, f32[160,128]{1,0:T(8,128)S(1)}, u32[]{:S(2)}, u32[]{:S(2)}) collective-permute-start(f32[160,128]{1,0:T(8,128)S(1)} %get-tuple-element.54), channel_id=1, source_target_pairs={{1,2},{3,4},{5,6},{7,0},{2,1},{4,3},{6,5},{0,7},{9,10},{11,12},{13... | collective-permute-start | bytes 245768 | tf_op jit(solution)/shard_map/ppermute | solution.py:449
  33.2 8.9 %collective-permute-start.12 = (f32[640,128]{1,0:T(8,128)S(1)}, f32[640,128]{1,0:T(8,128)S(1)}, u32[]{:S(2)}, u32[]{:S(2)}) collective-permute-start(f32[640,128]{1,0:T(8,128)S(1)} %shard_map.91.done.refs_0_.refs_1_), channel_id=1, source_target_pairs={{8,16},{9,17},{10,18},{11,19},{12,20},{13,21},{14,22},{15,23},{24,... | collective-permute-start | bytes 983048 | tf_op jit(solution)/shard_map/ppermute | solution.py:446
  33.8 9.3 %collective-permute-start.15 = (f32[640,128]{1,0:T(8,128)S(1)}, f32[640,128]{1,0:T(8,128)S(1)}, u32[]{:S(2)}, u32[]{:S(2)}) collective-permute-start(f32[640,128]{1,0:T(8,128)S(1)} %get-tuple-element.55.refs_1_.refs_0_), channel_id=1, source_target_pairs={{0,8},{8,0},{16,24},{24,16},{32,40},{40,32},{48,56},{56,48},{64,72... | collective-permute-start | bytes 983048 | tf_op jit(solution)/shard_map/ppermute | solution.py:447
  36.5 5.6 %collective-permute-start.14 = (f32[160,128]{1,0:T(8,128)S(1)}, f32[160,128]{1,0:T(8,128)S(1)}, u32[]{:S(2)}, u32[]{:S(2)}) collective-permute-start(f32[160,128]{1,0:T(8,128)S(1)} %get-tuple-element.57), channel_id=1, source_target_pairs={{1,2},{3,4},{5,6},{7,0},{2,1},{4,3},{6,5},{0,7},{9,10},{11,12},{13... | collective-permute-start | bytes 245768 | tf_op jit(solution)/shard_map/ppermute | solution.py:449
  42.6 9.2 %collective-permute-start.16 = (f32[640,128]{1,0:T(8,128)S(1)}, f32[640,128]{1,0:T(8,128)S(1)}, u32[]{:S(2)}, u32[]{:S(2)}) collective-permute-start(f32[640,128]{1,0:T(8,128)S(1)} %shard_map.93.done.refs_0_.refs_1_.refs_8_.first_out), channel_id=1, source_target_pairs={{8,16},{9,17},{10,18},{11,19},{12,20},{13,21},{14,22},{15,23},{24,... | collective-permute-start | bytes 983048 | tf_op jit(solution)/shard_map/ppermute | solution.py:446
  43.6 9.4 %collective-permute-start.19 = (f32[640,128]{1,0:T(8,128)S(1)}, f32[640,128]{1,0:T(8,128)S(1)}, u32[]{:S(2)}, u32[]{:S(2)}) collective-permute-start(f32[640,128]{1,0:T(8,128)S(1)} %get-tuple-element.58.refs_1_.refs_0_.refs_8_.first_in), channel_id=1, source_target_pairs={{0,8},{8,0},{16,24},{24,16},{32,40},{40,32},{48,56},{56,48},{64,72... | collective-permute-start | bytes 983048 | tf_op jit(solution)/shard_map/ppermute | solution.py:447
  46.2 5.6 %collective-permute-start.18 = (f32[160,128]{1,0:T(8,128)S(1)}, f32[160,128]{1,0:T(8,128)S(1)}, u32[]{:S(2)}, u32[]{:S(2)}) collective-permute-start(f32[160,128]{1,0:T(8,128)S(1)} %get-tuple-element.60), channel_id=1, source_target_pairs={{1,2},{3,4},{5,6},{7,0},{2,1},{4,3},{6,5},{0,7},{9,10},{11,12},{13... | collective-permute-start | bytes 245768 | tf_op jit(solution)/shard_map/ppermute | solution.py:449
  52.3 8.5 %collective-permute-start.20 = (f32[640,128]{1,0:T(8,128)S(1)}, f32[640,128]{1,0:T(8,128)S(1)}, u32[]{:S(2)}, u32[]{:S(2)}) collective-permute-start(f32[640,128]{1,0:T(8,128)S(1)} %shard_map.95.done.refs_0_.refs_1_.refs_9_), channel_id=1, source_target_pairs={{8,16},{9,17},{10,18},{11,19},{12,20},{13,21},{14,22},{15,23},{24,... | collective-permute-start | bytes 983048 | tf_op jit(solution)/shard_map/ppermute | solution.py:446
  53.5 8.7 %collective-permute-start.23 = (f32[640,128]{1,0:T(8,128)S(1)}, f32[640,128]{1,0:T(8,128)S(1)}, u32[]{:S(2)}, u32[]{:S(2)}) collective-permute-start(f32[640,128]{1,0:T(8,128)S(1)} %get-tuple-element.61.refs_1_.refs_0_.refs_9_), channel_id=1, source_target_pairs={{0,8},{8,0},{16,24},{24,16},{32,40},{40,32},{48,56},{56,48},{64,72... | collective-permute-start | bytes 983048 | tf_op jit(solution)/shard_map/ppermute | solution.py:447
  55.6 5.2 %collective-permute-start.22 = (f32[160,128]{1,0:T(8,128)S(1)}, f32[160,128]{1,0:T(8,128)S(1)}, u32[]{:S(2)}, u32[]{:S(2)}) collective-permute-start(f32[160,128]{1,0:T(8,128)S(1)} %get-tuple-element.63), channel_id=1, source_target_pairs={{1,2},{3,4},{5,6},{7,0},{2,1},{4,3},{6,5},{0,7},{9,10},{11,12},{13... | collective-permute-start | bytes 245768 | tf_op jit(solution)/shard_map/ppermute | solution.py:449
  61.2 8.9 %collective-permute-start.24 = (f32[640,128]{1,0:T(8,128)S(1)}, f32[640,128]{1,0:T(8,128)S(1)}, u32[]{:S(2)}, u32[]{:S(2)}) collective-permute-start(f32[640,128]{1,0:T(8,128)S(1)} %shard_map.97.done.refs_0_.refs_1_.refs_10_), channel_id=1, source_target_pairs={{8,16},{9,17},{10,18},{11,19},{12,20},{13,21},{14,22},{15,23},{24,... | collective-permute-start | bytes 983048 | tf_op jit(solution)/shard_map/ppermute | solution.py:446
  62.7 8.0 %collective-permute-start.27 = (f32[640,128]{1,0:T(8,128)S(1)}, f32[640,128]{1,0:T(8,128)S(1)}, u32[]{:S(2)}, u32[]{:S(2)}) collective-permute-start(f32[640,128]{1,0:T(8,128)S(1)} %get-tuple-element.64.refs_1_.refs_0_.refs_10_), channel_id=1, source_target_pairs={{0,8},{8,0},{16,24},{24,16},{32,40},{40,32},{48,56},{56,48},{64,72... | collective-permute-start | bytes 983048 | tf_op jit(solution)/shard_map/ppermute | solution.py:447
  71.1 6.8 %collective-permute-start.31 = (f32[640,128]{1,0:T(8,128)S(1)}, f32[640,128]{1,0:T(8,128)S(1)}, u32[]{:S(2)}, u32[]{:S(2)}) collective-permute-start(f32[640,128]{1,0:T(8,128)S(1)} %get-tuple-element.67.refs_1_.refs_0_), channel_id=1, source_target_pairs={{0,8},{8,0},{16,24},{24,16},{32,40},{40,32},{48,56},{56,48},{64,72... | collective-permute-start | bytes 983048 | tf_op jit(solution)/shard_map/ppermute | solution.py:447
  72.5 6.8 %collective-permute-start.28 = (f32[640,128]{1,0:T(8,128)S(1)}, f32[640,128]{1,0:T(8,128)S(1)}, u32[]{:S(2)}, u32[]{:S(2)}) collective-permute-start(f32[640,128]{1,0:T(8,128)S(1)} %shard_map.99.done.refs_0_.refs_1_), channel_id=1, source_target_pairs={{8,16},{9,17},{10,18},{11,19},{12,20},{13,21},{14,22},{15,23},{24,... | collective-permute-start | bytes 983048 | tf_op jit(solution)/shard_map/ppermute | solution.py:446
  72.5 5.4 %collective-permute-start.30 = (f32[160,128]{1,0:T(8,128)S(1)}, f32[160,128]{1,0:T(8,128)S(1)}, u32[]{:S(2)}, u32[]{:S(2)}) collective-permute-start(f32[160,128]{1,0:T(8,128)S(1)} %get-tuple-element.69), channel_id=1, source_target_pairs={{1,2},{3,4},{5,6},{7,0},{2,1},{4,3},{6,5},{0,7},{9,10},{11,12},{13... | collective-permute-start | bytes 245768 | tf_op jit(solution)/shard_map/ppermute | solution.py:449
  (9 other events, 103.1 us)

commit v3 on v2

--- a/solution.py
+++ b/solution.py
@@ -19,7 +19,7 @@
 VMEM = pl.BlockSpec(memory_space=pltpu.VMEM)
 HBM = pl.BlockSpec(memory_space=pltpu.MemorySpace.HBM)
 LIMIT = 48 << 20
-UNROLL = 4
+UNROLL = 8
 
 
 def frequencies():
@@ -235,31 +235,41 @@
         parts[pl.ds(place * 32 + n * 16, 16), lanes] = split[(0, 1, 2, 0, 1, 0)[place]]
 
 
-def gram_body(first_out, first_in, last_out, last_in, middle, final, packed, parts, sem):
+def early_body(outer, inner, state, parts, sem):
     odd_x, _ = parities()
-    cube = lambda ref: ref.reshape(NFORCE, NVAR, 8, 128)
-    copies = [
-        pltpu.make_async_copy(cube(ref), to.at[:, :, at], sem.at[i])
-        for i, (ref, to, at) in enumerate(
-            (
-                (first_out, middle, odd_x),
-                (first_in, middle, 1 - odd_x),
-                (last_out, final, odd_x),
-                (last_in, final, 1 - odd_x),
-            )
-        )
-    ]
+    copies = run_copies([(b, a) for a, b in halves(state, odd_x, outer, inner, 1)], sem)
+    for v in range(NVAR):
+        for half, ref in enumerate((outer, inner)):
+            for t in range(8):
+                lanes = pl.ds(half * 1024 + t * 128, 128)
+                split_rows(ref, v * 8 + t, 40, parts.at[v], 0, lanes, (0, 1, 2))
     for copy in copies:
-        copy.start()
-    layers = ((first_out, last_out), (first_in, last_in))
+        copy.wait()
+
+
+def early(outer, inner):
+    return call(
+        early_body,
+        [((NFORCE, NVAR, 2, 8, 128), F32), ((NVAR, 96, 2048), BF16)],
+        1 << 20,
+        in_specs=[VMEM] * 2,
+        out_specs=[HBM, VMEM],
+        scratch_shapes=[pltpu.SemaphoreType.DMA((2,))],
+    )(outer, inner)
+
+
+def gram_body(outer, inner, before, final, packed, parts, sem):
+    odd_x, _ = parities()
+    copies = run_copies([(b, a) for a, b in halves(final, odd_x, outer, inner, 1)], sem)
     total = jnp.zeros((96, 96), F32)
     for v in range(NVAR):
-        for half, pair in enumerate(layers):
+        for half, ref in enumerate((outer, inner)):
             for t in range(8):
                 lanes = pl.ds(half * 1024 + t * 128, 128)
-                for n, ref in enumerate(pair):
-                    split_rows(ref, v * 8 + t, 40, parts.at[v], n, lanes, (0, 1, 2))
-        block = parts[v]
+                split_rows(ref, v * 8 + t, 40, parts, 1, lanes, (0, 1, 2))
+        for place in range(3):
+            parts[pl.ds(place * 32, 16), :] = before[v, pl.ds(place * 32, 16), :]
+        block = parts[...]
         total = total + lax.dot_general(
             block, block, (((1,), (1,)), ((), ())), preferred_element_type=F32
         )
@@ -272,16 +282,15 @@
         copy.wait()
 
 
-def gram_parts(first_out, first_in, last_out, last_in):
-    state = ((NFORCE, NVAR, 2, 8, 128), F32)
+def gram_parts(outer, inner, before):
     return call(
         gram_body,
-        [state, state, ((32, 8, 128), F32)],
+        [((NFORCE, NVAR, 2, 8, 128), F32), ((32, 8, 128), F32)],
         1 << 22,
-        in_specs=[VMEM] * 4,
-        out_specs=[HBM] * 2 + [VMEM],
-        scratch_shapes=[pltpu.VMEM((NVAR, 96, 2048), BF16), pltpu.SemaphoreType.DMA((4,))],
-    )(first_out, first_in, last_out, last_in)
+        in_specs=[VMEM] * 3,
+        out_specs=[HBM, VMEM],
+        scratch_shapes=[pltpu.VMEM((96, 2048), BF16), pltpu.SemaphoreType.DMA((2,))],
+    )(outer, inner, before)
 
 
 def lane_tables():
@@ -344,7 +353,7 @@
     upper[...] = work[pl.ds(0, 128, stride=2), :][:, 64:80].reshape(NFREQ, NFORCE, NFORCE)
 
 
-def basis_body(gathered, table, middle, final, basis, upper, states, weights, work, parts, blocks, sem_in, sem_out):
+def basis_body(gathered, table, middle, final, basis, upper, triangle, states, weights, work, parts, blocks, sem_in, sem_out):
     arriving = [
         [
             pltpu.make_async_copy(ref.at[:, v], states.at[n, v], sem_in.at[n, v])
@@ -355,8 +364,10 @@
     for pair in arriving:
         for copy in pair:
             copy.start()
-    factor(gathered, table, weights, upper, work)
-    leaving = []
+    factor(gathered, table, weights, triangle, work)
+    copy = pltpu.make_async_copy(triangle, upper, sem_out.at[NVAR, 0])
+    copy.start()
+    leaving = [copy]
     for v in range(NVAR):
         for n, copy in enumerate(arriving[v]):
             copy.wait()
@@ -372,10 +383,8 @@
                 block = jnp.dot(weights[...], parts[:, lanes], preferred_element_type=F32)
                 for u in range(2):
                     flat[pl.ds(x * 8 + t + u, 256, stride=24), :] = block[:, u * 128 : u * 128 + 128]
-        for part in range(2):
-            k = pl.ds(part * 4, 4)
             copy = pltpu.make_async_copy(
-                blocks.at[v, k, :, :, pl.ds(0, 2)], basis.at[k, :, :, v], sem_out.at[v, part]
+                blocks.at[v, :, :, :, x], basis.at[:, :, :, v, x], sem_out.at[v, x]
             )
             copy.start()
             leaving.append(copy)
@@ -392,15 +401,16 @@
         ],
         1 << 24,
         in_specs=[VMEM, VMEM, HBM, HBM],
-        out_specs=[HBM, VMEM],
+        out_specs=[HBM, HBM],
         scratch_shapes=[
+            pltpu.VMEM((NFREQ, NFORCE, NFORCE), F32),
             pltpu.VMEM((2, NVAR, NFORCE, 2, 8, 128), F32),
             pltpu.VMEM((256, 192), BF16),
             pltpu.VMEM((256, 128), F32),
             pltpu.VMEM((192, 2048), BF16),
             pltpu.VMEM((NVAR, NFREQ, NFORCE, 2, 3, 8, 128), F32),
             pltpu.SemaphoreType.DMA((2, NVAR)),
-            pltpu.SemaphoreType.DMA((NVAR, 2)),
+            pltpu.SemaphoreType.DMA((NVAR + 1, 2)),
         ],
     )(gathered, jnp.asarray(lane_tables()), *in_hbm(middle, final))
 
@@ -462,7 +472,8 @@
             outer, inner = new_outer, new_inner
             history.append((outer, inner))
         kept.append((outer, inner))
-    middle, final, packed = gram_parts(*kept[0], *kept[1])
+    middle, before = early(*kept[0])
+    final, packed = gram_parts(*kept[1], before)
     gathered = lax.all_to_all(packed, "ax", 0, 0, tiled=True)
     partial = jnp.broadcast_to(jnp.sum(gathered, axis=0)[None], (8, 8, 128))
     gathered = lax.all_to_all(partial, "az", 0, 0, tiled=True)

time: 116 us -> 114 us (0.983)
  transfers between devices with their start and end apart: 32 -> 32, of which waited for: 13 -> 10; matrix products, arithmetic and copies ran while one was open for 0% -> 0% of each run, Pallas kernels for 7% -> 8%
where the time goes in v3:
time: 114 us
  starting transfers between devices  50.6 us (44%)
  blocking collectives  27.4 us (24%)
  Pallas kernels  17.9 us (16%)
  waiting for transfers between devices  17.2 us (15%)
    ppermute x8, starting transfers between devices, on_device(): r2 = lax.ppermute(second, 'az', z2)  26.7 us
    ppermute x8, waiting for transfers between devices, on_device(): r2 = lax.ppermute(second, 'az', z2)  15.9 us
    all_to_all x1, blocking collectives, on_device(): gathered = lax.all_to_all(packed, 'ax', 0, 0, tiled=True)  15.4 us
    all_to_all x1, blocking collectives, on_device(): gathered = lax.all_to_all(partial, 'az', 0, 0, tiled=True)  12.1 us
    ppermute x8, starting transfers between devices, on_device(): r1 = lax.ppermute(first, 'az', z1)  10.8 us
    ppermute x8, starting transfers between devices, on_device(): from_chip = lax.ppermute(outer, ('ax', 'az'), chip)  8.62 us
    pallas_call x1, Pallas kernels, basis_of(): call(basis_body, [((NFREQ, NFORCE, 2, NVAR, 2, 8, 128), F32), ((NFREQ, NF...  5.99 us
    ppermute x8, starting transfers between devices, on_device(): from_core = lax.ppermute(inner, 'ax', core)  4.49 us
  transfers between devices with their start and end apart: 32, of which 10 were waited for; matrix products, arithmetic and copies ran while one was open for 0% of the time, Pallas kernels for 8%

profile of v3, /device:TPU:1, one launch (start us, length us, event | category | flops | bytes accessed | tf_op | source)
XLA Modules:
  0.0 114.2 jit_solution(5899930071997746965)
XLA Ops:
  1.9 2.8 %collective-permute-start = (f32[640,128]{1,0:T(8,128)S(1)}, f32[640,128]{1,0:T(8,128)S(1)}, u32[]{:S(2)}, u32[]{:S(2)}) collective-permute-start(f32[640,128]{1,0:T(8,128)S(1)} %get-tuple-element.40.refs_0_.refs_1_.refs_8_), channel_id=1, source_target_pairs={{8,16},{9,17},{10,18},{11,19},{12,20},{13,21},{14,22},{15,23},{24,... | collective-permute-start | bytes 983048 | tf_op jit(solution)/shard_map/ppermute | solution.py:456
  7.0 4.0 %collective-permute-start.2 = (f32[160,128]{1,0:T(8,128)S(1)}, f32[160,128]{1,0:T(8,128)S(1)}, u32[]{:S(2)}, u32[]{:S(2)}) collective-permute-start(f32[160,128]{1,0:T(8,128)S(1)} %get-tuple-element.43), channel_id=1, source_target_pairs={{1,2},{3,4},{5,6},{7,0},{2,1},{4,3},{6,5},{0,7},{9,10},{11,12},{13... | collective-permute-start | bytes 245768 | tf_op jit(solution)/shard_map/ppermute | solution.py:459
  13.2 2.9 %collective-permute-start.4 = (f32[640,128]{1,0:T(8,128)S(1)}, f32[640,128]{1,0:T(8,128)S(1)}, u32[]{:S(2)}, u32[]{:S(2)}) collective-permute-start(f32[640,128]{1,0:T(8,128)S(1)} %shard_map.87.done.refs_0_.refs_1_.refs_9_), channel_id=1, source_target_pairs={{8,16},{9,17},{10,18},{11,19},{12,20},{13,21},{14,22},{15,23},{24,... | collective-permute-start | bytes 983048 | tf_op jit(solution)/shard_map/ppermute | solution.py:456
  17.3 3.4 %collective-permute-start.6 = (f32[160,128]{1,0:T(8,128)S(1)}, f32[160,128]{1,0:T(8,128)S(1)}, u32[]{:S(2)}, u32[]{:S(2)}) collective-permute-start(f32[160,128]{1,0:T(8,128)S(1)} %get-tuple-element.52), channel_id=1, source_target_pairs={{1,2},{3,4},{5,6},{7,0},{2,1},{4,3},{6,5},{0,7},{9,10},{11,12},{13... | collective-permute-start | bytes 245768 | tf_op jit(solution)/shard_map/ppermute | solution.py:459
  21.3 1.9 %collective-permute-done.6.refs_4_ = f32[160,128]{1,0:T(8,128)S(1)} collective-permute-done((f32[160,128]{1,0:T(8,128)S(1)}, f32[160,128]{1,0:T(8,128)S(1)}, u32[]{:S(2)}, u32[]{:S(2)}) %collective-permute-start.6) | collective-permute-done | bytes 81952 | tf_op jit(solution)/shard_map/ppermute | solution.py:459
  25.2 1.7 %collective-permute-start.9 = (f32[160,128]{1,0:T(8,128)S(1)}, f32[160,128]{1,0:T(8,128)S(1)}, u32[]{:S(2)}, u32[]{:S(2)}) collective-permute-start(f32[160,128]{1,0:T(8,128)S(1)} %get-tuple-element.54), channel_id=1, source_target_pairs={{0,1},{1,0},{2,3},{3,2},{4,5},{5,4},{6,7},{7,6},{8,9},{9,8},{10,11... | collective-permute-start | bytes 245768 | tf_op jit(solution)/shard_map/ppermute | solution.py:458
  27.0 3.1 %collective-permute-start.10 = (f32[160,128]{1,0:T(8,128)S(1)}, f32[160,128]{1,0:T(8,128)S(1)}, u32[]{:S(2)}, u32[]{:S(2)}) collective-permute-start(f32[160,128]{1,0:T(8,128)S(1)} %get-tuple-element.55), channel_id=1, source_target_pairs={{1,2},{3,4},{5,6},{7,0},{2,1},{4,3},{6,5},{0,7},{9,10},{11,12},{13... | collective-permute-start | bytes 245768 | tf_op jit(solution)/shard_map/ppermute | solution.py:459
  30.1 2.5 %collective-permute-done.10.refs_4_ = f32[160,128]{1,0:T(8,128)S(1)} collective-permute-done((f32[160,128]{1,0:T(8,128)S(1)}, f32[160,128]{1,0:T(8,128)S(1)}, u32[]{:S(2)}, u32[]{:S(2)}) %collective-permute-start.10) | collective-permute-done | bytes 81952 | tf_op jit(solution)/shard_map/ppermute | solution.py:459
  34.6 1.7 %collective-permute-start.13 = (f32[160,128]{1,0:T(8,128)S(1)}, f32[160,128]{1,0:T(8,128)S(1)}, u32[]{:S(2)}, u32[]{:S(2)}) collective-permute-start(f32[160,128]{1,0:T(8,128)S(1)} %get-tuple-element.57), channel_id=1, source_target_pairs={{0,1},{1,0},{2,3},{3,2},{4,5},{5,4},{6,7},{7,6},{8,9},{9,8},{10,11... | collective-permute-start | bytes 245768 | tf_op jit(solution)/shard_map/ppermute | solution.py:458
  36.3 3.1 %collective-permute-start.14 = (f32[160,128]{1,0:T(8,128)S(1)}, f32[160,128]{1,0:T(8,128)S(1)}, u32[]{:S(2)}, u32[]{:S(2)}) collective-permute-start(f32[160,128]{1,0:T(8,128)S(1)} %get-tuple-element.58), channel_id=1, source_target_pairs={{1,2},{3,4},{5,6},{7,0},{2,1},{4,3},{6,5},{0,7},{9,10},{11,12},{13... | collective-permute-start | bytes 245768 | tf_op jit(solution)/shard_map/ppermute | solution.py:459
  39.4 2.5 %collective-permute-done.14.refs_4_ = f32[160,128]{1,0:T(8,128)S(1)} collective-permute-done((f32[160,128]{1,0:T(8,128)S(1)}, f32[160,128]{1,0:T(8,128)S(1)}, u32[]{:S(2)}, u32[]{:S(2)}) %collective-permute-start.14) | collective-permute-done | bytes 81952 | tf_op jit(solution)/shard_map/ppermute | solution.py:459
  44.2 1.7 %collective-permute-start.17 = (f32[160,128]{1,0:T(8,128)S(1)}, f32[160,128]{1,0:T(8,128)S(1)}, u32[]{:S(2)}, u32[]{:S(2)}) collective-permute-start(f32[160,128]{1,0:T(8,128)S(1)} %get-tuple-element.60), channel_id=1, source_target_pairs={{0,1},{1,0},{2,3},{3,2},{4,5},{5,4},{6,7},{7,6},{8,9},{9,8},{10,11... | collective-permute-start | bytes 245768 | tf_op jit(solution)/shard_map/ppermute | solution.py:458
  46.0 3.1 %collective-permute-start.18 = (f32[160,128]{1,0:T(8,128)S(1)}, f32[160,128]{1,0:T(8,128)S(1)}, u32[]{:S(2)}, u32[]{:S(2)}) collective-permute-start(f32[160,128]{1,0:T(8,128)S(1)} %get-tuple-element.61), channel_id=1, source_target_pairs={{1,2},{3,4},{5,6},{7,0},{2,1},{4,3},{6,5},{0,7},{9,10},{11,12},{13... | collective-permute-start | bytes 245768 | tf_op jit(solution)/shard_map/ppermute | solution.py:459
  49.1 2.5 %collective-permute-done.18.refs_4_ = f32[160,128]{1,0:T(8,128)S(1)} collective-permute-done((f32[160,128]{1,0:T(8,128)S(1)}, f32[160,128]{1,0:T(8,128)S(1)}, u32[]{:S(2)}, u32[]{:S(2)}) %collective-permute-start.18) | collective-permute-done | bytes 81952 | tf_op jit(solution)/shard_map/ppermute | solution.py:459
  53.6 1.7 %collective-permute-start.21 = (f32[160,128]{1,0:T(8,128)S(1)}, f32[160,128]{1,0:T(8,128)S(1)}, u32[]{:S(2)}, u32[]{:S(2)}) collective-permute-start(f32[160,128]{1,0:T(8,128)S(1)} %get-tuple-element.63), channel_id=1, source_target_pairs={{0,1},{1,0},{2,3},{3,2},{4,5},{5,4},{6,7},{7,6},{8,9},{9,8},{10,11... | collective-permute-start | bytes 245768 | tf_op jit(solution)/shard_map/ppermute | solution.py:458
  55.3 3.1 %collective-permute-start.22 = (f32[160,128]{1,0:T(8,128)S(1)}, f32[160,128]{1,0:T(8,128)S(1)}, u32[]{:S(2)}, u32[]{:S(2)}) collective-permute-start(f32[160,128]{1,0:T(8,128)S(1)} %get-tuple-element.64), channel_id=1, source_target_pairs={{1,2},{3,4},{5,6},{7,0},{2,1},{4,3},{6,5},{0,7},{9,10},{11,12},{13... | collective-permute-start | bytes 245768 | tf_op jit(solution)/shard_map/ppermute | solution.py:459
  58.4 2.5 %collective-permute-done.22.refs_4_ = f32[160,128]{1,0:T(8,128)S(1)} collective-permute-done((f32[160,128]{1,0:T(8,128)S(1)}, f32[160,128]{1,0:T(8,128)S(1)}, u32[]{:S(2)}, u32[]{:S(2)}) %collective-permute-start.22) | collective-permute-done | bytes 81952 | tf_op jit(solution)/shard_map/ppermute | solution.py:459
  63.0 1.7 %collective-permute-start.25 = (f32[160,128]{1,0:T(8,128)S(1)}, f32[160,128]{1,0:T(8,128)S(1)}, u32[]{:S(2)}, u32[]{:S(2)}) collective-permute-start(f32[160,128]{1,0:T(8,128)S(1)} %get-tuple-element.66), channel_id=1, source_target_pairs={{0,1},{1,0},{2,3},{3,2},{4,5},{5,4},{6,7},{7,6},{8,9},{9,8},{10,11... | collective-permute-start | bytes 245768 | tf_op jit(solution)/shard_map/ppermute | solution.py:458
  64.7 3.1 %collective-permute-start.26 = (f32[160,128]{1,0:T(8,128)S(1)}, f32[160,128]{1,0:T(8,128)S(1)}, u32[]{:S(2)}, u32[]{:S(2)}) collective-permute-start(f32[160,128]{1,0:T(8,128)S(1)} %get-tuple-element.67), channel_id=1, source_target_pairs={{1,2},{3,4},{5,6},{7,0},{2,1},{4,3},{6,5},{0,7},{9,10},{11,12},{13... | collective-permute-start | bytes 245768 | tf_op jit(solution)/shard_map/ppermute | solution.py:459
  67.8 2.5 %collective-permute-done.26.refs_4_ = f32[160,128]{1,0:T(8,128)S(1)} collective-permute-done((f32[160,128]{1,0:T(8,128)S(1)}, f32[160,128]{1,0:T(8,128)S(1)}, u32[]{:S(2)}, u32[]{:S(2)}) %collective-permute-start.26) | collective-permute-done | bytes 81952 | tf_op jit(solution)/shard_map/ppermute | solution.py:459
  72.2 3.8 %collective-permute-start.30 = (f32[160,128]{1,0:T(8,128)S(1)}, f32[160,128]{1,0:T(8,128)S(1)}, u32[]{:S(2)}, u32[]{:S(2)}) collective-permute-start(f32[160,128]{1,0:T(8,128)S(1)} %get-tuple-element.70), channel_id=1, source_target_pairs={{1,2},{3,4},{5,6},{7,0},{2,1},{4,3},{6,5},{0,7},{9,10},{11,12},{13... | collective-permute-start | bytes 245768 | tf_op jit(solution)/shard_map/ppermute | solution.py:459
  80.5 15.4 %all_to_all.10 = f32[32,8,128]{2,1,0:T(8,128)S(1)} all-to-all(f32[32,8,128]{2,1,0:T(8,128)S(1)} %get-tuple-element.73), channel_id=1, replica_groups=mesh['ax'=32,'az'=8] {'ax'}, dimensions={0} | all-to-all | bytes 262144 | tf_op jit(solution)/shard_map/all_to_all | solution.py:477
  95.9 12.1 %all_to_all.11.gathered = f32[8,8,128]{2,1,0:T(8,128)S(1)} all-to-all(f32[8,8,128]{2,1,0:T(8,128)S(1)} %broadcast_in_dim.2), channel_id=1, replica_groups=mesh['ax'=32,'az'=8] {'az'}, dimensions={0} | all-to-all | bytes 65536 | tf_op jit(solution)/shard_map/all_to_all | solution.py:479
  108.0 6.0 %shard_map.105 = (f32[8,16,2,5,2,8,128]{6,5,4,3,2,1,0:T(8,128)}, f32[8,16,16]{2,1,0:T(8,128)}) custom-call(f32[8,8,128]{2,1,0:T(8,128)S(1)} %all_to_all.11.gathered, f32[8,256]{1,0:T(8,128)S(1)} %copy-done, f32[16,5,2,8,128]{4,3,2,1,0:T(8,128)} %get-tuple-element.74.middle, f32[16,5,2,8,128]{4,3,2,1,0:T(8,128)} %get-tuple-element.37.final), custom_call_target="tpu_custom_call" | custom-call | flops 16777216 | bytes 16777216 | tf_op jit(solution)/shard_map/pallas_call | solution.py:396
  (67 shorter events, 24.2 us)
Async XLA Ops:
  1.9 10.9 %collective-permute-start = (f32[640,128]{1,0:T(8,128)S(1)}, f32[640,128]{1,0:T(8,128)S(1)}, u32[]{:S(2)}, u32[]{:S(2)}) collective-permute-start(f32[640,128]{1,0:T(8,128)S(1)} %get-tuple-element.40.refs_0_.refs_1_.refs_8_), channel_id=1, source_target_pairs={{8,16},{9,17},{10,18},{11,19},{12,20},{13,21},{14,22},{15,23},{24,... | collective-permute-start | bytes 983048 | tf_op jit(solution)/shard_map/ppermute | solution.py:456
  4.7 11.5 %collective-permute-start.3 = (f32[640,128]{1,0:T(8,128)S(1)}, f32[640,128]{1,0:T(8,128)S(1)}, u32[]{:S(2)}, u32[]{:S(2)}) collective-permute-start(f32[640,128]{1,0:T(8,128)S(1)} %get-tuple-element.41.refs_1_.refs_0_.refs_8_), channel_id=1, source_target_pairs={{0,8},{8,0},{16,24},{24,16},{32,40},{40,32},{48,56},{56,48},{64,72... | collective-permute-start | bytes 983048 | tf_op jit(solution)/shard_map/ppermute | solution.py:457
  5.4 6.9 %collective-permute-start.1 = (f32[160,128]{1,0:T(8,128)S(1)}, f32[160,128]{1,0:T(8,128)S(1)}, u32[]{:S(2)}, u32[]{:S(2)}) collective-permute-start(f32[160,128]{1,0:T(8,128)S(1)} %get-tuple-element.42), channel_id=1, source_target_pairs={{0,1},{1,0},{2,3},{3,2},{4,5},{5,4},{6,7},{7,6},{8,9},{9,8},{10,11... | collective-permute-start | bytes 245768 | tf_op jit(solution)/shard_map/ppermute | solution.py:458
  7.0 5.8 %collective-permute-start.2 = (f32[160,128]{1,0:T(8,128)S(1)}, f32[160,128]{1,0:T(8,128)S(1)}, u32[]{:S(2)}, u32[]{:S(2)}) collective-permute-start(f32[160,128]{1,0:T(8,128)S(1)} %get-tuple-element.43), channel_id=1, source_target_pairs={{1,2},{3,4},{5,6},{7,0},{2,1},{4,3},{6,5},{0,7},{9,10},{11,12},{13... | collective-permute-start | bytes 245768 | tf_op jit(solution)/shard_map/ppermute | solution.py:459
  13.2 10.0 %collective-permute-start.4 = (f32[640,128]{1,0:T(8,128)S(1)}, f32[640,128]{1,0:T(8,128)S(1)}, u32[]{:S(2)}, u32[]{:S(2)}) collective-permute-start(f32[640,128]{1,0:T(8,128)S(1)} %shard_map.87.done.refs_0_.refs_1_.refs_9_), channel_id=1, source_target_pairs={{8,16},{9,17},{10,18},{11,19},{12,20},{13,21},{14,22},{15,23},{24,... | collective-permute-start | bytes 983048 | tf_op jit(solution)/shard_map/ppermute | solution.py:456
  16.6 8.0 %collective-permute-start.7 = (f32[640,128]{1,0:T(8,128)S(1)}, f32[640,128]{1,0:T(8,128)S(1)}, u32[]{:S(2)}, u32[]{:S(2)}) collective-permute-start(f32[640,128]{1,0:T(8,128)S(1)} %get-tuple-element.50.refs_1_.refs_0_.refs_9_), channel_id=1, source_target_pairs={{0,8},{8,0},{16,24},{24,16},{32,40},{40,32},{48,56},{56,48},{64,72... | collective-permute-start | bytes 983048 | tf_op jit(solution)/shard_map/ppermute | solution.py:457
  17.3 6.0 %collective-permute-start.6 = (f32[160,128]{1,0:T(8,128)S(1)}, f32[160,128]{1,0:T(8,128)S(1)}, u32[]{:S(2)}, u32[]{:S(2)}) collective-permute-start(f32[160,128]{1,0:T(8,128)S(1)} %get-tuple-element.52), channel_id=1, source_target_pairs={{1,2},{3,4},{5,6},{7,0},{2,1},{4,3},{6,5},{0,7},{9,10},{11,12},{13... | collective-permute-start | bytes 245768 | tf_op jit(solution)/shard_map/ppermute | solution.py:459
  23.7 8.9 %collective-permute-start.8 = (f32[640,128]{1,0:T(8,128)S(1)}, f32[640,128]{1,0:T(8,128)S(1)}, u32[]{:S(2)}, u32[]{:S(2)}) collective-permute-start(f32[640,128]{1,0:T(8,128)S(1)} %shard_map.89.done.refs_0_.refs_1_.refs_10_), channel_id=1, source_target_pairs={{8,16},{9,17},{10,18},{11,19},{12,20},{13,21},{14,22},{15,23},{24,... | collective-permute-start | bytes 983048 | tf_op jit(solution)/shard_map/ppermute | solution.py:456
  25.1 8.0 %collective-permute-start.11 = (f32[640,128]{1,0:T(8,128)S(1)}, f32[640,128]{1,0:T(8,128)S(1)}, u32[]{:S(2)}, u32[]{:S(2)}) collective-permute-start(f32[640,128]{1,0:T(8,128)S(1)} %get-tuple-element.53.refs_1_.refs_0_.refs_10_), channel_id=1, source_target_pairs={{0,8},{8,0},{16,24},{24,16},{32,40},{40,32},{48,56},{56,48},{64,72... | collective-permute-start | bytes 983048 | tf_op jit(solution)/shard_map/ppermute | solution.py:457
  27.0 5.7 %collective-permute-start.10 = (f32[160,128]{1,0:T(8,128)S(1)}, f32[160,128]{1,0:T(8,128)S(1)}, u32[]{:S(2)}, u32[]{:S(2)}) collective-permute-start(f32[160,128]{1,0:T(8,128)S(1)} %get-tuple-element.55), channel_id=1, source_target_pairs={{1,2},{3,4},{5,6},{7,0},{2,1},{4,3},{6,5},{0,7},{9,10},{11,12},{13... | collective-permute-start | bytes 245768 | tf_op jit(solution)/shard_map/ppermute | solution.py:459
  33.1 8.9 %collective-permute-start.12 = (f32[640,128]{1,0:T(8,128)S(1)}, f32[640,128]{1,0:T(8,128)S(1)}, u32[]{:S(2)}, u32[]{:S(2)}) collective-permute-start(f32[640,128]{1,0:T(8,128)S(1)} %shard_map.91.done.refs_0_.refs_1_), channel_id=1, source_target_pairs={{8,16},{9,17},{10,18},{11,19},{12,20},{13,21},{14,22},{15,23},{24,... | collective-permute-start | bytes 983048 | tf_op jit(solution)/shard_map/ppermute | solution.py:456
  33.6 9.4 %collective-permute-start.15 = (f32[640,128]{1,0:T(8,128)S(1)}, f32[640,128]{1,0:T(8,128)S(1)}, u32[]{:S(2)}, u32[]{:S(2)}) collective-permute-start(f32[640,128]{1,0:T(8,128)S(1)} %get-tuple-element.56.refs_1_.refs_0_), channel_id=1, source_target_pairs={{0,8},{8,0},{16,24},{24,16},{32,40},{40,32},{48,56},{56,48},{64,72... | collective-permute-start | bytes 983048 | tf_op jit(solution)/shard_map/ppermute | solution.py:457
  36.3 5.6 %collective-permute-start.14 = (f32[160,128]{1,0:T(8,128)S(1)}, f32[160,128]{1,0:T(8,128)S(1)}, u32[]{:S(2)}, u32[]{:S(2)}) collective-permute-start(f32[160,128]{1,0:T(8,128)S(1)} %get-tuple-element.58), channel_id=1, source_target_pairs={{1,2},{3,4},{5,6},{7,0},{2,1},{4,3},{6,5},{0,7},{9,10},{11,12},{13... | collective-permute-start | bytes 245768 | tf_op jit(solution)/shard_map/ppermute | solution.py:459
  42.5 9.2 %collective-permute-start.16 = (f32[640,128]{1,0:T(8,128)S(1)}, f32[640,128]{1,0:T(8,128)S(1)}, u32[]{:S(2)}, u32[]{:S(2)}) collective-permute-start(f32[640,128]{1,0:T(8,128)S(1)} %shard_map.93.done.refs_0_.refs_1_.refs_8_.outer), channel_id=1, source_target_pairs={{8,16},{9,17},{10,18},{11,19},{12,20},{13,21},{14,22},{15,23},{24,... | collective-permute-start | bytes 983048 | tf_op jit(solution)/shard_map/ppermute | solution.py:456
  43.6 9.2 %collective-permute-start.19 = (f32[640,128]{1,0:T(8,128)S(1)}, f32[640,128]{1,0:T(8,128)S(1)}, u32[]{:S(2)}, u32[]{:S(2)}) collective-permute-start(f32[640,128]{1,0:T(8,128)S(1)} %get-tuple-element.59.refs_1_.refs_0_.refs_8_.inner), channel_id=1, source_target_pairs={{0,8},{8,0},{16,24},{24,16},{32,40},{40,32},{48,56},{56,48},{64,72... | collective-permute-start | bytes 983048 | tf_op jit(solution)/shard_map/ppermute | solution.py:457
  46.0 5.6 %collective-permute-start.18 = (f32[160,128]{1,0:T(8,128)S(1)}, f32[160,128]{1,0:T(8,128)S(1)}, u32[]{:S(2)}, u32[]{:S(2)}) collective-permute-start(f32[160,128]{1,0:T(8,128)S(1)} %get-tuple-element.61), channel_id=1, source_target_pairs={{1,2},{3,4},{5,6},{7,0},{2,1},{4,3},{6,5},{0,7},{9,10},{11,12},{13... | collective-permute-start | bytes 245768 | tf_op jit(solution)/shard_map/ppermute | solution.py:459
  52.1 8.9 %collective-permute-start.20 = (f32[640,128]{1,0:T(8,128)S(1)}, f32[640,128]{1,0:T(8,128)S(1)}, u32[]{:S(2)}, u32[]{:S(2)}) collective-permute-start(f32[640,128]{1,0:T(8,128)S(1)} %shard_map.95.done.refs_0_.refs_1_.refs_9_), channel_id=1, source_target_pairs={{8,16},{9,17},{10,18},{11,19},{12,20},{13,21},{14,22},{15,23},{24,... | collective-permute-start | bytes 983048 | tf_op jit(solution)/shard_map/ppermute | solution.py:456
  53.2 8.7 %collective-permute-start.23 = (f32[640,128]{1,0:T(8,128)S(1)}, f32[640,128]{1,0:T(8,128)S(1)}, u32[]{:S(2)}, u32[]{:S(2)}) collective-permute-start(f32[640,128]{1,0:T(8,128)S(1)} %get-tuple-element.62.refs_1_.refs_0_.refs_9_), channel_id=1, source_target_pairs={{0,8},{8,0},{16,24},{24,16},{32,40},{40,32},{48,56},{56,48},{64,72... | collective-permute-start | bytes 983048 | tf_op jit(solution)/shard_map/ppermute | solution.py:457
  55.3 5.6 %collective-permute-start.22 = (f32[160,128]{1,0:T(8,128)S(1)}, f32[160,128]{1,0:T(8,128)S(1)}, u32[]{:S(2)}, u32[]{:S(2)}) collective-permute-start(f32[160,128]{1,0:T(8,128)S(1)} %get-tuple-element.64), channel_id=1, source_target_pairs={{1,2},{3,4},{5,6},{7,0},{2,1},{4,3},{6,5},{0,7},{9,10},{11,12},{13... | collective-permute-start | bytes 245768 | tf_op jit(solution)/shard_map/ppermute | solution.py:459
  61.3 8.9 %collective-permute-start.24 = (f32[640,128]{1,0:T(8,128)S(1)}, f32[640,128]{1,0:T(8,128)S(1)}, u32[]{:S(2)}, u32[]{:S(2)}) collective-permute-start(f32[640,128]{1,0:T(8,128)S(1)} %shard_map.97.done.refs_0_.refs_1_.refs_10_), channel_id=1, source_target_pairs={{8,16},{9,17},{10,18},{11,19},{12,20},{13,21},{14,22},{15,23},{24,... | collective-permute-start | bytes 983048 | tf_op jit(solution)/shard_map/ppermute | solution.py:456
  62.4 8.3 %collective-permute-start.27 = (f32[640,128]{1,0:T(8,128)S(1)}, f32[640,128]{1,0:T(8,128)S(1)}, u32[]{:S(2)}, u32[]{:S(2)}) collective-permute-start(f32[640,128]{1,0:T(8,128)S(1)} %get-tuple-element.65.refs_1_.refs_0_.refs_10_), channel_id=1, source_target_pairs={{0,8},{8,0},{16,24},{24,16},{32,40},{40,32},{48,56},{56,48},{64,72... | collective-permute-start | bytes 983048 | tf_op jit(solution)/shard_map/ppermute | solution.py:457
  71.2 6.7 %collective-permute-start.31 = (f32[640,128]{1,0:T(8,128)S(1)}, f32[640,128]{1,0:T(8,128)S(1)}, u32[]{:S(2)}, u32[]{:S(2)}) collective-permute-start(f32[640,128]{1,0:T(8,128)S(1)} %get-tuple-element.68.refs_1_.refs_0_), channel_id=1, source_target_pairs={{0,8},{8,0},{16,24},{24,16},{32,40},{40,32},{48,56},{56,48},{64,72... | collective-permute-start | bytes 983048 | tf_op jit(solution)/shard_map/ppermute | solution.py:457
  72.2 6.8 %collective-permute-start.28 = (f32[640,128]{1,0:T(8,128)S(1)}, f32[640,128]{1,0:T(8,128)S(1)}, u32[]{:S(2)}, u32[]{:S(2)}) collective-permute-start(f32[640,128]{1,0:T(8,128)S(1)} %shard_map.99.done.refs_0_.refs_1_), channel_id=1, source_target_pairs={{8,16},{9,17},{10,18},{11,19},{12,20},{13,21},{14,22},{15,23},{24,... | collective-permute-start | bytes 983048 | tf_op jit(solution)/shard_map/ppermute | solution.py:456
  72.2 5.6 %collective-permute-start.30 = (f32[160,128]{1,0:T(8,128)S(1)}, f32[160,128]{1,0:T(8,128)S(1)}, u32[]{:S(2)}, u32[]{:S(2)}) collective-permute-start(f32[160,128]{1,0:T(8,128)S(1)} %get-tuple-element.70), channel_id=1, source_target_pairs={{1,2},{3,4},{5,6},{7,0},{2,1},{4,3},{6,5},{0,7},{9,10},{11,12},{13... | collective-permute-start | bytes 245768 | tf_op jit(solution)/shard_map/ppermute | solution.py:459
  (9 other events, 95.0 us)

commit v4 on v3

--- a/solution.py
+++ b/solution.py
@@ -377,17 +377,23 @@
                     lanes = pl.ds(x * 1024 + t * 128, 128)
                     split_rows(rows, x * 8 + t, 16, parts, n, lanes, range(6))
         flat = blocks.at[v].reshape(256 * 24, 128)
+        cuts = 2 if v == 0 else 1
+        size = 256 // cuts
         for x in range(2):
-            for t in range(0, 8, 2):
-                lanes = pl.ds(x * 1024 + t * 128, 256)
-                block = jnp.dot(weights[...], parts[:, lanes], preferred_element_type=F32)
-                for u in range(2):
-                    flat[pl.ds(x * 8 + t + u, 256, stride=24), :] = block[:, u * 128 : u * 128 + 128]
-            copy = pltpu.make_async_copy(
-                blocks.at[v, :, :, :, x], basis.at[:, :, :, v, x], sem_out.at[v, x]
-            )
-            copy.start()
-            leaving.append(copy)
+            for cut in range(cuts):
+                for t in range(0, 8, 2):
+                    lanes = pl.ds(x * 1024 + t * 128, 256)
+                    rows = weights[cut * size : cut * size + size, :]
+                    block = jnp.dot(rows, parts[:, lanes], preferred_element_type=F32)
+                    for u in range(2):
+                        to = pl.ds(cut * size * 24 + x * 8 + t + u, size, stride=24)
+                        flat[to, :] = block[:, u * 128 : u * 128 + 128]
+                k = pl.ds(cut * (NFREQ // cuts), NFREQ // cuts)
+                copy = pltpu.make_async_copy(
+                    blocks.at[v, k, :, :, x], basis.at[k, :, :, v, x], sem_out.at[v, x * 2 + cut]
+                )
+                copy.start()
+                leaving.append(copy)
     for copy in leaving:
         copy.wait()
 
@@ -410,7 +416,7 @@
             pltpu.VMEM((192, 2048), BF16),
             pltpu.VMEM((NVAR, NFREQ, NFORCE, 2, 3, 8, 128), F32),
             pltpu.SemaphoreType.DMA((2, NVAR)),
-            pltpu.SemaphoreType.DMA((NVAR + 1, 2)),
+            pltpu.SemaphoreType.DMA((NVAR + 1, 4)),
         ],
     )(gathered, jnp.asarray(lane_tables()), *in_hbm(middle, final))
 

time: 114 us -> 114 us (level)
  no operation moved by 1% of the time
where the time goes in v4:
time: 114 us
  starting transfers between devices  50.6 us (44%)
  blocking collectives  27.4 us (24%)
  Pallas kernels  18 us (16%)
  waiting for transfers between devices  17.2 us (15%)
    ppermute x8, starting transfers between devices, on_device(): r2 = lax.ppermute(second, 'az', z2)  26.7 us
    ppermute x8, waiting for transfers between devices, on_device(): r2 = lax.ppermute(second, 'az', z2)  15.9 us
    all_to_all x1, blocking collectives, on_device(): gathered = lax.all_to_all(packed, 'ax', 0, 0, tiled=True)  15.4 us
    all_to_all x1, blocking collectives, on_device(): gathered = lax.all_to_all(partial, 'az', 0, 0, tiled=True)  12.1 us
    ppermute x8, starting transfers between devices, on_device(): r1 = lax.ppermute(first, 'az', z1)  10.8 us
    ppermute x8, starting transfers between devices, on_device(): from_chip = lax.ppermute(outer, ('ax', 'az'), chip)  8.62 us
    pallas_call x1, Pallas kernels, basis_of(): call(basis_body, [((NFREQ, NFORCE, 2, NVAR, 2, 8, 128), F32), ((NFREQ, NF...  6.06 us
    ppermute x8, starting transfers between devices, on_device(): from_core = lax.ppermute(inner, 'ax', core)  4.49 us
  transfers between devices with their start and end apart: 32, of which 10 were waited for; matrix products, arithmetic and copies ran while one was open for 0% of the time, Pallas kernels for 8%

profile of v4, /device:TPU:1, one launch (start us, length us, event | category | flops | bytes accessed | tf_op | source)
XLA Modules:
  0.0 114.2 jit_solution(975003631491245915)
XLA Ops:
  1.9 2.8 %collective-permute-start = (f32[640,128]{1,0:T(8,128)S(1)}, f32[640,128]{1,0:T(8,128)S(1)}, u32[]{:S(2)}, u32[]{:S(2)}) collective-permute-start(f32[640,128]{1,0:T(8,128)S(1)} %get-tuple-element.40.refs_0_.refs_1_.refs_8_), channel_id=1, source_target_pairs={{8,16},{9,17},{10,18},{11,19},{12,20},{13,21},{14,22},{15,23},{24,... | collective-permute-start | bytes 983048 | tf_op jit(solution)/shard_map/ppermute | solution.py:462
  7.0 4.0 %collective-permute-start.2 = (f32[160,128]{1,0:T(8,128)S(1)}, f32[160,128]{1,0:T(8,128)S(1)}, u32[]{:S(2)}, u32[]{:S(2)}) collective-permute-start(f32[160,128]{1,0:T(8,128)S(1)} %get-tuple-element.43), channel_id=1, source_target_pairs={{1,2},{3,4},{5,6},{7,0},{2,1},{4,3},{6,5},{0,7},{9,10},{11,12},{13... | collective-permute-start | bytes 245768 | tf_op jit(solution)/shard_map/ppermute | solution.py:465
  13.2 2.9 %collective-permute-start.4 = (f32[640,128]{1,0:T(8,128)S(1)}, f32[640,128]{1,0:T(8,128)S(1)}, u32[]{:S(2)}, u32[]{:S(2)}) collective-permute-start(f32[640,128]{1,0:T(8,128)S(1)} %shard_map.87.done.refs_0_.refs_1_.refs_9_), channel_id=1, source_target_pairs={{8,16},{9,17},{10,18},{11,19},{12,20},{13,21},{14,22},{15,23},{24,... | collective-permute-start | bytes 983048 | tf_op jit(solution)/shard_map/ppermute | solution.py:462
  17.3 3.4 %collective-permute-start.6 = (f32[160,128]{1,0:T(8,128)S(1)}, f32[160,128]{1,0:T(8,128)S(1)}, u32[]{:S(2)}, u32[]{:S(2)}) collective-permute-start(f32[160,128]{1,0:T(8,128)S(1)} %get-tuple-element.52), channel_id=1, source_target_pairs={{1,2},{3,4},{5,6},{7,0},{2,1},{4,3},{6,5},{0,7},{9,10},{11,12},{13... | collective-permute-start | bytes 245768 | tf_op jit(solution)/shard_map/ppermute | solution.py:465
  21.3 1.9 %collective-permute-done.6.refs_4_ = f32[160,128]{1,0:T(8,128)S(1)} collective-permute-done((f32[160,128]{1,0:T(8,128)S(1)}, f32[160,128]{1,0:T(8,128)S(1)}, u32[]{:S(2)}, u32[]{:S(2)}) %collective-permute-start.6) | collective-permute-done | bytes 81952 | tf_op jit(solution)/shard_map/ppermute | solution.py:465
  25.2 1.7 %collective-permute-start.9 = (f32[160,128]{1,0:T(8,128)S(1)}, f32[160,128]{1,0:T(8,128)S(1)}, u32[]{:S(2)}, u32[]{:S(2)}) collective-permute-start(f32[160,128]{1,0:T(8,128)S(1)} %get-tuple-element.54), channel_id=1, source_target_pairs={{0,1},{1,0},{2,3},{3,2},{4,5},{5,4},{6,7},{7,6},{8,9},{9,8},{10,11... | collective-permute-start | bytes 245768 | tf_op jit(solution)/shard_map/ppermute | solution.py:464
  27.0 3.1 %collective-permute-start.10 = (f32[160,128]{1,0:T(8,128)S(1)}, f32[160,128]{1,0:T(8,128)S(1)}, u32[]{:S(2)}, u32[]{:S(2)}) collective-permute-start(f32[160,128]{1,0:T(8,128)S(1)} %get-tuple-element.55), channel_id=1, source_target_pairs={{1,2},{3,4},{5,6},{7,0},{2,1},{4,3},{6,5},{0,7},{9,10},{11,12},{13... | collective-permute-start | bytes 245768 | tf_op jit(solution)/shard_map/ppermute | solution.py:465
  30.1 2.5 %collective-permute-done.10.refs_4_ = f32[160,128]{1,0:T(8,128)S(1)} collective-permute-done((f32[160,128]{1,0:T(8,128)S(1)}, f32[160,128]{1,0:T(8,128)S(1)}, u32[]{:S(2)}, u32[]{:S(2)}) %collective-permute-start.10) | collective-permute-done | bytes 81952 | tf_op jit(solution)/shard_map/ppermute | solution.py:465
  34.6 1.7 %collective-permute-start.13 = (f32[160,128]{1,0:T(8,128)S(1)}, f32[160,128]{1,0:T(8,128)S(1)}, u32[]{:S(2)}, u32[]{:S(2)}) collective-permute-start(f32[160,128]{1,0:T(8,128)S(1)} %get-tuple-element.57), channel_id=1, source_target_pairs={{0,1},{1,0},{2,3},{3,2},{4,5},{5,4},{6,7},{7,6},{8,9},{9,8},{10,11... | collective-permute-start | bytes 245768 | tf_op jit(solution)/shard_map/ppermute | solution.py:464
  36.3 3.1 %collective-permute-start.14 = (f32[160,128]{1,0:T(8,128)S(1)}, f32[160,128]{1,0:T(8,128)S(1)}, u32[]{:S(2)}, u32[]{:S(2)}) collective-permute-start(f32[160,128]{1,0:T(8,128)S(1)} %get-tuple-element.58), channel_id=1, source_target_pairs={{1,2},{3,4},{5,6},{7,0},{2,1},{4,3},{6,5},{0,7},{9,10},{11,12},{13... | collective-permute-start | bytes 245768 | tf_op jit(solution)/shard_map/ppermute | solution.py:465
  39.4 2.5 %collective-permute-done.14.refs_4_ = f32[160,128]{1,0:T(8,128)S(1)} collective-permute-done((f32[160,128]{1,0:T(8,128)S(1)}, f32[160,128]{1,0:T(8,128)S(1)}, u32[]{:S(2)}, u32[]{:S(2)}) %collective-permute-start.14) | collective-permute-done | bytes 81952 | tf_op jit(solution)/shard_map/ppermute | solution.py:465
  44.2 1.7 %collective-permute-start.17 = (f32[160,128]{1,0:T(8,128)S(1)}, f32[160,128]{1,0:T(8,128)S(1)}, u32[]{:S(2)}, u32[]{:S(2)}) collective-permute-start(f32[160,128]{1,0:T(8,128)S(1)} %get-tuple-element.60), channel_id=1, source_target_pairs={{0,1},{1,0},{2,3},{3,2},{4,5},{5,4},{6,7},{7,6},{8,9},{9,8},{10,11... | collective-permute-start | bytes 245768 | tf_op jit(solution)/shard_map/ppermute | solution.py:464
  46.0 3.1 %collective-permute-start.18 = (f32[160,128]{1,0:T(8,128)S(1)}, f32[160,128]{1,0:T(8,128)S(1)}, u32[]{:S(2)}, u32[]{:S(2)}) collective-permute-start(f32[160,128]{1,0:T(8,128)S(1)} %get-tuple-element.61), channel_id=1, source_target_pairs={{1,2},{3,4},{5,6},{7,0},{2,1},{4,3},{6,5},{0,7},{9,10},{11,12},{13... | collective-permute-start | bytes 245768 | tf_op jit(solution)/shard_map/ppermute | solution.py:465
  49.1 2.5 %collective-permute-done.18.refs_4_ = f32[160,128]{1,0:T(8,128)S(1)} collective-permute-done((f32[160,128]{1,0:T(8,128)S(1)}, f32[160,128]{1,0:T(8,128)S(1)}, u32[]{:S(2)}, u32[]{:S(2)}) %collective-permute-start.18) | collective-permute-done | bytes 81952 | tf_op jit(solution)/shard_map/ppermute | solution.py:465
  53.6 1.7 %collective-permute-start.21 = (f32[160,128]{1,0:T(8,128)S(1)}, f32[160,128]{1,0:T(8,128)S(1)}, u32[]{:S(2)}, u32[]{:S(2)}) collective-permute-start(f32[160,128]{1,0:T(8,128)S(1)} %get-tuple-element.63), channel_id=1, source_target_pairs={{0,1},{1,0},{2,3},{3,2},{4,5},{5,4},{6,7},{7,6},{8,9},{9,8},{10,11... | collective-permute-start | bytes 245768 | tf_op jit(solution)/shard_map/ppermute | solution.py:464
  55.3 3.1 %collective-permute-start.22 = (f32[160,128]{1,0:T(8,128)S(1)}, f32[160,128]{1,0:T(8,128)S(1)}, u32[]{:S(2)}, u32[]{:S(2)}) collective-permute-start(f32[160,128]{1,0:T(8,128)S(1)} %get-tuple-element.64), channel_id=1, source_target_pairs={{1,2},{3,4},{5,6},{7,0},{2,1},{4,3},{6,5},{0,7},{9,10},{11,12},{13... | collective-permute-start | bytes 245768 | tf_op jit(solution)/shard_map/ppermute | solution.py:465
  58.4 2.5 %collective-permute-done.22.refs_4_ = f32[160,128]{1,0:T(8,128)S(1)} collective-permute-done((f32[160,128]{1,0:T(8,128)S(1)}, f32[160,128]{1,0:T(8,128)S(1)}, u32[]{:S(2)}, u32[]{:S(2)}) %collective-permute-start.22) | collective-permute-done | bytes 81952 | tf_op jit(solution)/shard_map/ppermute | solution.py:465
  63.0 1.7 %collective-permute-start.25 = (f32[160,128]{1,0:T(8,128)S(1)}, f32[160,128]{1,0:T(8,128)S(1)}, u32[]{:S(2)}, u32[]{:S(2)}) collective-permute-start(f32[160,128]{1,0:T(8,128)S(1)} %get-tuple-element.66), channel_id=1, source_target_pairs={{0,1},{1,0},{2,3},{3,2},{4,5},{5,4},{6,7},{7,6},{8,9},{9,8},{10,11... | collective-permute-start | bytes 245768 | tf_op jit(solution)/shard_map/ppermute | solution.py:464
  64.7 3.1 %collective-permute-start.26 = (f32[160,128]{1,0:T(8,128)S(1)}, f32[160,128]{1,0:T(8,128)S(1)}, u32[]{:S(2)}, u32[]{:S(2)}) collective-permute-start(f32[160,128]{1,0:T(8,128)S(1)} %get-tuple-element.67), channel_id=1, source_target_pairs={{1,2},{3,4},{5,6},{7,0},{2,1},{4,3},{6,5},{0,7},{9,10},{11,12},{13... | collective-permute-start | bytes 245768 | tf_op jit(solution)/shard_map/ppermute | solution.py:465
  67.8 2.5 %collective-permute-done.26.refs_4_ = f32[160,128]{1,0:T(8,128)S(1)} collective-permute-done((f32[160,128]{1,0:T(8,128)S(1)}, f32[160,128]{1,0:T(8,128)S(1)}, u32[]{:S(2)}, u32[]{:S(2)}) %collective-permute-start.26) | collective-permute-done | bytes 81952 | tf_op jit(solution)/shard_map/ppermute | solution.py:465
  72.2 3.8 %collective-permute-start.30 = (f32[160,128]{1,0:T(8,128)S(1)}, f32[160,128]{1,0:T(8,128)S(1)}, u32[]{:S(2)}, u32[]{:S(2)}) collective-permute-start(f32[160,128]{1,0:T(8,128)S(1)} %get-tuple-element.70), channel_id=1, source_target_pairs={{1,2},{3,4},{5,6},{7,0},{2,1},{4,3},{6,5},{0,7},{9,10},{11,12},{13... | collective-permute-start | bytes 245768 | tf_op jit(solution)/shard_map/ppermute | solution.py:465
  80.5 15.4 %all_to_all.10 = f32[32,8,128]{2,1,0:T(8,128)S(1)} all-to-all(f32[32,8,128]{2,1,0:T(8,128)S(1)} %get-tuple-element.73), channel_id=1, replica_groups=mesh['ax'=32,'az'=8] {'ax'}, dimensions={0} | all-to-all | bytes 262144 | tf_op jit(solution)/shard_map/all_to_all | solution.py:483
  95.9 12.1 %all_to_all.11.gathered = f32[8,8,128]{2,1,0:T(8,128)S(1)} all-to-all(f32[8,8,128]{2,1,0:T(8,128)S(1)} %broadcast_in_dim.2), channel_id=1, replica_groups=mesh['ax'=32,'az'=8] {'az'}, dimensions={0} | all-to-all | bytes 65536 | tf_op jit(solution)/shard_map/all_to_all | solution.py:485
  108.0 6.1 %shard_map.105 = (f32[8,16,2,5,2,8,128]{6,5,4,3,2,1,0:T(8,128)}, f32[8,16,16]{2,1,0:T(8,128)}) custom-call(f32[8,8,128]{2,1,0:T(8,128)S(1)} %all_to_all.11.gathered, f32[8,256]{1,0:T(8,128)S(1)} %copy-done, f32[16,5,2,8,128]{4,3,2,1,0:T(8,128)} %get-tuple-element.74.middle, f32[16,5,2,8,128]{4,3,2,1,0:T(8,128)} %get-tuple-element.37.final), custom_call_target="tpu_custom_call" | custom-call | flops 16777216 | bytes 16777216 | tf_op jit(solution)/shard_map/pallas_call | solution.py:402
  (67 shorter events, 24.2 us)
Async XLA Ops:
  1.9 10.9 %collective-permute-start = (f32[640,128]{1,0:T(8,128)S(1)}, f32[640,128]{1,0:T(8,128)S(1)}, u32[]{:S(2)}, u32[]{:S(2)}) collective-permute-start(f32[640,128]{1,0:T(8,128)S(1)} %get-tuple-element.40.refs_0_.refs_1_.refs_8_), channel_id=1, source_target_pairs={{8,16},{9,17},{10,18},{11,19},{12,20},{13,21},{14,22},{15,23},{24,... | collective-permute-start | bytes 983048 | tf_op jit(solution)/shard_map/ppermute | solution.py:462
  4.7 11.5 %collective-permute-start.3 = (f32[640,128]{1,0:T(8,128)S(1)}, f32[640,128]{1,0:T(8,128)S(1)}, u32[]{:S(2)}, u32[]{:S(2)}) collective-permute-start(f32[640,128]{1,0:T(8,128)S(1)} %get-tuple-element.41.refs_1_.refs_0_.refs_8_), channel_id=1, source_target_pairs={{0,8},{8,0},{16,24},{24,16},{32,40},{40,32},{48,56},{56,48},{64,72... | collective-permute-start | bytes 983048 | tf_op jit(solution)/shard_map/ppermute | solution.py:463
  5.4 6.9 %collective-permute-start.1 = (f32[160,128]{1,0:T(8,128)S(1)}, f32[160,128]{1,0:T(8,128)S(1)}, u32[]{:S(2)}, u32[]{:S(2)}) collective-permute-start(f32[160,128]{1,0:T(8,128)S(1)} %get-tuple-element.42), channel_id=1, source_target_pairs={{0,1},{1,0},{2,3},{3,2},{4,5},{5,4},{6,7},{7,6},{8,9},{9,8},{10,11... | collective-permute-start | bytes 245768 | tf_op jit(solution)/shard_map/ppermute | solution.py:464
  7.0 5.8 %collective-permute-start.2 = (f32[160,128]{1,0:T(8,128)S(1)}, f32[160,128]{1,0:T(8,128)S(1)}, u32[]{:S(2)}, u32[]{:S(2)}) collective-permute-start(f32[160,128]{1,0:T(8,128)S(1)} %get-tuple-element.43), channel_id=1, source_target_pairs={{1,2},{3,4},{5,6},{7,0},{2,1},{4,3},{6,5},{0,7},{9,10},{11,12},{13... | collective-permute-start | bytes 245768 | tf_op jit(solution)/shard_map/ppermute | solution.py:465
  13.2 10.0 %collective-permute-start.4 = (f32[640,128]{1,0:T(8,128)S(1)}, f32[640,128]{1,0:T(8,128)S(1)}, u32[]{:S(2)}, u32[]{:S(2)}) collective-permute-start(f32[640,128]{1,0:T(8,128)S(1)} %shard_map.87.done.refs_0_.refs_1_.refs_9_), channel_id=1, source_target_pairs={{8,16},{9,17},{10,18},{11,19},{12,20},{13,21},{14,22},{15,23},{24,... | collective-permute-start | bytes 983048 | tf_op jit(solution)/shard_map/ppermute | solution.py:462
  16.6 8.0 %collective-permute-start.7 = (f32[640,128]{1,0:T(8,128)S(1)}, f32[640,128]{1,0:T(8,128)S(1)}, u32[]{:S(2)}, u32[]{:S(2)}) collective-permute-start(f32[640,128]{1,0:T(8,128)S(1)} %get-tuple-element.50.refs_1_.refs_0_.refs_9_), channel_id=1, source_target_pairs={{0,8},{8,0},{16,24},{24,16},{32,40},{40,32},{48,56},{56,48},{64,72... | collective-permute-start | bytes 983048 | tf_op jit(solution)/shard_map/ppermute | solution.py:463
  17.3 6.0 %collective-permute-start.6 = (f32[160,128]{1,0:T(8,128)S(1)}, f32[160,128]{1,0:T(8,128)S(1)}, u32[]{:S(2)}, u32[]{:S(2)}) collective-permute-start(f32[160,128]{1,0:T(8,128)S(1)} %get-tuple-element.52), channel_id=1, source_target_pairs={{1,2},{3,4},{5,6},{7,0},{2,1},{4,3},{6,5},{0,7},{9,10},{11,12},{13... | collective-permute-start | bytes 245768 | tf_op jit(solution)/shard_map/ppermute | solution.py:465
  23.7 8.9 %collective-permute-start.8 = (f32[640,128]{1,0:T(8,128)S(1)}, f32[640,128]{1,0:T(8,128)S(1)}, u32[]{:S(2)}, u32[]{:S(2)}) collective-permute-start(f32[640,128]{1,0:T(8,128)S(1)} %shard_map.89.done.refs_0_.refs_1_.refs_10_), channel_id=1, source_target_pairs={{8,16},{9,17},{10,18},{11,19},{12,20},{13,21},{14,22},{15,23},{24,... | collective-permute-start | bytes 983048 | tf_op jit(solution)/shard_map/ppermute | solution.py:462
  25.1 8.0 %collective-permute-start.11 = (f32[640,128]{1,0:T(8,128)S(1)}, f32[640,128]{1,0:T(8,128)S(1)}, u32[]{:S(2)}, u32[]{:S(2)}) collective-permute-start(f32[640,128]{1,0:T(8,128)S(1)} %get-tuple-element.53.refs_1_.refs_0_.refs_10_), channel_id=1, source_target_pairs={{0,8},{8,0},{16,24},{24,16},{32,40},{40,32},{48,56},{56,48},{64,72... | collective-permute-start | bytes 983048 | tf_op jit(solution)/shard_map/ppermute | solution.py:463
  27.0 5.7 %collective-permute-start.10 = (f32[160,128]{1,0:T(8,128)S(1)}, f32[160,128]{1,0:T(8,128)S(1)}, u32[]{:S(2)}, u32[]{:S(2)}) collective-permute-start(f32[160,128]{1,0:T(8,128)S(1)} %get-tuple-element.55), channel_id=1, source_target_pairs={{1,2},{3,4},{5,6},{7,0},{2,1},{4,3},{6,5},{0,7},{9,10},{11,12},{13... | collective-permute-start | bytes 245768 | tf_op jit(solution)/shard_map/ppermute | solution.py:465
  33.1 8.9 %collective-permute-start.12 = (f32[640,128]{1,0:T(8,128)S(1)}, f32[640,128]{1,0:T(8,128)S(1)}, u32[]{:S(2)}, u32[]{:S(2)}) collective-permute-start(f32[640,128]{1,0:T(8,128)S(1)} %shard_map.91.done.refs_0_.refs_1_), channel_id=1, source_target_pairs={{8,16},{9,17},{10,18},{11,19},{12,20},{13,21},{14,22},{15,23},{24,... | collective-permute-start | bytes 983048 | tf_op jit(solution)/shard_map/ppermute | solution.py:462
  33.6 9.4 %collective-permute-start.15 = (f32[640,128]{1,0:T(8,128)S(1)}, f32[640,128]{1,0:T(8,128)S(1)}, u32[]{:S(2)}, u32[]{:S(2)}) collective-permute-start(f32[640,128]{1,0:T(8,128)S(1)} %get-tuple-element.56.refs_1_.refs_0_), channel_id=1, source_target_pairs={{0,8},{8,0},{16,24},{24,16},{32,40},{40,32},{48,56},{56,48},{64,72... | collective-permute-start | bytes 983048 | tf_op jit(solution)/shard_map/ppermute | solution.py:463
  36.3 5.6 %collective-permute-start.14 = (f32[160,128]{1,0:T(8,128)S(1)}, f32[160,128]{1,0:T(8,128)S(1)}, u32[]{:S(2)}, u32[]{:S(2)}) collective-permute-start(f32[160,128]{1,0:T(8,128)S(1)} %get-tuple-element.58), channel_id=1, source_target_pairs={{1,2},{3,4},{5,6},{7,0},{2,1},{4,3},{6,5},{0,7},{9,10},{11,12},{13... | collective-permute-start | bytes 245768 | tf_op jit(solution)/shard_map/ppermute | solution.py:465
  42.5 9.2 %collective-permute-start.16 = (f32[640,128]{1,0:T(8,128)S(1)}, f32[640,128]{1,0:T(8,128)S(1)}, u32[]{:S(2)}, u32[]{:S(2)}) collective-permute-start(f32[640,128]{1,0:T(8,128)S(1)} %shard_map.93.done.refs_0_.refs_1_.refs_8_.outer), channel_id=1, source_target_pairs={{8,16},{9,17},{10,18},{11,19},{12,20},{13,21},{14,22},{15,23},{24,... | collective-permute-start | bytes 983048 | tf_op jit(solution)/shard_map/ppermute | solution.py:462
  43.6 9.2 %collective-permute-start.19 = (f32[640,128]{1,0:T(8,128)S(1)}, f32[640,128]{1,0:T(8,128)S(1)}, u32[]{:S(2)}, u32[]{:S(2)}) collective-permute-start(f32[640,128]{1,0:T(8,128)S(1)} %get-tuple-element.59.refs_1_.refs_0_.refs_8_.inner), channel_id=1, source_target_pairs={{0,8},{8,0},{16,24},{24,16},{32,40},{40,32},{48,56},{56,48},{64,72... | collective-permute-start | bytes 983048 | tf_op jit(solution)/shard_map/ppermute | solution.py:463
  46.0 5.6 %collective-permute-start.18 = (f32[160,128]{1,0:T(8,128)S(1)}, f32[160,128]{1,0:T(8,128)S(1)}, u32[]{:S(2)}, u32[]{:S(2)}) collective-permute-start(f32[160,128]{1,0:T(8,128)S(1)} %get-tuple-element.61), channel_id=1, source_target_pairs={{1,2},{3,4},{5,6},{7,0},{2,1},{4,3},{6,5},{0,7},{9,10},{11,12},{13... | collective-permute-start | bytes 245768 | tf_op jit(solution)/shard_map/ppermute | solution.py:465
  52.1 8.9 %collective-permute-start.20 = (f32[640,128]{1,0:T(8,128)S(1)}, f32[640,128]{1,0:T(8,128)S(1)}, u32[]{:S(2)}, u32[]{:S(2)}) collective-permute-start(f32[640,128]{1,0:T(8,128)S(1)} %shard_map.95.done.refs_0_.refs_1_.refs_9_), channel_id=1, source_target_pairs={{8,16},{9,17},{10,18},{11,19},{12,20},{13,21},{14,22},{15,23},{24,... | collective-permute-start | bytes 983048 | tf_op jit(solution)/shard_map/ppermute | solution.py:462
  53.2 8.7 %collective-permute-start.23 = (f32[640,128]{1,0:T(8,128)S(1)}, f32[640,128]{1,0:T(8,128)S(1)}, u32[]{:S(2)}, u32[]{:S(2)}) collective-permute-start(f32[640,128]{1,0:T(8,128)S(1)} %get-tuple-element.62.refs_1_.refs_0_.refs_9_), channel_id=1, source_target_pairs={{0,8},{8,0},{16,24},{24,16},{32,40},{40,32},{48,56},{56,48},{64,72... | collective-permute-start | bytes 983048 | tf_op jit(solution)/shard_map/ppermute | solution.py:463
  55.3 5.6 %collective-permute-start.22 = (f32[160,128]{1,0:T(8,128)S(1)}, f32[160,128]{1,0:T(8,128)S(1)}, u32[]{:S(2)}, u32[]{:S(2)}) collective-permute-start(f32[160,128]{1,0:T(8,128)S(1)} %get-tuple-element.64), channel_id=1, source_target_pairs={{1,2},{3,4},{5,6},{7,0},{2,1},{4,3},{6,5},{0,7},{9,10},{11,12},{13... | collective-permute-start | bytes 245768 | tf_op jit(solution)/shard_map/ppermute | solution.py:465
  61.3 8.9 %collective-permute-start.24 = (f32[640,128]{1,0:T(8,128)S(1)}, f32[640,128]{1,0:T(8,128)S(1)}, u32[]{:S(2)}, u32[]{:S(2)}) collective-permute-start(f32[640,128]{1,0:T(8,128)S(1)} %shard_map.97.done.refs_0_.refs_1_.refs_10_), channel_id=1, source_target_pairs={{8,16},{9,17},{10,18},{11,19},{12,20},{13,21},{14,22},{15,23},{24,... | collective-permute-start | bytes 983048 | tf_op jit(solution)/shard_map/ppermute | solution.py:462
  62.4 8.3 %collective-permute-start.27 = (f32[640,128]{1,0:T(8,128)S(1)}, f32[640,128]{1,0:T(8,128)S(1)}, u32[]{:S(2)}, u32[]{:S(2)}) collective-permute-start(f32[640,128]{1,0:T(8,128)S(1)} %get-tuple-element.65.refs_1_.refs_0_.refs_10_), channel_id=1, source_target_pairs={{0,8},{8,0},{16,24},{24,16},{32,40},{40,32},{48,56},{56,48},{64,72... | collective-permute-start | bytes 983048 | tf_op jit(solution)/shard_map/ppermute | solution.py:463
  71.2 6.7 %collective-permute-start.31 = (f32[640,128]{1,0:T(8,128)S(1)}, f32[640,128]{1,0:T(8,128)S(1)}, u32[]{:S(2)}, u32[]{:S(2)}) collective-permute-start(f32[640,128]{1,0:T(8,128)S(1)} %get-tuple-element.68.refs_1_.refs_0_), channel_id=1, source_target_pairs={{0,8},{8,0},{16,24},{24,16},{32,40},{40,32},{48,56},{56,48},{64,72... | collective-permute-start | bytes 983048 | tf_op jit(solution)/shard_map/ppermute | solution.py:463
  72.2 6.8 %collective-permute-start.28 = (f32[640,128]{1,0:T(8,128)S(1)}, f32[640,128]{1,0:T(8,128)S(1)}, u32[]{:S(2)}, u32[]{:S(2)}) collective-permute-start(f32[640,128]{1,0:T(8,128)S(1)} %shard_map.99.done.refs_0_.refs_1_), channel_id=1, source_target_pairs={{8,16},{9,17},{10,18},{11,19},{12,20},{13,21},{14,22},{15,23},{24,... | collective-permute-start | bytes 983048 | tf_op jit(solution)/shard_map/ppermute | solution.py:462
  72.2 5.6 %collective-permute-start.30 = (f32[160,128]{1,0:T(8,128)S(1)}, f32[160,128]{1,0:T(8,128)S(1)}, u32[]{:S(2)}, u32[]{:S(2)}) collective-permute-start(f32[160,128]{1,0:T(8,128)S(1)} %get-tuple-element.70), channel_id=1, source_target_pairs={{1,2},{3,4},{5,6},{7,0},{2,1},{4,3},{6,5},{0,7},{9,10},{11,12},{13... | collective-permute-start | bytes 245768 | tf_op jit(solution)/shard_map/ppermute | solution.py:465
  (9 other events, 95.0 us)
